TPU v7x, 32 devices: a whole 2x2x4 slice. The times are simulated.
32 devices in a mesh: gx: 2 (over x), gy: 4 (over z), gz: 4 (over y, core).
Axes of the slice: x: 2, y: 2, z: 4, core: 2. Of those that a mesh axis runs over, the one named last changes fastest.
Arguments:
- a_blocks: bfloat16 [8, 16, 8, 7, 4096], P('gx', 'gy', 'gz'), may hold values from -6 to 6
- prolong: bfloat16 [8, 16, 8, 4096], P('gx', 'gy', 'gz'), may hold values from -0.75 to 0.75
- pairing: int32 [4, 8, 8], P('gx', 'gy', 'gz'), may hold values 0 or 1
- route: int32 [512, 1], P(('gx', 'gy', 'gz')), may hold values from 0 to 1; in each aligned block of 16 rows (0 to 15, 16 to 31, ...) at most 12 rows name the same one
Outputs:
- coarse_rows: bfloat16 [768, 11, 4096], P(('gx', 'gy', 'gz'))
Inputs may be any that keep to these rules, and one draw needn't show every extreme that they name: `pairing`: 0 pairs each patch's elements along the first direction, 1 along the second. `route`: among the 16 aggregates of one device no destination is named more than 12 times, and in every draw some device names one destination exactly 12 times.
All inputs are finite; a program needn't handle non-finite values. No bound on the sum of `pairing` on one device may be relied on, other than what follows from the above.
Results may differ from a plain program's by a relative error of at most 0.0049.
Values may be sent and summed in bfloat16 or wider, within the bound.
No kernel may reach another device: no remote copies, remote signals or barrier semaphores. Data moves between devices by JAX's collectives and lax.ppermute only.
A program may use at most 128 MiB of HBM per device.

v0:
```python
import functools
import math

import jax
import jax.numpy as jnp
from jax import lax
from jax.experimental import pallas as pl
from jax.experimental.pallas import tpu as pltpu
from jax.sharding import PartitionSpec as P


x_first_order = [0, 2, 1, 3, 4, 5, 6]
x_second_order = [0, 1, 2, 3, 4, 5, 6]
y_first_order = [0, 4, 1, 2, 3, 5, 6]
y_second_order = [0, 3, 1, 2, 4, 5, 6]

LANES = 128
SUB = 8


def padded_2(array, sides, width):
    for axis, dim in sides:
        devices, length = (lax.axis_size(axis), array.shape[dim])
        up = [(i, (i + 1) % devices) for i in range(devices - 1)]
        down = [(j, i) for i, j in up]
        last = lax.slice_in_dim(array, length - width, length, axis=dim)
        initial = lax.slice_in_dim(array, 0, width, axis=dim)
        before = lax.ppermute(last, axis, up)
        after = lax.ppermute(initial, axis, down)
        array = jnp.concatenate([before, array, after], axis=dim)
    return array


def neighbours(padded):
    shifted = [
        padded[1:-1, 1:-1, 1:-1],
        padded[:-2, 1:-1, 1:-1],
        padded[2:, 1:-1, 1:-1],
        padded[1:-1, :-2, 1:-1],
        padded[1:-1, 2:, 1:-1],
        padded[1:-1, 1:-1, :-2],
        padded[1:-1, 1:-1, 2:],
    ]
    return jnp.stack(shifted, axis=3)


def triple(blocks, nearby):
    block_side = math.isqrt(blocks.shape[-1])
    leading = blocks.shape[:-1]
    left_mat = blocks.reshape(leading + (block_side, block_side))
    right_mat = nearby.reshape(leading + (block_side, block_side))
    own_block = jnp.swapaxes(right_mat[..., :1, :, :], -1, -2)
    product = jnp.matmul(left_mat, right_mat, preferred_element_type=jnp.float32).astype(
        jnp.bfloat16
    )
    result = jnp.matmul(own_block, product, preferred_element_type=jnp.float32)
    return result.reshape(leading + (block_side * block_side,))


def members(element_grid, pairs):
    size_x, size_y, size_z = element_grid.shape[:3]
    trailing = element_grid.shape[3:]
    patches = element_grid.reshape((size_x // 2, 2, size_y // 2, 2, size_z) + trailing)

    def pick(upper, lower, slot_order):
        return jnp.take(patches[:, upper, :, lower], jnp.array(slot_order, dtype=jnp.int32), axis=3)

    x_one = jnp.stack([pick(0, 0, x_first_order), pick(0, 1, x_first_order)], axis=3)
    x_two = jnp.stack([pick(1, 0, x_second_order), pick(1, 1, x_second_order)], axis=3)
    y_one = jnp.stack([pick(0, 0, y_first_order), pick(1, 0, y_first_order)], axis=3)
    y_two = jnp.stack([pick(0, 1, y_second_order), pick(1, 1, y_second_order)], axis=3)
    along_x = (pairs == 0).reshape(pairs.shape + (1,) * (x_one.ndim - 3))
    member_one = jnp.where(along_x, x_one, y_one)
    member_two = jnp.where(along_x, x_two, y_two)
    return (
        member_one.reshape((-1,) + member_one.shape[4:]),
        member_two.reshape((-1,) + member_two.shape[4:]),
    )


def arrange(member_one, member_two):
    diagonal = (
        member_one[..., 0, :]
        + member_two[..., 0, :]
        + member_one[..., 1, :]
        + member_two[..., 1, :]
    )
    return jnp.concatenate(
        [diagonal[..., None, :], member_one[..., 2:, :], member_two[..., 2:, :]], axis=-2
    )


def slot_sources(routes, n_dest, capacity):
    total = routes.shape[0]
    chosen = (routes[:, None] == jnp.arange(n_dest, dtype=jnp.int32)[None, :]).astype(jnp.int32)
    before = jnp.cumsum(chosen, axis=0) - chosen
    ranking = jnp.sum(before * chosen, axis=1)
    position = routes * capacity + ranking
    targets = jnp.arange(n_dest * capacity, dtype=jnp.int32)
    matches = position[None, :] == targets[:, None]
    anchor = jnp.sum(jnp.where(matches, jnp.arange(total, dtype=jnp.int32)[None, :], 0), axis=1)
    filled = jnp.any(matches, axis=1)
    return (anchor, filled)


def pack_slots(payload, anchor, filled):
    taken = jnp.take(payload, anchor, axis=0)
    keep_row = filled.reshape(filled.shape + (1,) * (payload.ndim - 1))
    return jnp.where(keep_row, taken, jnp.zeros_like(taken))


def general(a_blocks, prolong, pairing, route, capacity):
    padded = padded_2(prolong, (("gx", 0), ("gy", 1), ("gz", 2)), 1)
    nearby = neighbours(padded)
    anchor, filled = slot_sources(route[:, 0], lax.axis_size("gx"), capacity)
    galerkin = triple(a_blocks, nearby)
    member_one, member_two = members(galerkin, pairing)
    coarse = arrange(member_one, member_two).astype(jnp.bfloat16)
    return lax.all_to_all(
        pack_slots(coarse, anchor, filled), "gx", split_axis=0, concat_axis=0, tiled=True
    )


def dot(left, right):
    return jnp.dot(left, right, preferred_element_type=jnp.float32)


def iota(shape, axis):
    return lax.broadcasted_iota(jnp.int32, shape, axis)


def as_bf16(mask):
    return mask.astype(jnp.float32).astype(jnp.bfloat16)


def pair(one, two):
    h = one.shape[1] // 2
    low = jnp.concatenate([one[:, :h], two[:, :h]], axis=1)
    high = jnp.concatenate([one[:, h:], two[:, h:]], axis=1)
    return jnp.concatenate([low, high], axis=0)


def unpair(both):
    rows, h = both.shape[0] // 2, both.shape[1] // 2
    even, odd = both[:rows], both[rows:]
    return (
        jnp.concatenate([even[:, :h], odd[:, :h]], axis=1),
        jnp.concatenate([even[:, h:], odd[:, h:]], axis=1),
    )


def constants(blk):
    n = 2 * blk
    row, col = iota((n, n), 0), iota((n, n), 1)
    c, z = row % blk, row // blk
    clean = as_bf16(col == (c % 2) * blk + (c // 2) * 2 + z)
    q = blk // 2
    k, p = row // blk, (row // q) % 2
    spread = as_bf16(col == k * blk + 2 * (row % q) + p)
    return clean, spread


def even_lanes(rows):
    return as_bf16(iota((rows, LANES), 1) % 2 == 0), as_bf16(iota((rows, LANES), 1) % 2 == 1)


def even_rows(rows):
    return as_bf16(iota((rows, LANES), 0) % 2 == 0), as_bf16(iota((rows, LANES), 0) % 2 == 1)


def transposed_dot(left, right):
    return lax.dot_general(
        left, right, (((1,), (1,)), ((), ())), preferred_element_type=jnp.float32
    )


def store_left(left_ref, x, b, both_t, masks):
    q = masks[0].shape[0]
    for k in range(2):
        for p in range(2):
            part = both_t[(2 * k + p) * q : (2 * k + p + 1) * q]
            for z in range(2):
                left_ref[x, 2 * b + k, (2 * p + z) * q : (2 * p + z + 1) * q] = part * masks[z]


def store_weight(ref, one):
    none = jnp.zeros_like(one)
    rows = one.shape[0]
    ref[:rows] = jnp.concatenate([one, none], axis=1)
    ref[rows:] = jnp.concatenate([none, one], axis=1)


def halves(part):
    h = part.shape[1] // 2
    return part[:, :h], part[:, h:]


def places(route_ref, where_ref, table_ref, dims, blocks):
    aggregates, cap, rows = dims
    me = lax.axis_index("gx")
    lines = rows // cap
    rest = cap % SUB
    half = (cap - rest) * lines
    at_zero = me == 0
    for c in range(cap):
        if c < cap - rest:
            zero = (c, c + half // 2, c, c)
        else:
            h = c - (cap - rest)
            zero = (half + h, half + h + rest, SUB + h, SUB + h + rest)
        if c < rest:
            one = (half + c + rest, half + c, SUB + c, SUB + c + rest)
        else:
            h = c - rest
            one = (h, h + half // 2, h, h)
        for k in range(4):
            table_ref[k, c] = jnp.where(at_zero, zero[k], one[k])
    sent, kept = jnp.int32(0), jnp.int32(0)
    for i in range(aggregates):
        away = route_ref[0, i] != me
        one = away.astype(jnp.int32)
        c = jnp.where(away, sent, kept)
        sent = sent + one
        kept = kept + (1 - one)
        base = jnp.where(away, 0, blocks * rows)
        where_ref[0, i] = base + table_ref[0, c]
        where_ref[1, i] = base + table_ref[1, c]
        where_ref[2, i] = jnp.where(away, 0, 2 * SUB) + table_ref[2, c]
        where_ref[3, i] = jnp.where(away, 0, 2 * SUB) + table_ref[3, c]
    return sent, kept


def put(total_ref, where_ref, i, block, rows, value):
    n = value.shape[0] // 2
    one = where_ref[0, i] + block * rows
    two = where_ref[1, i] + block * rows
    total_ref[pl.ds(one, n, stride=SUB), :] = value[:n]
    total_ref[pl.ds(two, n, stride=SUB), :] = value[n:]


def finish(out, total_ref, kind, blocks, dims, count):
    _, cap, rows = dims
    rest = cap % SUB
    full = (cap - rest) * (rows // cap)
    me = lax.axis_index("gx")
    line = iota((SUB, LANES), 0)
    in_full = (line + jnp.where(me == 0, 0, rest) < count)[None]
    in_half = (line % rest + jnp.where(me == 0, cap - rest, 0) < count)[None]
    for k in range(blocks):
        for at, size, filled in ((0, full, in_full), (full, rows - full, in_half)):
            value = total_ref[pl.ds((kind * blocks + k) * rows + at, size), :].reshape(-1, SUB, LANES)
            value = jnp.where(filled, value, 0.0).reshape(size, LANES)
            out[k * rows + at : k * rows + at + size] = value.astype(jnp.bfloat16)


GROUP = 4


def in_groups(items, size):
    items = list(items)
    return [items[k : k + size] for k in range(0, len(items), size)]


def inner_kernel(
    dims, grid, route_ref, pair_ref, p_ref, a_hbm, send_ref, keep_ref, xface_ref, yup_ref, ydn_ref, zup_ref, zdn_ref,
    a_ref, left_ref, weight_ref, part_ref, total_ref, codes_ref, where_ref, table_ref, sems,
):
    px, py, nz = grid
    aggregates, _, rows = dims
    blk = p_ref.shape[2]
    q = blk // 2
    nb = 5
    patches = [(a, b) for a in range(px) for b in range(py)]

    def fetch(n):
        a, b = patches[n]
        at = (pl.ds(2 * a, 2), pl.ds(2 * b, 2))
        return pltpu.make_async_copy(a_hbm.at[at], a_ref.at[at], sems.at[n])

    for n in range(len(patches)):
        fetch(n).start()
    clean, spread = constants(blk)
    lanes_of = even_lanes(q)
    sent, kept = places(route_ref, where_ref, table_ref, dims, nb)
    codes_ref[...] = jnp.zeros_like(codes_ref)
    for i in range(aggregates):
        a, b, z, t = i // (py * nz * 2), (i // (nz * 2)) % py, (i // 2) % nz, i % 2
        code = (2 * (jnp.where(pair_ref[a, b, z] == 0, 2, 1) - t) + z).astype(jnp.float32)
        line = jnp.full((1, LANES), code, jnp.float32)
        codes_ref[pl.ds(where_ref[2, i], 1), :] = line
        codes_ref[pl.ds(where_ref[3, i], 1), :] = line
    me = lax.axis_index("gx")
    xface_ref[...] = p_ref[jnp.where(me == 0, 2 * px - 1, 0)]
    for x in range(2 * px):
        yup_ref[x] = p_ref[x, 2 * py - 1]
        ydn_ref[x] = p_ref[x, 0]

    for group in in_groups([(x, b) for x in range(2 * px) for b in range(py)], GROUP):
        both = [pair(p_ref[x, 2 * b], p_ref[x, 2 * b + 1]) for x, b in group]
        tidy = [dot(clean, one).astype(jnp.bfloat16) for one in both]
        left = [transposed_dot(spread, one).astype(jnp.bfloat16) for one in both]
        for (x, b), one in zip(group, tidy):
            zdn_ref[x * py + b] = one[:blk]
            zup_ref[x * py + b] = one[blk:]
            for z in range(nz):
                for v, part in enumerate(halves(one[z * blk : (z + 1) * blk])):
                    store_weight(weight_ref.at[x, 2 * b + v, z], part)
        for (x, b), one in zip(group, left):
            store_left(left_ref, x, b, one, lanes_of)

    first, second = even_rows(blk)
    for n, (a, b) in enumerate(patches):
        fetch(n).wait()
        group = [(2 * a + u, 2 * b + v) for u in range(2) for v in range(2)]
        right = []
        for x, y in group:
            here = a_ref.at[x, y]
            along_z = here[6] * first + here[5] * second
            right.append(
                jnp.concatenate(
                    [pair(here[0], here[2 - x % 2]), pair(here[4 - y % 2], along_z)], axis=1
                )
            )
        got = [dot(left_ref[x, y], one).astype(jnp.bfloat16) for (x, y), one in zip(group, right)]
        for (x, y), one in zip(group, got):
            parts = unpair(one[:, : 2 * blk]) + unpair(one[:, 2 * blk :])
            for k in range(4):
                part_ref[x, y, k] = parts[k]

    for a, b in patches:
        own, with_x, with_y, with_z = {}, {}, {}, {}
        group = [(u, v, z) for z in range(nz) for u in range(2) for v in range(2)]
        stacks = []
        for u, v, z in group:
            x, y = 2 * a + u, 2 * b + v
            zs, zo = pl.ds(z * q, q), pl.ds((1 - z) * q, q)
            stacks.append(
                jnp.concatenate(
                    [
                        part_ref[x, y, 0, zs],
                        part_ref[2 * a + 1 - u, y, 1, zs],
                        part_ref[x, 2 * b + 1 - v, 2, zs],
                        part_ref[x, y, 3, zo],
                    ],
                    axis=0,
                )
            )
        made = [
            dot(one, weight_ref[2 * a + u, 2 * b + v, z]) for (u, v, z), one in zip(group, stacks)
        ]
        for (u, v, z), got in zip(group, made):
            own[u, v, z] = got[:q]
            with_x[1 - u, v, z] = got[q : 2 * q]
            with_y[u, 1 - v, z] = got[2 * q : 3 * q]
            with_z[u, v, 1 - z] = got[3 * q :]
        for z in range(nz):
            flat = pair_ref[a, b, z] == 0
            i = ((a * py + b) * nz + z) * 2
            sums = {}
            for u in range(2):
                for v in range(2):
                    t = u if u == v else jnp.where(flat, v, u)
                    m = u if u == v else jnp.where(flat, u, v)
                    e = (u, v, z)
                    sums[u, v] = own[e] + jnp.where(flat, with_x[e], with_y[e])
                    cross = jnp.where(flat, with_y[e], with_x[e])
                    put(total_ref, where_ref, i + t, 1 + 2 * m, rows, cross)
                    put(total_ref, where_ref, i + t, 2 + 2 * m, rows, with_z[e])
            put(total_ref, where_ref, i, 0, rows, sums[0, 0] + jnp.where(flat, sums[1, 0], sums[0, 1]))
            put(total_ref, where_ref, i + 1, 0, rows, sums[1, 1] + jnp.where(flat, sums[0, 1], sums[1, 0]))

    for kind, (out, count) in enumerate(((send_ref, sent), (keep_ref, kept))):
        finish(out, total_ref, kind, nb, dims, count)
        out[nb * rows :] = codes_ref[kind * 2 * SUB : (kind + 1) * 2 * SUB].astype(jnp.bfloat16)


def outer_kernel(
    dims, grid, route_ref, pair_ref, p_ref, a_hbm, zup_ref, zdn_ref, xface_hbm, ylow_hbm, yhigh_hbm, zlow_hbm, zhigh_hbm,
    send_ref, keep_ref,
    a_ref, xface_ref, ylow_ref, yhigh_ref, zlow_ref, zhigh_ref,
    weight_ref, zweight_ref, left_ref, part_ref, total_ref, where_ref, table_ref, sems,
):
    px, py, nz = grid
    _, _, rows = dims
    nx, ny = 2 * px, 2 * py
    blk = p_ref.shape[2]
    q = blk // 2
    nb = 6
    copies = [
        pltpu.make_async_copy(one, two, sems.at[k])
        for k, (one, two) in enumerate((
            (a_hbm, a_ref), (xface_hbm, xface_ref), (ylow_hbm, ylow_ref), (yhigh_hbm, yhigh_ref),
            (zlow_hbm, zlow_ref), (zhigh_hbm, zhigh_ref),
        ))
    ]
    for copy in copies:
        copy.start()
    sent, kept = places(route_ref, where_ref, table_ref, dims, nb)
    me = lax.axis_index("gx")
    clean, spread = constants(blk)
    lanes_of = even_lanes(q)
    first, second = even_rows(blk)

    for group in in_groups([(x, b) for x in range(nx) for b in range(py)], GROUP):
        both = [pair(p_ref[x, 2 * b], p_ref[x, 2 * b + 1]) for x, b in group]
        left = [transposed_dot(spread, one).astype(jnp.bfloat16) for one in both]
        for x, b in group:
            for z, ref in enumerate((zdn_ref, zup_ref)):
                for v, part in enumerate(halves(ref[x * py + b])):
                    store_weight(weight_ref.at[x + 1, 2 * b + v + 1, z], part)
        for (x, b), one in zip(group, left):
            store_left(left_ref, x, b, one, lanes_of)
    copies[0].wait()
    for group in in_groups([(x, y) for x in range(nx) for y in range(ny)], GROUP):
        right = []
        for x, y in group:
            here = a_ref.at[x, y]
            along_z = here[5] * first + here[6] * second
            low, high = halves(along_z)
            right.append(
                jnp.concatenate(
                    [pair(here[1 + x % 2], here[3 + y % 2]), jnp.concatenate([low, high], axis=0)],
                    axis=1,
                )
            )
        got = [dot(left_ref[x, y], one).astype(jnp.bfloat16) for (x, y), one in zip(group, right)]
        for (x, y), one in zip(group, got):
            part_ref[x, y, 0], part_ref[x, y, 1] = unpair(one[:, : 2 * blk])
            along = one[:, 2 * blk :]
            part_ref[x, y, 2] = jnp.concatenate([along[:blk], along[blk:]], axis=1)

    for copy in copies[1:]:
        copy.wait()
    above = jnp.where(me == 0, 0.0, 1.0)
    sides = [xface_ref[y] for y in range(ny)], [ylow_ref[x] for x in range(nx)], [yhigh_ref[x] for x in range(nx)]
    both = [[pair(one[k], one[k + 1]) for k in range(0, len(one), 2)] for one in sides]
    tidy = [[dot(clean, one) for one in some] for some in both]
    for b in range(py):
        for at, scale in ((0, above), (nx + 1, 1.0 - above)):
            one = (tidy[0][b] * scale).astype(jnp.bfloat16)
            for z in range(nz):
                for v, part in enumerate(halves(one[z * blk : (z + 1) * blk])):
                    store_weight(weight_ref.at[at, 2 * b + v + 1, z], part)
    for at, some in ((0, tidy[1]), (ny + 1, tidy[2])):
        for a in range(px):
            one = some[a].astype(jnp.bfloat16)
            for z in range(nz):
                for u, part in enumerate(halves(one[z * blk : (z + 1) * blk])):
                    store_weight(weight_ref.at[2 * a + u + 1, at, z], part)
    for side, ref in enumerate((zlow_ref, zhigh_ref)):
        for x in range(nx):
            for b in range(py):
                for v, part in enumerate(halves(ref[x * py + b])):
                    store_weight(zweight_ref.at[side, x, 2 * b + v], part)

    for group in in_groups([(x, y) for x in range(nx) for y in range(ny)], 2):
        work = []
        for x, y in group:
            for z in range(nz):
                zs = pl.ds(z * q, q)
                a, b, u, v = x // 2, y // 2, x % 2, y % 2
                flat = pair_ref[a, b, z] == 0
                t = u if u == v else jnp.where(flat, v, u)
                m = u if u == v else jnp.where(flat, u, v)
                i = ((a * py + b) * nz + z) * 2 + t
                for k, weight in enumerate((
                    weight_ref.at[x + 2 * u, y + 1, z],
                    weight_ref.at[x + 1, y + 2 * v, z],
                    zweight_ref.at[z, x, y],
                )):
                    work.append((i, 3 * m + k, part_ref[x, y, k, zs], weight))
        made = [dot(left, weight[...]) for _, _, left, weight in work]
        for (i, block, _, _), got in zip(work, made):
            put(total_ref, where_ref, i, block, rows, got)

    for kind, (out, count) in enumerate(((send_ref, sent), (keep_ref, kept))):
        finish(out, total_ref, kind, nb, dims, count)


def placed_blocks(early_ref, late_ref, rows, at, size, codes):
    code = jnp.concatenate([codes, codes], axis=0)
    near_low, near_high = (code < 1.5)[None], (code > 3.5)[None]
    upper = ((code == 1.0) | (code == 3.0) | (code == 5.0))[None]

    def tiles(ref, k):
        return ref[k * rows + at : k * rows + at + size].reshape(-1, 2 * SUB, LANES)

    yield tiles(early_ref, 0)
    for m in range(2):
        cross, z_in = tiles(early_ref, 1 + 2 * m), tiles(early_ref, 2 + 2 * m)
        x_out, y_out, z_out = (tiles(late_ref, 3 * m + k) for k in range(3))
        yield jnp.where(near_low, cross, x_out)
        yield jnp.where(near_low, x_out, jnp.where(near_high, y_out, cross))
        yield jnp.where(near_high, cross, y_out)
        yield jnp.where(upper, z_in, z_out)
        yield jnp.where(upper, z_out, z_in)


def keep_kernel(dims, early_ref, late_ref, half_ref, out_hbm, full_ref, sem):
    cap, rows = dims
    full = (cap - cap % SUB) * (rows // cap)
    me = lax.axis_index("gx")
    codes = early_ref[5 * rows :]
    copies = []
    for k, value in enumerate(placed_blocks(early_ref, late_ref, rows, 0, full, codes[:SUB])):
        full_ref[k] = value.reshape(full, LANES)
        to = out_hbm.at[k, pl.ds(me * (2 * full), full), :]
        copies.append(pltpu.make_async_copy(full_ref.at[k], to, sem.at[k]))
        copies[-1].start()
    for k, value in enumerate(placed_blocks(early_ref, late_ref, rows, full, rows - full, codes[SUB:])):
        half_ref[k] = value.reshape(rows - full, LANES)
    for copy in copies:
        copy.wait()


def take_kernel(dims, early_ref, late_ref, half_ref, _, out_hbm, full_ref, mixed_ref, sem):
    cap, rows = dims
    full = (cap - cap % SUB) * (rows // cap)
    me = lax.axis_index("gx")
    codes = early_ref[5 * rows :]
    copies = []
    for k, value in enumerate(placed_blocks(early_ref, late_ref, rows, 0, full, codes[:SUB])):
        full_ref[k] = value.reshape(full, LANES)
        to = out_hbm.at[k, pl.ds((1 - me) * (2 * full), full), :]
        copies.append(pltpu.make_async_copy(full_ref.at[k], to, sem.at[0, k]))
        copies[-1].start()
    first_half = (iota((SUB, LANES), 0) < SUB // 2)[None]
    pick = first_half == (me == 0)
    for k, value in enumerate(placed_blocks(early_ref, late_ref, rows, full, rows - full, codes[SUB:])):
        theirs = value.reshape(rows - full, LANES).astype(jnp.float32).reshape(-1, SUB, LANES)
        mine = half_ref[k].astype(jnp.float32).reshape(-1, SUB, LANES)
        low = jnp.where(pick, mine, theirs)
        high = pltpu.roll(jnp.where(pick, theirs, mine), SUB // 2, 1)
        mixed_ref[k, : rows - full] = low.reshape(rows - full, LANES).astype(jnp.bfloat16)
        mixed_ref[k, rows - full :] = high.reshape(rows - full, LANES).astype(jnp.bfloat16)
        to = out_hbm.at[k, full : 2 * full, :]
        copies.append(pltpu.make_async_copy(mixed_ref.at[k], to, sem.at[1, k]))
        copies[-1].start()
    for copy in copies:
        copy.wait()


SMEM = pl.BlockSpec(memory_space=pltpu.SMEM)
VMEM = pl.BlockSpec(memory_space=pltpu.VMEM)
ANY = pl.BlockSpec(memory_space=pl.ANY)


def bf16(*shape):
    return jax.ShapeDtypeStruct(shape, jnp.bfloat16)


def local(a_blocks, prolong, pairing, route):
    devices_gx = lax.axis_size("gx")
    aggregates = route.shape[0]
    capacity = max(2, 3 * aggregates // (2 * devices_gx))
    nx, ny, nz, faces, entries = a_blocks.shape
    fits = (
        devices_gx == 2
        and nz == 2
        and nx % 2 == 0
        and ny % 2 == 0
        and faces == 7
        and entries == (LANES // 2) ** 2
        and capacity // SUB == 1
        and capacity % SUB == SUB // 2
    )
    if not fits:
        return general(a_blocks, prolong, pairing, route, capacity)
    px, py = nx // 2, ny // 2
    blk = math.isqrt(entries)
    lines = entries // LANES
    a_view = a_blocks.transpose(0, 1, 3, 2, 4).reshape(nx, ny, faces, nz, lines, LANES)
    a_view = a_view.transpose(0, 1, 2, 4, 3, 5).reshape(nx, ny, faces, nz * lines, LANES)
    p_view = prolong.reshape(nx, ny, nz, lines, LANES).transpose(0, 1, 3, 2, 4)
    p_view = p_view.reshape(nx, ny, nz * lines, LANES)
    route_row = route.reshape(1, aggregates)
    rows = capacity * lines
    dims, grid = (aggregates, capacity, rows), (px, py, nz)
    f32 = jnp.float32
    half_type = jnp.bfloat16
    face_x, face_y, face_z = (ny, blk, LANES), (nx, blk, LANES), (nx * py, blk, LANES)
    room = pltpu.CompilerParams(vmem_limit_bytes=67_043_328)
    cost = pl.CostEstimate(flops=10**9, bytes_accessed=4 * 10**6, transcendentals=0)

    send_0, keep_0, xface, yup, ydn, zup, zdn = pl.pallas_call(
        functools.partial(inner_kernel, dims, grid),
        out_shape=(
            bf16(5 * rows + 2 * SUB, LANES),
            bf16(5 * rows + 2 * SUB, LANES),
            bf16(*face_x),
            bf16(*face_y),
            bf16(*face_y),
            bf16(*face_z),
            bf16(*face_z),
        ),
        in_specs=[SMEM, SMEM, VMEM, ANY],
        out_specs=[VMEM] * 7,
        scratch_shapes=[
            pltpu.VMEM(a_view.shape, half_type),
            pltpu.VMEM((nx, ny, 2 * blk, LANES), half_type),
            pltpu.VMEM((nx, ny, nz, 2 * blk, LANES), half_type),
            pltpu.VMEM((nx, ny, 4, blk, LANES), half_type),
            pltpu.VMEM((10 * rows, LANES), f32),
            pltpu.VMEM((4 * SUB, LANES), f32),
            pltpu.SMEM((4, aggregates), jnp.int32),
            pltpu.SMEM((4, capacity), jnp.int32),
            pltpu.SemaphoreType.DMA((px * py,)),
        ],
        compiler_params=room,
        cost_estimate=cost,
        name="inner_blocks",
    )(route_row, pairing, p_view, a_view)

    def chain(axis):
        n = lax.axis_size(axis)
        up = [(i, i + 1) for i in range(n - 1)]
        return up, [(j, i) for i, j in up]

    swap = [(0, 1), (1, 0)]
    xface = lax.ppermute(xface, "gx", swap)
    got_0 = lax.ppermute(send_0, "gx", swap)
    up, down = chain("gy")
    ylow = lax.ppermute(yup, "gy", up)
    yhigh = lax.ppermute(ydn, "gy", down)
    up, down = chain("gz")
    zlow = lax.ppermute(zup, "gz", up)
    zhigh = lax.ppermute(zdn, "gz", down)

    send_1, keep_1 = pl.pallas_call(
        functools.partial(outer_kernel, dims, grid),
        out_shape=(bf16(6 * rows, LANES), bf16(6 * rows, LANES)),
        in_specs=[SMEM, SMEM, VMEM, ANY, VMEM, VMEM] + [ANY] * 5,
        out_specs=[VMEM] * 2,
        scratch_shapes=[
            pltpu.VMEM(a_view.shape, half_type),
            pltpu.VMEM(face_x, half_type),
            pltpu.VMEM(face_y, half_type),
            pltpu.VMEM(face_y, half_type),
            pltpu.VMEM(face_z, half_type),
            pltpu.VMEM(face_z, half_type),
            pltpu.VMEM((nx + 2, ny + 2, nz, 2 * blk, LANES), half_type),
            pltpu.VMEM((2, nx, ny, 2 * blk, LANES), half_type),
            pltpu.VMEM((nx, ny, 2 * blk, LANES), half_type),
            pltpu.VMEM((nx, ny, 3, blk, LANES), half_type),
            pltpu.VMEM((12 * rows, LANES), f32),
            pltpu.SMEM((4, aggregates), jnp.int32),
            pltpu.SMEM((4, capacity), jnp.int32),
            pltpu.SemaphoreType.DMA((6,)),
        ],
        compiler_params=pltpu.CompilerParams(vmem_limit_bytes=67_043_328 - 1400 * 1024),
        cost_estimate=cost,
        name="outer_blocks",
    )(route_row, pairing, p_view, a_view, zup, zdn, xface, ylow, yhigh, zlow, zhigh)
    got_1 = lax.ppermute(send_1, "gx", swap)

    full = (capacity // SUB) * SUB * lines
    whole = 2 * rows
    half, out = pl.pallas_call(
        functools.partial(keep_kernel, (capacity, rows)),
        out_shape=(bf16(11, rows - full, LANES), bf16(11, whole, LANES)),
        in_specs=[VMEM] * 2,
        out_specs=[VMEM, ANY],
        scratch_shapes=[pltpu.VMEM((11, full, LANES), half_type), pltpu.SemaphoreType.DMA((11,))],
        compiler_params=room,
        cost_estimate=cost,
        name="place_kept",
    )(keep_0, keep_1)
    out = pl.pallas_call(
        functools.partial(take_kernel, (capacity, rows)),
        out_shape=bf16(11, whole, LANES),
        in_specs=[VMEM] * 3 + [ANY],
        out_specs=ANY,
        input_output_aliases={3: 0},
        scratch_shapes=[
            pltpu.VMEM((11, full, LANES), half_type),
            pltpu.VMEM((11, full, LANES), half_type),
            pltpu.SemaphoreType.DMA((2, 11)),
        ],
        compiler_params=room,
        cost_estimate=cost,
        name="place_received",
    )(got_0, got_1, half, out)
    out = out.reshape(11, whole // (SUB * lines), lines, SUB, LANES).transpose(1, 3, 0, 2, 4)
    return out.reshape(2 * capacity, 11, entries)


def solution(mesh):
    placed = (
        P("gx", "gy", "gz", None, None),
        P("gx", "gy", "gz", None),
        P("gx", "gy", "gz"),
        P(("gx", "gy", "gz"), None),
    )
    return jax.shard_map(
        local,
        mesh=mesh,
        in_specs=placed,
        out_specs=P(("gx", "gy", "gz"), None, None),
        check_vma=False,
    )
```

profile of v0, /device:TPU:0, one launch (start us, length us, event | category | flops | bytes accessed | tf_op | source)
XLA Modules:
  0.0 58.1 jit_solution(15192121844223732336)
XLA Ops:
  0.0 5.3 %inner_blocks.1 = (bf16[1936,128]{1,0:T(8,128)(2,1)}, bf16[1936,128]{1,0:T(8,128)(2,1)}, bf16[4,64,128]{2,1,0:T(8,128)(2,1)}, bf16[4,64,128]{2,1,0:T(8,128)(2,1)...) custom-call(s32[1,16]{1,0:T(1,128)} %bitcast.22, s32[2,2,2]{2,1,0:T(2,128)} %pair_ref.3, ...), custom_call_target="tpu_custom_call" | custom-call | flops 1000000000 | bytes 4000000 | tf_op jit(solution)/shard_map/inner_blocks/pallas_call | solution.py:585
  5.3 2.4 %collective-permute-start.4 = (bf16[8,64,128]{2,1,0:T(8,128)(2,1)}, bf16[8,64,128]{2,1,0:T(8,128)(2,1)S(1)}, u32[]{:S(2)}, u32[]{:S(2)}) collective-permute-start(bf16[8,64,128]{2,1,0:T(8,128)(2,1)} %get-tuple-element.17.zup_ref), channel_id=1, source_target_pairs={{0,1},{1,2},{2,3},{4,5},{5,6},{6,7},{8,9},{9,10},{10,11},{12,13},{... | collective-permute-start | bytes 393224 | tf_op jit(solution)/shard_map/ppermute | solution.py:626
  7.8 1.3 %collective-permute-start.5 = (bf16[8,64,128]{2,1,0:T(8,128)(2,1)}, bf16[8,64,128]{2,1,0:T(8,128)(2,1)S(1)}, u32[]{:S(2)}, u32[]{:S(2)}) collective-permute-start(bf16[8,64,128]{2,1,0:T(8,128)(2,1)} %get-tuple-element.18.zdn_ref), channel_id=1, source_target_pairs={{1,0},{2,1},{3,2},{5,4},{6,5},{7,6},{9,8},{10,9},{11,10},{13,12},{... | collective-permute-start | bytes 393224 | tf_op jit(solution)/shard_map/ppermute | solution.py:627
  9.1 2.3 %collective-permute-start.1 = (bf16[4,64,128]{2,1,0:T(8,128)(2,1)}, bf16[4,64,128]{2,1,0:T(8,128)(2,1)S(1)}, u32[]{:S(2)}, u32[]{:S(2)}) collective-permute-start(bf16[4,64,128]{2,1,0:T(8,128)(2,1)} %get-tuple-element.19), channel_id=1, source_target_pairs={{0,16},{16,0},{1,17},{17,1},{2,18},{18,2},{3,19},{19,3},{4,20},{20... | collective-permute-start | bytes 196616 | tf_op jit(solution)/shard_map/ppermute | solution.py:620
  11.4 3.5 %collective-permute-start.2 = (bf16[4,64,128]{2,1,0:T(8,128)(2,1)}, bf16[4,64,128]{2,1,0:T(8,128)(2,1)S(1)}, u32[]{:S(2)}, u32[]{:S(2)}) collective-permute-start(bf16[4,64,128]{2,1,0:T(8,128)(2,1)} %get-tuple-element.20), channel_id=1, source_target_pairs={{0,4},{4,8},{8,12},{1,5},{5,9},{9,13},{2,6},{6,10},{10,14},{3,7},{... | collective-permute-start | bytes 196616 | tf_op jit(solution)/shard_map/ppermute | solution.py:623
  14.9 1.3 %collective-permute-start.3 = (bf16[4,64,128]{2,1,0:T(8,128)(2,1)}, bf16[4,64,128]{2,1,0:T(8,128)(2,1)S(1)}, u32[]{:S(2)}, u32[]{:S(2)}) collective-permute-start(bf16[4,64,128]{2,1,0:T(8,128)(2,1)} %get-tuple-element.21), channel_id=1, source_target_pairs={{4,0},{8,4},{12,8},{5,1},{9,5},{13,9},{6,2},{10,6},{14,10},{7,3},{... | collective-permute-start | bytes 196616 | tf_op jit(solution)/shard_map/ppermute | solution.py:624
  16.2 0.0 collective-permute-done.1.xface_hbm
  16.2 0.0 copy-start.2
  16.2 0.9 %collective-permute-done.2.ylow_hbm = bf16[4,64,128]{2,1,0:T(8,128)(2,1)S(1)} collective-permute-done((bf16[4,64,128]{2,1,0:T(8,128)(2,1)}, bf16[4,64,128]{2,1,0:T(8,128)(2,1)S(1)}, u32[]{:S(2)}, u32[]{:S(2)}) %collective-permute-start.2) | collective-permute-done | bytes 65568 | tf_op jit(solution)/shard_map/ppermute | solution.py:623
  17.1 0.0 copy-start.3
  17.1 4.2 %collective-permute-done.3.yhigh_hbm = bf16[4,64,128]{2,1,0:T(8,128)(2,1)S(1)} collective-permute-done((bf16[4,64,128]{2,1,0:T(8,128)(2,1)}, bf16[4,64,128]{2,1,0:T(8,128)(2,1)S(1)}, u32[]{:S(2)}, u32[]{:S(2)}) %collective-permute-start.3) | collective-permute-done | bytes 65568 | tf_op jit(solution)/shard_map/ppermute | solution.py:624
  21.2 0.0 copy-start.4
  21.2 0.0 collective-permute-done.4.zlow_hbm
  21.2 0.0 copy-start
  21.3 0.0 collective-permute-done.5.zhigh_hbm
  21.3 0.0 copy-done.2
  21.3 0.0 copy-done.3
  21.3 0.6 %copy-done.4 = bf16[4,64,128]{2,1,0:T(8,128)(2,1)} copy-done((bf16[4,64,128]{2,1,0:T(8,128)(2,1)}, bf16[4,64,128]{2,1,0:T(8,128)(2,1)S(1)}, u32[]{:S(2)}) %copy-start.4) | copy-done | bytes 65560
  21.9 0.0 copy-done
  21.9 0.0 copy-start.1
  21.9 0.7 %copy-done.1 = bf16[8,64,128]{2,1,0:T(8,128)(2,1)} copy-done((bf16[8,64,128]{2,1,0:T(8,128)(2,1)}, bf16[8,64,128]{2,1,0:T(8,128)(2,1)S(1)}, u32[]{:S(2)}) %copy-start.1) | copy-done | bytes 131096
  22.6 5.9 %outer_blocks.1 = (bf16[2304,128]{1,0:T(8,128)(2,1)}, bf16[2304,128]{1,0:T(8,128)(2,1)}) custom-call(s32[1,16]{1,0:T(1,128)} %bitcast.23, s32[2,2,2]{2,1,0:T(2,128)} %pair_ref.3, bf16[4,4,64,128]{3,2,1,0:T(8,128)(2,1)} %bitcast.21, bf16[4,4,7,64,128]{4,3,2,1,0:T(8,128)(2,1)} %bitcast.19, bf16[8,64,128]{2,1,0:T(8,128)(2,1)} %get-tuple-element.17.zup_ref, ...), custom_call_target="tpu_custom_call" | custom-call | flops 1000000000 | bytes 4000000 | tf_op jit(solution)/shard_map/outer_blocks/pallas_call | solution.py:629
  28.5 0.6 %collective-permute-start.6 = (bf16[2304,128]{1,0:T(8,128)(2,1)}, bf16[2304,128]{1,0:T(8,128)(2,1)}, u32[]{:S(2)}, u32[]{:S(2)}) collective-permute-start(bf16[2304,128]{1,0:T(8,128)(2,1)} %get-tuple-element.22), channel_id=1, source_target_pairs={{0,16},{16,0},{1,17},{17,1},{2,18},{18,2},{3,19},{19,3},{4,20},{20... | collective-permute-start | bytes 1769480 | tf_op jit(solution)/shard_map/ppermute | solution.py:654
  29.1 1.5 %collective-permute-start = (bf16[1936,128]{1,0:T(8,128)(2,1)}, bf16[1936,128]{1,0:T(8,128)(2,1)}, u32[]{:S(2)}, u32[]{:S(2)}) collective-permute-start(bf16[1936,128]{1,0:T(8,128)(2,1)} %get-tuple-element.16), channel_id=1, source_target_pairs={{0,16},{16,0},{1,17},{17,1},{2,18},{18,2},{3,19},{19,3},{4,20},{20... | collective-permute-start | bytes 1486856 | tf_op jit(solution)/shard_map/ppermute | solution.py:621
  30.6 2.9 %place_kept.1 = (bf16[11,128,128]{2,1,0:T(8,128)(2,1)}, bf16[11,768,128]{2,1,0:T(8,128)(2,1)}) custom-call(bf16[1936,128]{1,0:T(8,128)(2,1)} %get-tuple-element.23.early_ref, bf16[2304,128]{1,0:T(8,128)(2,1)} %get-tuple-element.24.late_ref), custom_call_target="tpu_custom_call" | custom-call | flops 1000000000 | bytes 4000000 | tf_op jit(solution)/shard_map/place_kept/pallas_call | solution.py:658
  33.5 21.9 %collective-permute-done.early_ref = bf16[1936,128]{1,0:T(8,128)(2,1)} collective-permute-done((bf16[1936,128]{1,0:T(8,128)(2,1)}, bf16[1936,128]{1,0:T(8,128)(2,1)}, u32[]{:S(2)}, u32[]{:S(2)}) %collective-permute-start) | collective-permute-done | bytes 495648 | tf_op jit(solution)/shard_map/ppermute | solution.py:621
  55.5 0.0 collective-permute-done.6.late_ref
  55.5 2.6 %place_received.1 = bf16[11,768,128]{2,1,0:T(8,128)(2,1)} custom-call(bf16[1936,128]{1,0:T(8,128)(2,1)} %collective-permute-done.early_ref, bf16[2304,128]{1,0:T(8,128)(2,1)} %collective-permute-done.6.late_ref, bf16[11,128,128]{2,1,0:T(8,128)(2,1)} %get-tuple-element.25.half_ref, ...), custom_call_target="tpu_custom_call", output_to_operand_aliasing={{}: (3, {})} | custom-call | flops 1000000000 | bytes 4000000 | tf_op jit(solution)/shard_map/place_received/pallas_call | solution.py:668
Async XLA Ops:
  5.3 15.9 %collective-permute-start.4 = (bf16[8,64,128]{2,1,0:T(8,128)(2,1)}, bf16[8,64,128]{2,1,0:T(8,128)(2,1)S(1)}, u32[]{:S(2)}, u32[]{:S(2)}) collective-permute-start(bf16[8,64,128]{2,1,0:T(8,128)(2,1)} %get-tuple-element.17.zup_ref), channel_id=1, source_target_pairs={{0,1},{1,2},{2,3},{4,5},{5,6},{6,7},{8,9},{9,10},{10,11},{12,13},{... | collective-permute-start | bytes 393224 | tf_op jit(solution)/shard_map/ppermute | solution.py:626
  7.8 13.5 %collective-permute-start.5 = (bf16[8,64,128]{2,1,0:T(8,128)(2,1)}, bf16[8,64,128]{2,1,0:T(8,128)(2,1)S(1)}, u32[]{:S(2)}, u32[]{:S(2)}) collective-permute-start(bf16[8,64,128]{2,1,0:T(8,128)(2,1)} %get-tuple-element.18.zdn_ref), channel_id=1, source_target_pairs={{1,0},{2,1},{3,2},{5,4},{6,5},{7,6},{9,8},{10,9},{11,10},{13,12},{... | collective-permute-start | bytes 393224 | tf_op jit(solution)/shard_map/ppermute | solution.py:627
  9.1 7.1 %collective-permute-start.1 = (bf16[4,64,128]{2,1,0:T(8,128)(2,1)}, bf16[4,64,128]{2,1,0:T(8,128)(2,1)S(1)}, u32[]{:S(2)}, u32[]{:S(2)}) collective-permute-start(bf16[4,64,128]{2,1,0:T(8,128)(2,1)} %get-tuple-element.19), channel_id=1, source_target_pairs={{0,16},{16,0},{1,17},{17,1},{2,18},{18,2},{3,19},{19,3},{4,20},{20... | collective-permute-start | bytes 196616 | tf_op jit(solution)/shard_map/ppermute | solution.py:620
  11.4 5.7 %collective-permute-start.2 = (bf16[4,64,128]{2,1,0:T(8,128)(2,1)}, bf16[4,64,128]{2,1,0:T(8,128)(2,1)S(1)}, u32[]{:S(2)}, u32[]{:S(2)}) collective-permute-start(bf16[4,64,128]{2,1,0:T(8,128)(2,1)} %get-tuple-element.20), channel_id=1, source_target_pairs={{0,4},{4,8},{8,12},{1,5},{5,9},{9,13},{2,6},{6,10},{10,14},{3,7},{... | collective-permute-start | bytes 196616 | tf_op jit(solution)/shard_map/ppermute | solution.py:623
  14.9 6.4 %collective-permute-start.3 = (bf16[4,64,128]{2,1,0:T(8,128)(2,1)}, bf16[4,64,128]{2,1,0:T(8,128)(2,1)S(1)}, u32[]{:S(2)}, u32[]{:S(2)}) collective-permute-start(bf16[4,64,128]{2,1,0:T(8,128)(2,1)} %get-tuple-element.21), channel_id=1, source_target_pairs={{4,0},{8,4},{12,8},{5,1},{9,5},{13,9},{6,2},{10,6},{14,10},{7,3},{... | collective-permute-start | bytes 196616 | tf_op jit(solution)/shard_map/ppermute | solution.py:624
  16.2 5.1 %copy-start.2 = (bf16[4,64,128]{2,1,0:T(8,128)(2,1)}, bf16[4,64,128]{2,1,0:T(8,128)(2,1)S(1)}, u32[]{:S(2)}) copy-start(bf16[4,64,128]{2,1,0:T(8,128)(2,1)S(1)} %collective-permute-done.1.xface_hbm) | copy-start | bytes 196612
  17.1 4.2 %copy-start.3 = (bf16[4,64,128]{2,1,0:T(8,128)(2,1)}, bf16[4,64,128]{2,1,0:T(8,128)(2,1)S(1)}, u32[]{:S(2)}) copy-start(bf16[4,64,128]{2,1,0:T(8,128)(2,1)S(1)} %collective-permute-done.2.ylow_hbm) | copy-start | bytes 196612
  21.2 0.6 %copy-start.4 = (bf16[4,64,128]{2,1,0:T(8,128)(2,1)}, bf16[4,64,128]{2,1,0:T(8,128)(2,1)S(1)}, u32[]{:S(2)}) copy-start(bf16[4,64,128]{2,1,0:T(8,128)(2,1)S(1)} %collective-permute-done.3.yhigh_hbm) | copy-start | bytes 196612
  21.2 0.7 %copy-start = (bf16[8,64,128]{2,1,0:T(8,128)(2,1)}, bf16[8,64,128]{2,1,0:T(8,128)(2,1)S(1)}, u32[]{:S(2)}) copy-start(bf16[8,64,128]{2,1,0:T(8,128)(2,1)S(1)} %collective-permute-done.4.zlow_hbm) | copy-start | bytes 393220
  21.9 0.7 %copy-start.1 = (bf16[8,64,128]{2,1,0:T(8,128)(2,1)}, bf16[8,64,128]{2,1,0:T(8,128)(2,1)S(1)}, u32[]{:S(2)}) copy-start(bf16[8,64,128]{2,1,0:T(8,128)(2,1)S(1)} %collective-permute-done.5.zhigh_hbm) | copy-start | bytes 393220
  28.5 26.9 %collective-permute-start.6 = (bf16[2304,128]{1,0:T(8,128)(2,1)}, bf16[2304,128]{1,0:T(8,128)(2,1)}, u32[]{:S(2)}, u32[]{:S(2)}) collective-permute-start(bf16[2304,128]{1,0:T(8,128)(2,1)} %get-tuple-element.22), channel_id=1, source_target_pairs={{0,16},{16,0},{1,17},{17,1},{2,18},{18,2},{3,19},{19,3},{4,20},{20... | collective-permute-start | bytes 1769480 | tf_op jit(solution)/shard_map/ppermute | solution.py:654
  29.1 26.4 %collective-permute-start = (bf16[1936,128]{1,0:T(8,128)(2,1)}, bf16[1936,128]{1,0:T(8,128)(2,1)}, u32[]{:S(2)}, u32[]{:S(2)}) collective-permute-start(bf16[1936,128]{1,0:T(8,128)(2,1)} %get-tuple-element.16), channel_id=1, source_target_pairs={{0,16},{16,0},{1,17},{17,1},{2,18},{18,2},{3,19},{19,3},{4,20},{20... | collective-permute-start | bytes 1486856 | tf_op jit(solution)/shard_map/ppermute | solution.py:621
where the time goes:
time: 58.4 us; the launch traced here: 58.1 us
  waiting for transfers between devices  27 us (46%)
  Pallas kernels  16.8 us (29%)
  starting transfers between devices  12.9 us (22%)
  local copies, waits for them, and re-layouts  1.31 us (2%)
    ppermute x1, waiting for transfers between devices, local(): got_0 = lax.ppermute(send_0, 'gx', swap)  21.9 us
    pallas_call x1, Pallas kernels, local(): pl.pallas_call(functools.partial(outer_kernel, dims, grid), out_shape=(bf...  5.92 us
    pallas_call x1, Pallas kernels, local(): pl.pallas_call(functools.partial(inner_kernel, dims, grid), out_shape=(bf...  5.34 us
    ppermute x1, waiting for transfers between devices, local(): yhigh = lax.ppermute(ydn, 'gy', down)  4.17 us
    ppermute x1, starting transfers between devices, local(): ylow = lax.ppermute(yup, 'gy', up)  3.47 us
    pallas_call x1, Pallas kernels, local(): pl.pallas_call(functools.partial(keep_kernel, (capacity, rows)), out_shap...  2.9 us
    pallas_call x1, Pallas kernels, local(): pl.pallas_call(functools.partial(take_kernel, (capacity, rows)), out_shap...  2.59 us
    ppermute x1, starting transfers between devices, local(): zlow = lax.ppermute(zup, 'gz', up)  2.4 us
  transfers between devices with their start and end apart: 7, of which 3 were waited for; matrix products, arithmetic and copies ran while one was open for 0% of the time, Pallas kernels for 5%

commit v1 on v0

v1 whole, which is shorter than its diff:
```python
import functools
import math

import jax
import jax.numpy as jnp
from jax import lax
from jax.experimental import pallas as pl
from jax.experimental.pallas import tpu as pltpu
from jax.sharding import PartitionSpec as P


x_first_order = [0, 2, 1, 3, 4, 5, 6]
x_second_order = [0, 1, 2, 3, 4, 5, 6]
y_first_order = [0, 4, 1, 2, 3, 5, 6]
y_second_order = [0, 3, 1, 2, 4, 5, 6]

LANES = 128
SUB = 8


def padded_2(array, sides, width):
    for axis, dim in sides:
        devices, length = (lax.axis_size(axis), array.shape[dim])
        up = [(i, (i + 1) % devices) for i in range(devices - 1)]
        down = [(j, i) for i, j in up]
        last = lax.slice_in_dim(array, length - width, length, axis=dim)
        initial = lax.slice_in_dim(array, 0, width, axis=dim)
        before = lax.ppermute(last, axis, up)
        after = lax.ppermute(initial, axis, down)
        array = jnp.concatenate([before, array, after], axis=dim)
    return array


def neighbours(padded):
    shifted = [
        padded[1:-1, 1:-1, 1:-1],
        padded[:-2, 1:-1, 1:-1],
        padded[2:, 1:-1, 1:-1],
        padded[1:-1, :-2, 1:-1],
        padded[1:-1, 2:, 1:-1],
        padded[1:-1, 1:-1, :-2],
        padded[1:-1, 1:-1, 2:],
    ]
    return jnp.stack(shifted, axis=3)


def triple(blocks, nearby):
    block_side = math.isqrt(blocks.shape[-1])
    leading = blocks.shape[:-1]
    left_mat = blocks.reshape(leading + (block_side, block_side))
    right_mat = nearby.reshape(leading + (block_side, block_side))
    own_block = jnp.swapaxes(right_mat[..., :1, :, :], -1, -2)
    product = jnp.matmul(left_mat, right_mat, preferred_element_type=jnp.float32).astype(
        jnp.bfloat16
    )
    result = jnp.matmul(own_block, product, preferred_element_type=jnp.float32)
    return result.reshape(leading + (block_side * block_side,))


def members(element_grid, pairs):
    size_x, size_y, size_z = element_grid.shape[:3]
    trailing = element_grid.shape[3:]
    patches = element_grid.reshape((size_x // 2, 2, size_y // 2, 2, size_z) + trailing)

    def pick(upper, lower, slot_order):
        return jnp.take(patches[:, upper, :, lower], jnp.array(slot_order, dtype=jnp.int32), axis=3)

    x_one = jnp.stack([pick(0, 0, x_first_order), pick(0, 1, x_first_order)], axis=3)
    x_two = jnp.stack([pick(1, 0, x_second_order), pick(1, 1, x_second_order)], axis=3)
    y_one = jnp.stack([pick(0, 0, y_first_order), pick(1, 0, y_first_order)], axis=3)
    y_two = jnp.stack([pick(0, 1, y_second_order), pick(1, 1, y_second_order)], axis=3)
    along_x = (pairs == 0).reshape(pairs.shape + (1,) * (x_one.ndim - 3))
    member_one = jnp.where(along_x, x_one, y_one)
    member_two = jnp.where(along_x, x_two, y_two)
    return (
        member_one.reshape((-1,) + member_one.shape[4:]),
        member_two.reshape((-1,) + member_two.shape[4:]),
    )


def arrange(member_one, member_two):
    diagonal = (
        member_one[..., 0, :]
        + member_two[..., 0, :]
        + member_one[..., 1, :]
        + member_two[..., 1, :]
    )
    return jnp.concatenate(
        [diagonal[..., None, :], member_one[..., 2:, :], member_two[..., 2:, :]], axis=-2
    )


def slot_sources(routes, n_dest, capacity):
    total = routes.shape[0]
    chosen = (routes[:, None] == jnp.arange(n_dest, dtype=jnp.int32)[None, :]).astype(jnp.int32)
    before = jnp.cumsum(chosen, axis=0) - chosen
    ranking = jnp.sum(before * chosen, axis=1)
    position = routes * capacity + ranking
    targets = jnp.arange(n_dest * capacity, dtype=jnp.int32)
    matches = position[None, :] == targets[:, None]
    anchor = jnp.sum(jnp.where(matches, jnp.arange(total, dtype=jnp.int32)[None, :], 0), axis=1)
    filled = jnp.any(matches, axis=1)
    return (anchor, filled)


def pack_slots(payload, anchor, filled):
    taken = jnp.take(payload, anchor, axis=0)
    keep_row = filled.reshape(filled.shape + (1,) * (payload.ndim - 1))
    return jnp.where(keep_row, taken, jnp.zeros_like(taken))


def general(a_blocks, prolong, pairing, route, capacity):
    padded = padded_2(prolong, (("gx", 0), ("gy", 1), ("gz", 2)), 1)
    nearby = neighbours(padded)
    anchor, filled = slot_sources(route[:, 0], lax.axis_size("gx"), capacity)
    galerkin = triple(a_blocks, nearby)
    member_one, member_two = members(galerkin, pairing)
    coarse = arrange(member_one, member_two).astype(jnp.bfloat16)
    return lax.all_to_all(
        pack_slots(coarse, anchor, filled), "gx", split_axis=0, concat_axis=0, tiled=True
    )


def dot(left, right):
    return jnp.dot(left, right, preferred_element_type=jnp.float32)


def iota(shape, axis):
    return lax.broadcasted_iota(jnp.int32, shape, axis)


def as_bf16(mask):
    return mask.astype(jnp.float32).astype(jnp.bfloat16)


def pair(one, two):
    h = one.shape[1] // 2
    low = jnp.concatenate([one[:, :h], two[:, :h]], axis=1)
    high = jnp.concatenate([one[:, h:], two[:, h:]], axis=1)
    return jnp.concatenate([low, high], axis=0)


def unpair(both):
    rows, h = both.shape[0] // 2, both.shape[1] // 2
    even, odd = both[:rows], both[rows:]
    return (
        jnp.concatenate([even[:, :h], odd[:, :h]], axis=1),
        jnp.concatenate([even[:, h:], odd[:, h:]], axis=1),
    )


def constants(blk):
    n = 2 * blk
    row, col = iota((n, n), 0), iota((n, n), 1)
    c, z = row % blk, row // blk
    clean = as_bf16(col == (c % 2) * blk + (c // 2) * 2 + z)
    q = blk // 2
    k, p = row // blk, (row // q) % 2
    spread = as_bf16(col == k * blk + 2 * (row % q) + p)
    return clean, spread


def even_lanes(rows):
    return as_bf16(iota((rows, LANES), 1) % 2 == 0), as_bf16(iota((rows, LANES), 1) % 2 == 1)


def even_rows(rows):
    return as_bf16(iota((rows, LANES), 0) % 2 == 0), as_bf16(iota((rows, LANES), 0) % 2 == 1)


def transposed_dot(left, right):
    return lax.dot_general(
        left, right, (((1,), (1,)), ((), ())), preferred_element_type=jnp.float32
    )


def left_factors(both_t, k, masks):
    q = masks[0].shape[0]
    parts = [both_t[(2 * k + p) * q : (2 * k + p + 1) * q] for p in range(2)]
    return jnp.concatenate([part * mask for part in parts for mask in masks], axis=0)


def weights_of(part):
    h = part.shape[1] // 2
    none = jnp.zeros((part.shape[0], h), part.dtype)
    made = []
    for k in range(2):
        one = part[:, k * h : (k + 1) * h]
        made.append(
            jnp.concatenate(
                [jnp.concatenate([one, none], axis=1), jnp.concatenate([none, one], axis=1)], axis=0
            )
        )
    return made


def halves(part):
    h = part.shape[1] // 2
    return part[:, :h], part[:, h:]


def places(route_ref, where_ref, table_ref, dims, blocks):
    aggregates, cap, rows = dims
    me = lax.axis_index("gx")
    lines = rows // cap
    rest = cap % SUB
    half = (cap - rest) * lines
    at_zero = me == 0
    for c in range(cap):
        if c < cap - rest:
            zero = (c, c + half // 2, c, c)
        else:
            h = c - (cap - rest)
            zero = (half + h, half + h + rest, SUB + h, SUB + h + rest)
        if c < rest:
            one = (half + c + rest, half + c, SUB + c, SUB + c + rest)
        else:
            h = c - rest
            one = (h, h + half // 2, h, h)
        for k in range(4):
            table_ref[k, c] = jnp.where(at_zero, zero[k], one[k])
    sent, kept = jnp.int32(0), jnp.int32(0)
    for i in range(aggregates):
        away = route_ref[0, i] != me
        one = away.astype(jnp.int32)
        c = jnp.where(away, sent, kept)
        sent = sent + one
        kept = kept + (1 - one)
        base = jnp.where(away, 0, blocks * rows)
        where_ref[0, i] = base + table_ref[0, c]
        where_ref[1, i] = base + table_ref[1, c]
        where_ref[2, i] = jnp.where(away, 0, 2 * SUB) + table_ref[2, c]
        where_ref[3, i] = jnp.where(away, 0, 2 * SUB) + table_ref[3, c]
    return sent, kept


def put(total_ref, where_ref, i, block, rows, value):
    n = value.shape[0] // 2
    one = where_ref[0, i] + block * rows
    two = where_ref[1, i] + block * rows
    total_ref[pl.ds(one, n, stride=SUB), :] = value[:n]
    total_ref[pl.ds(two, n, stride=SUB), :] = value[n:]


def finish(outs, total_ref, kind, dims, count):
    _, cap, rows = dims
    rest = cap % SUB
    full = (cap - rest) * (rows // cap)
    me = lax.axis_index("gx")
    line = iota((2 * SUB, LANES), 0)
    in_full = as_bf16(line % SUB + jnp.where(me == 0, 0, rest) < count) > 0.5
    in_half = as_bf16(line % rest + jnp.where(me == 0, cap - rest, 0) < count) > 0.5
    blocks = sum(n for _, n in outs)
    done = 0
    for out, n in outs:
        for k in range(n):
            for at, size, filled in ((0, full, in_full), (full, rows - full, in_half)):
                value = total_ref[pl.ds((kind * blocks + done + k) * rows + at, size), :]
                value = value.astype(jnp.bfloat16).reshape(-1, 2 * SUB, LANES)
                value = jnp.where(filled[None], value, jnp.zeros_like(value))
                out[k * rows + at : k * rows + at + size] = value.reshape(size, LANES)
        done += n


def inner_kernel(
    dims, grid, route_ref, pair_ref, p_ref, a_hbm,
    send_ref, keep_ref, xface_ref, yup_ref, ydn_ref, zup_ref, zdn_ref, left_ref,
    a_ref, part_ref, total_ref, codes_ref, where_ref, table_ref, sems,
):
    px, py, nz = grid
    aggregates, _, rows = dims
    nx, ny = 2 * px, 2 * py
    blk = p_ref.shape[2]
    q = blk // 2
    nb = 5
    copy = pltpu.make_async_copy(a_hbm, a_ref, sems.at[0])
    copy.start()
    clean, spread = constants(blk)
    masks = even_lanes(q)
    first, second = even_rows(blk)
    me = lax.axis_index("gx")

    pairs = [(x, b) for x in range(nx) for b in range(py)]
    both = {e: pair(p_ref[e[0], 2 * e[1]], p_ref[e[0], 2 * e[1] + 1]) for e in pairs}
    tidy = {e: dot(clean, both[e]).astype(jnp.bfloat16) for e in pairs}
    for x, b in pairs:
        left_ref[x * py + b] = transposed_dot(spread, both[x, b]).astype(jnp.bfloat16)
        zdn_ref[x * py + b] = tidy[x, b][:blk]
        zup_ref[x * py + b] = tidy[x, b][blk:]
    for a in range(px):
        one, two = tidy[2 * a, 0], tidy[2 * a + 1, 0]
        ydn_ref[a] = jnp.concatenate([one[:, :blk], two[:, :blk]], axis=1)
        one, two = tidy[2 * a, py - 1], tidy[2 * a + 1, py - 1]
        yup_ref[a] = jnp.concatenate([one[:, blk:], two[:, blk:]], axis=1)
    for b in range(py):
        for z, ref in enumerate((zdn_ref, zup_ref)):
            xface_ref[b, z * blk : (z + 1) * blk] = ref[jnp.where(me == 0, nx - 1, 0) * py + b]
    copy.wait()

    for x, y in [(x, y) for x in range(nx) for y in range(ny)]:
        here = a_ref.at[x, y]
        along_z = here[6] * first + here[5] * second
        right = jnp.concatenate(
            [pair(here[0], here[2 - x % 2]), pair(here[4 - y % 2], along_z)], axis=1
        )
        left = left_factors(left_ref[x * py + y // 2], y % 2, masks)
        got = dot(left, right).astype(jnp.bfloat16)
        parts = unpair(got[:, : 2 * blk]) + unpair(got[:, 2 * blk :])
        for k in range(4):
            part_ref[x, y, k] = parts[k]

    sent, kept = places(route_ref, where_ref, table_ref, dims, nb)
    codes_ref[...] = jnp.zeros_like(codes_ref)
    for i in range(aggregates):
        a, b, z, t = i // (py * nz * 2), (i // (nz * 2)) % py, (i // 2) % nz, i % 2
        code = (2 * (jnp.where(pair_ref[a, b, z] == 0, 2, 1) - t) + z).astype(jnp.float32)
        line = jnp.full((1, LANES), code, jnp.float32)
        codes_ref[pl.ds(where_ref[2, i], 1), :] = line
        codes_ref[pl.ds(where_ref[3, i], 1), :] = line

    for a, b in [(a, b) for a in range(px) for b in range(py)]:
        own, with_x, with_y, with_z = {}, {}, {}, {}
        for z, ref in enumerate((zdn_ref, zup_ref)):
            zs, zo = pl.ds(z * q, q), pl.ds((1 - z) * q, q)
            for u in range(2):
                x = 2 * a + u
                weight = weights_of(ref[x * py + b])
                for v in range(2):
                    y = 2 * b + v
                    stack = jnp.concatenate(
                        [
                            part_ref[x, y, 0, zs],
                            part_ref[2 * a + 1 - u, y, 1, zs],
                            part_ref[x, 2 * b + 1 - v, 2, zs],
                            part_ref[x, y, 3, zo],
                        ],
                        axis=0,
                    )
                    got = dot(stack, weight[v])
                    own[u, v, z] = got[:q]
                    with_x[1 - u, v, z] = got[q : 2 * q]
                    with_y[u, 1 - v, z] = got[2 * q : 3 * q]
                    with_z[u, v, 1 - z] = got[3 * q :]
        for z in range(nz):
            flat = pair_ref[a, b, z] == 0
            i = ((a * py + b) * nz + z) * 2
            sums = {}
            for u in range(2):
                for v in range(2):
                    t = u if u == v else jnp.where(flat, v, u)
                    m = u if u == v else jnp.where(flat, u, v)
                    e = (u, v, z)
                    sums[u, v] = own[e] + jnp.where(flat, with_x[e], with_y[e])
                    cross = jnp.where(flat, with_y[e], with_x[e])
                    put(total_ref, where_ref, i + t, 1 + m, rows, cross)
                    put(total_ref, where_ref, i + t, 3 + m, rows, with_z[e])
            put(total_ref, where_ref, i, 0, rows, sums[0, 0] + jnp.where(flat, sums[1, 0], sums[0, 1]))
            put(total_ref, where_ref, i + 1, 0, rows, sums[1, 1] + jnp.where(flat, sums[0, 1], sums[1, 0]))

    for kind, (out, count) in enumerate(((send_ref, sent), (keep_ref, kept))):
        finish(((out, nb),), total_ref, kind, dims, count)
        out[nb * rows :] = codes_ref[kind * 2 * SUB : (kind + 1) * 2 * SUB].astype(jnp.bfloat16)


def outer_left_kernel(grid, left_ref, a_hbm, part_ref, a_ref, sems):
    px, py, _ = grid
    nx, ny = 2 * px, 2 * py
    blk = a_ref.shape[3]
    copy = pltpu.make_async_copy(a_hbm, a_ref, sems.at[0])
    copy.start()
    masks = even_lanes(blk // 2)
    first, second = even_rows(blk)
    copy.wait()
    for x, y in [(x, y) for x in range(nx) for y in range(ny)]:
        here = a_ref.at[x, y]
        along_z = here[5] * first + here[6] * second
        low, high = halves(along_z)
        right = jnp.concatenate(
            [pair(here[1 + x % 2], here[3 + y % 2]), jnp.concatenate([low, high], axis=0)], axis=1
        )
        left = left_factors(left_ref[x * py + y // 2], y % 2, masks)
        got = dot(left, right).astype(jnp.bfloat16)
        part_ref[x, y, 0], part_ref[x, y, 1] = unpair(got[:, : 2 * blk])
        along = got[:, 2 * blk :]
        part_ref[x, y, 2] = jnp.concatenate([along[:blk], along[blk:]], axis=1)


def outer_kernel(
    dims, grid, route_ref, pair_ref, part_ref, zup_ref, zdn_ref,
    xface_hbm, ylow_hbm, yhigh_hbm, zlow_hbm, zhigh_hbm,
    send_xy_ref, send_z_ref, keep_xy_ref, keep_z_ref,
    xface_ref, ylow_ref, yhigh_ref, zlow_ref, zhigh_ref, total_ref, where_ref, table_ref, sems,
):
    px, py, nz = grid
    _, _, rows = dims
    nx, ny = 2 * px, 2 * py
    blk = part_ref.shape[3]
    q = blk // 2
    nb = 6
    copies = [
        pltpu.make_async_copy(one, two, sems.at[k])
        for k, (one, two) in enumerate((
            (xface_hbm, xface_ref), (ylow_hbm, ylow_ref), (yhigh_hbm, yhigh_ref),
            (zlow_hbm, zlow_ref), (zhigh_hbm, zhigh_ref),
        ))
    ]
    for copy in copies:
        copy.start()
    sent, kept = places(route_ref, where_ref, table_ref, dims, nb)
    me = lax.axis_index("gx")
    above = (iota((blk, LANES), 0) * 0 + me) > 0
    for copy in copies:
        copy.wait()

    def beside_x(x, b, z, u):
        to = x - 1 if u == 0 else x + 1
        if 0 <= to < nx:
            return (zdn_ref, zup_ref)[z][to * py + b]
        part = xface_ref[b, z * blk : (z + 1) * blk].astype(jnp.float32)
        part = jnp.where(above, part, 0.0) if u == 0 else jnp.where(above, 0.0, part)
        return part.astype(jnp.bfloat16)

    def beside_y(x, y, z, v):
        to = y - 1 if v == 0 else y + 1
        if 0 <= to < ny:
            return (zdn_ref, zup_ref)[z][x * py + to // 2], to % 2
        ref = ylow_ref if v == 0 else yhigh_ref
        return ref[x // 2, z * blk : (z + 1) * blk], x % 2

    for x in range(nx):
        made = []
        for b, z in [(b, z) for b in range(py) for z in range(nz)]:
            zs = pl.ds(z * q, q)
            u, a = x % 2, x // 2
            along_x = weights_of(beside_x(x, b, z, u))
            along_z = weights_of((zlow_ref, zhigh_ref)[z][x * py + b])
            flat = pair_ref[a, b, z] == 0
            for v in range(2):
                y = 2 * b + v
                t = u if u == v else jnp.where(flat, v, u)
                m = u if u == v else jnp.where(flat, u, v)
                i = ((a * py + b) * nz + z) * 2 + t
                other, k = beside_y(x, y, z, v)
                along_y = weights_of(other)[k]
                made.append((i, 2 * m, dot(part_ref[x, y, 0, zs], along_x[v])))
                made.append((i, 2 * m + 1, dot(part_ref[x, y, 1, zs], along_y)))
                made.append((i, 4 + m, dot(part_ref[x, y, 2, zs], along_z[v])))
        for i, block, got in made:
            put(total_ref, where_ref, i, block, rows, got)

    for kind, (xy, along, count) in enumerate((
        (send_xy_ref, send_z_ref, sent), (keep_xy_ref, keep_z_ref, kept),
    )):
        finish(((xy, 4), (along, 2)), total_ref, kind, dims, count)


def placed_blocks(early_ref, xy_ref, z_ref, codes, rows, at, size):
    code = jnp.concatenate([codes, codes], axis=0)
    near_low, near_high = (code < 1.5)[None], (code > 3.5)[None]
    upper = ((code == 1.0) | (code == 3.0) | (code == 5.0))[None]

    def tiles(ref, k):
        return ref[k * rows + at : k * rows + at + size].reshape(-1, 2 * SUB, LANES)

    if xy_ref is not None:
        yield 0, tiles(early_ref, 0)
        for m in range(2):
            cross, x_out, y_out = tiles(early_ref, 1 + m), tiles(xy_ref, 2 * m), tiles(xy_ref, 2 * m + 1)
            yield 1 + 5 * m, jnp.where(near_low, cross, x_out)
            yield 2 + 5 * m, jnp.where(near_low, x_out, jnp.where(near_high, y_out, cross))
            yield 3 + 5 * m, jnp.where(near_high, cross, y_out)
    if z_ref is not None:
        for m in range(2):
            z_in, z_out = tiles(early_ref, 3 + m), tiles(z_ref, m)
            yield 4 + 5 * m, jnp.where(upper, z_in, z_out)
            yield 5 + 5 * m, jnp.where(upper, z_out, z_in)


def keep_kernel(dims, early_ref, xy_ref, z_ref, half_ref, out_hbm, full_ref, sem):
    cap, rows = dims
    full = (cap - cap % SUB) * (rows // cap)
    me = lax.axis_index("gx")
    codes = early_ref[5 * rows :]
    copies = []
    for k, value in placed_blocks(early_ref, xy_ref, z_ref, codes[:SUB], rows, 0, full):
        full_ref[k] = value.reshape(full, LANES)
        to = out_hbm.at[k, pl.ds(me * (2 * full), full), :]
        copies.append(pltpu.make_async_copy(full_ref.at[k], to, sem.at[k]))
        copies[-1].start()
    for k, value in placed_blocks(early_ref, xy_ref, z_ref, codes[SUB:], rows, full, rows - full):
        half_ref[k] = value.reshape(rows - full, LANES)
    for copy in copies:
        copy.wait()


def take_kernel(dims, with_xy, early_ref, late_ref, half_ref, _, out_hbm, full_ref, mixed_ref, sem):
    cap, rows = dims
    full = (cap - cap % SUB) * (rows // cap)
    me = lax.axis_index("gx")
    codes = early_ref[5 * rows :]
    xy_ref, z_ref = (late_ref, None) if with_xy else (None, late_ref)
    copies = []
    for k, value in placed_blocks(early_ref, xy_ref, z_ref, codes[:SUB], rows, 0, full):
        full_ref[k] = value.reshape(full, LANES)
        to = out_hbm.at[k, pl.ds((1 - me) * (2 * full), full), :]
        copies.append(pltpu.make_async_copy(full_ref.at[k], to, sem.at[0, k]))
        copies[-1].start()
    first_half = (iota((SUB, LANES), 0) < SUB // 2)[None]
    pick = first_half == (me == 0)
    for k, value in placed_blocks(early_ref, xy_ref, z_ref, codes[SUB:], rows, full, rows - full):
        theirs = value.reshape(rows - full, LANES).astype(jnp.float32).reshape(-1, SUB, LANES)
        mine = half_ref[k].astype(jnp.float32).reshape(-1, SUB, LANES)
        low = jnp.where(pick, mine, theirs)
        high = pltpu.roll(jnp.where(pick, theirs, mine), SUB // 2, 1)
        mixed_ref[k, : rows - full] = low.reshape(rows - full, LANES).astype(jnp.bfloat16)
        mixed_ref[k, rows - full :] = high.reshape(rows - full, LANES).astype(jnp.bfloat16)
        to = out_hbm.at[k, full : 2 * full, :]
        copies.append(pltpu.make_async_copy(mixed_ref.at[k], to, sem.at[1, k]))
        copies[-1].start()
    for copy in copies:
        copy.wait()


SMEM = pl.BlockSpec(memory_space=pltpu.SMEM)
VMEM = pl.BlockSpec(memory_space=pltpu.VMEM)
ANY = pl.BlockSpec(memory_space=pl.ANY)


def bf16(*shape):
    return jax.ShapeDtypeStruct(shape, jnp.bfloat16)


def local(a_blocks, prolong, pairing, route):
    devices_gx = lax.axis_size("gx")
    aggregates = route.shape[0]
    capacity = max(2, 3 * aggregates // (2 * devices_gx))
    nx, ny, nz, faces, entries = a_blocks.shape
    fits = (
        devices_gx == 2
        and nz == 2
        and nx % 2 == 0
        and ny % 2 == 0
        and faces == 7
        and entries == (LANES // 2) ** 2
        and capacity // SUB == 1
        and capacity % SUB == SUB // 2
    )
    if not fits:
        return general(a_blocks, prolong, pairing, route, capacity)
    px, py = nx // 2, ny // 2
    blk = math.isqrt(entries)
    lines = entries // LANES
    a_view = a_blocks.transpose(0, 1, 3, 2, 4).reshape(nx, ny, faces, nz, lines, LANES)
    a_view = a_view.transpose(0, 1, 2, 4, 3, 5).reshape(nx, ny, faces, nz * lines, LANES)
    p_view = prolong.reshape(nx, ny, nz, lines, LANES).transpose(0, 1, 3, 2, 4)
    p_view = p_view.reshape(nx, ny, nz * lines, LANES)
    route_row = route.reshape(1, aggregates)
    rows = capacity * lines
    dims, grid = (aggregates, capacity, rows), (px, py, nz)
    f32 = jnp.float32
    half_type = jnp.bfloat16
    face_x, face_y, face_z = (py, 2 * blk, LANES), (px, 2 * blk, LANES), (nx * py, blk, LANES)
    parts = (nx, ny, 3, blk, LANES)
    room = pltpu.CompilerParams(vmem_limit_bytes=67_043_328)
    cost = pl.CostEstimate(flops=10**9, bytes_accessed=4 * 10**6, transcendentals=0)

    send_0, keep_0, xface, yup, ydn, zup, zdn, left = pl.pallas_call(
        functools.partial(inner_kernel, dims, grid),
        out_shape=(
            bf16(5 * rows + 2 * SUB, LANES),
            bf16(5 * rows + 2 * SUB, LANES),
            bf16(*face_x),
            bf16(*face_y),
            bf16(*face_y),
            bf16(*face_z),
            bf16(*face_z),
            bf16(nx * py, 2 * blk, LANES),
        ),
        in_specs=[SMEM, SMEM, VMEM, ANY],
        out_specs=[VMEM] * 8,
        scratch_shapes=[
            pltpu.VMEM(a_view.shape, half_type),
            pltpu.VMEM((nx, ny, 4, blk, LANES), half_type),
            pltpu.VMEM((10 * rows, LANES), f32),
            pltpu.VMEM((4 * SUB, LANES), f32),
            pltpu.SMEM((4, aggregates), jnp.int32),
            pltpu.SMEM((4, capacity), jnp.int32),
            pltpu.SemaphoreType.DMA((1,)),
        ],
        compiler_params=room,
        cost_estimate=cost,
        name="inner_blocks",
    )(route_row, pairing, p_view, a_view)

    def chain(axis):
        n = lax.axis_size(axis)
        up = [(i, i + 1) for i in range(n - 1)]
        return up, [(j, i) for i, j in up]

    swap = [(0, 1), (1, 0)]
    xface = lax.ppermute(xface, "gx", swap)
    got_0 = lax.ppermute(send_0, "gx", swap)
    up, down = chain("gy")
    ylow = lax.ppermute(yup, "gy", up)
    yhigh = lax.ppermute(ydn, "gy", down)
    up, down = chain("gz")
    zlow = lax.ppermute(zup, "gz", up)
    zhigh = lax.ppermute(zdn, "gz", down)

    part = pl.pallas_call(
        functools.partial(outer_left_kernel, grid),
        out_shape=bf16(*parts),
        in_specs=[VMEM, ANY],
        out_specs=VMEM,
        scratch_shapes=[pltpu.VMEM(a_view.shape, half_type), pltpu.SemaphoreType.DMA((1,))],
        compiler_params=room,
        cost_estimate=cost,
        name="outer_left",
    )(left, a_view)
    send_xy, send_z, keep_xy, keep_z = pl.pallas_call(
        functools.partial(outer_kernel, dims, grid),
        out_shape=(bf16(4 * rows, LANES), bf16(2 * rows, LANES)) * 2,
        in_specs=[SMEM, SMEM, VMEM, VMEM, VMEM] + [ANY] * 5,
        out_specs=[VMEM] * 4,
        scratch_shapes=[
            pltpu.VMEM(face_x, half_type),
            pltpu.VMEM(face_y, half_type),
            pltpu.VMEM(face_y, half_type),
            pltpu.VMEM(face_z, half_type),
            pltpu.VMEM(face_z, half_type),
            pltpu.VMEM((12 * rows, LANES), f32),
            pltpu.SMEM((4, aggregates), jnp.int32),
            pltpu.SMEM((4, capacity), jnp.int32),
            pltpu.SemaphoreType.DMA((5,)),
        ],
        compiler_params=pltpu.CompilerParams(vmem_limit_bytes=67_043_328 - 1400 * 1024),
        cost_estimate=cost,
        name="outer_blocks",
    )(route_row, pairing, part, zup, zdn, xface, ylow, yhigh, zlow, zhigh)
    got_xy = lax.ppermute(send_xy, "gx", swap)
    got_z = lax.ppermute(send_z, "gx", swap)

    full = (capacity // SUB) * SUB * lines
    whole = 2 * rows
    half, out = pl.pallas_call(
        functools.partial(keep_kernel, (capacity, rows)),
        out_shape=(bf16(11, rows - full, LANES), bf16(11, whole, LANES)),
        in_specs=[VMEM] * 3,
        out_specs=[VMEM, ANY],
        scratch_shapes=[pltpu.VMEM((11, full, LANES), half_type), pltpu.SemaphoreType.DMA((11,))],
        compiler_params=room,
        cost_estimate=cost,
        name="place_kept",
    )(keep_0, keep_xy, keep_z)
    for with_xy, late in ((True, got_xy), (False, got_z)):
        out = pl.pallas_call(
            functools.partial(take_kernel, (capacity, rows), with_xy),
            out_shape=bf16(11, whole, LANES),
            in_specs=[VMEM] * 3 + [ANY],
            out_specs=ANY,
            input_output_aliases={3: 0},
            scratch_shapes=[
                pltpu.VMEM((11, full, LANES), half_type),
                pltpu.VMEM((11, full, LANES), half_type),
                pltpu.SemaphoreType.DMA((2, 11)),
            ],
            compiler_params=room,
            cost_estimate=cost,
            name="place_xy" if with_xy else "place_z",
        )(got_0, late, half, out)
    out = out.reshape(11, whole // (SUB * lines), lines, SUB, LANES).transpose(1, 3, 0, 2, 4)
    return out.reshape(2 * capacity, 11, entries)


def solution(mesh):
    placed = (
        P("gx", "gy", "gz", None, None),
        P("gx", "gy", "gz", None),
        P("gx", "gy", "gz"),
        P(("gx", "gy", "gz"), None),
    )
    return jax.shard_map(
        local,
        mesh=mesh,
        in_specs=placed,
        out_specs=P(("gx", "gy", "gz"), None, None),
        check_vma=False,
    )
```

time: 58.4 us -> 46.1 us (0.79)
  waiting for transfers between devices: 27 us -> 10 us
  Pallas kernels: 16.8 us -> 20.7 us
  starting transfers between devices: 12.9 us -> 14.5 us
  local copies, waits for them, and re-layouts: 1.31 us -> 0 us
    ppermute x1, waiting for transfers between devices: 21.9 us -> 0.01 us  [local(): got_0 = lax.ppermute(send_0, 'gx', swap)]
    ppermute x1 -> x2, waiting for transfers between devices: 0.01 us -> 9.39 us  [the longest x1 7.54 us: local(): got_xy = lax.ppermute(send_xy, 'gx', swap)]
    pallas_call x1 -> x3, Pallas kernels: 2.59 us -> 8.53 us  [the longest x2 4.6 us: local(): pl.pallas_call(functools.partial(take_kernel, (capacity, rows), with_xy),...]
    ppermute x1, waiting for transfers between devices: 4.17 us -> 0.6 us  [local(): yhigh = lax.ppermute(ydn, 'gy', down)]
    ppermute x1 -> x2, starting transfers between devices: 0.59 us -> 2.09 us  [the longest x1 1.17 us: local(): got_z = lax.ppermute(send_z, 'gx', swap)]
    pallas_call x1, Pallas kernels: 5.92 us -> 4.46 us  [local(): pl.pallas_call(functools.partial(outer_kernel, dims, grid), out_shape=(bf...]
    unnamed x10 -> x0, local copies, waits for them, and re-layouts: 1.31 us -> none
    ppermute x1, waiting for transfers between devices: 0.88 us -> 0.01 us  [local(): ylow = lax.ppermute(yup, 'gy', up)]
  transfers between devices with their start and end apart: 7 -> 8, of which waited for: 3 -> 3; matrix products, arithmetic and copies ran while one was open for 0% -> 0% of each run, Pallas kernels for 5% -> 30%
where the time goes in v1:
time: 46.1 us; the launch traced here: 45.2 us
  Pallas kernels  20.7 us (45%)
  starting transfers between devices  14.5 us (31%)
  waiting for transfers between devices  10 us (22%)
    ppermute x1, waiting for transfers between devices, local(): got_xy = lax.ppermute(send_xy, 'gx', swap)  7.54 us
    pallas_call x1, Pallas kernels, local(): pl.pallas_call(functools.partial(inner_kernel, dims, grid), out_shape=(bf...  4.79 us
    pallas_call x2, Pallas kernels, local(): pl.pallas_call(functools.partial(take_kernel, (capacity, rows), with_xy),...  4.6 us
    pallas_call x1, Pallas kernels, local(): pl.pallas_call(functools.partial(outer_kernel, dims, grid), out_shape=(bf...  4.46 us
    ppermute x1, starting transfers between devices, local(): ylow = lax.ppermute(yup, 'gy', up)  4.12 us
    pallas_call x1, Pallas kernels, local(): pl.pallas_call(functools.partial(outer_left_kernel, grid), out_shape=bf16...  3.92 us
    ppermute x1, starting transfers between devices, local(): xface = lax.ppermute(xface, 'gx', swap)  2.99 us
    pallas_call x1, Pallas kernels, local(): pl.pallas_call(functools.partial(keep_kernel, (capacity, rows)), out_shap...  2.89 us
  transfers between devices with their start and end apart: 8, of which 3 were waited for; matrix products, arithmetic and copies ran while one was open for 0% of the time, Pallas kernels for 30%

profile of v1, /device:TPU:0, one launch (start us, length us, event | category | flops | bytes accessed | tf_op | source)
XLA Modules:
  0.0 45.2 jit_solution(3231238251322202203)
XLA Ops:
  0.0 4.8 %inner_blocks.1 = (bf16[1936,128]{1,0:T(8,128)(2,1)}, bf16[1936,128]{1,0:T(8,128)(2,1)}, bf16[2,128,128]{2,1,0:T(8,128)(2,1)}, bf16[2,128,128]{2,1,0:T(8,128)(2,...) custom-call(s32[1,16]{1,0:T(1,128)} %bitcast.21, ...), custom_call_target="tpu_custom_call" | custom-call | flops 1000000000 | bytes 4000000 | tf_op jit(solution)/shard_map/inner_blocks/pallas_call | solution.py:567
  4.8 3.0 %collective-permute-start.1 = (bf16[2,128,128]{2,1,0:T(8,128)(2,1)}, bf16[2,128,128]{2,1,0:T(8,128)(2,1)}, u32[]{:S(2)}, u32[]{:S(2)}) collective-permute-start(bf16[2,128,128]{2,1,0:T(8,128)(2,1)} %get-tuple-element.23), channel_id=1, source_target_pairs={{0,16},{16,0},{1,17},{17,1},{2,18},{18,2},{3,19},{19,3},{4,20},{20... | collective-permute-start | bytes 196616 | tf_op jit(solution)/shard_map/ppermute | solution.py:601
  7.8 2.1 %collective-permute-start.4 = (bf16[8,64,128]{2,1,0:T(8,128)(2,1)}, bf16[8,64,128]{2,1,0:T(8,128)(2,1)}, u32[]{:S(2)}, u32[]{:S(2)}) collective-permute-start(bf16[8,64,128]{2,1,0:T(8,128)(2,1)} %get-tuple-element.21.zup_ref), channel_id=1, source_target_pairs={{0,1},{1,2},{2,3},{4,5},{5,6},{6,7},{8,9},{9,10},{10,11},{12,13},{... | collective-permute-start | bytes 393224 | tf_op jit(solution)/shard_map/ppermute | solution.py:607
  9.9 1.3 %collective-permute-start.5 = (bf16[8,64,128]{2,1,0:T(8,128)(2,1)}, bf16[8,64,128]{2,1,0:T(8,128)(2,1)}, u32[]{:S(2)}, u32[]{:S(2)}) collective-permute-start(bf16[8,64,128]{2,1,0:T(8,128)(2,1)} %get-tuple-element.22.zdn_ref), channel_id=1, source_target_pairs={{1,0},{2,1},{3,2},{5,4},{6,5},{7,6},{9,8},{10,9},{11,10},{13,12},{... | collective-permute-start | bytes 393224 | tf_op jit(solution)/shard_map/ppermute | solution.py:608
  11.2 4.1 %collective-permute-start.2 = (bf16[2,128,128]{2,1,0:T(8,128)(2,1)}, bf16[2,128,128]{2,1,0:T(8,128)(2,1)}, u32[]{:S(2)}, u32[]{:S(2)}) collective-permute-start(bf16[2,128,128]{2,1,0:T(8,128)(2,1)} %get-tuple-element.24), channel_id=1, source_target_pairs={{0,4},{4,8},{8,12},{1,5},{5,9},{9,13},{2,6},{6,10},{10,14},{3,7},{... | collective-permute-start | bytes 196616 | tf_op jit(solution)/shard_map/ppermute | solution.py:604
  15.3 1.3 %collective-permute-start.3 = (bf16[2,128,128]{2,1,0:T(8,128)(2,1)}, bf16[2,128,128]{2,1,0:T(8,128)(2,1)}, u32[]{:S(2)}, u32[]{:S(2)}) collective-permute-start(bf16[2,128,128]{2,1,0:T(8,128)(2,1)} %get-tuple-element.25), channel_id=1, source_target_pairs={{4,0},{8,4},{12,8},{5,1},{9,5},{13,9},{6,2},{10,6},{14,10},{7,3},{... | collective-permute-start | bytes 196616 | tf_op jit(solution)/shard_map/ppermute | solution.py:605
  16.6 0.0 collective-permute-done.1.xface_hbm
  16.6 0.6 %collective-permute-start = (bf16[1936,128]{1,0:T(8,128)(2,1)}, bf16[1936,128]{1,0:T(8,128)(2,1)}, u32[]{:S(2)}, u32[]{:S(2)}) collective-permute-start(bf16[1936,128]{1,0:T(8,128)(2,1)} %get-tuple-element.19), channel_id=1, source_target_pairs={{0,16},{16,0},{1,17},{17,1},{2,18},{18,2},{3,19},{19,3},{4,20},{20... | collective-permute-start | bytes 1486856 | tf_op jit(solution)/shard_map/ppermute | solution.py:602
  17.2 3.9 %outer_left.1.part_ref = bf16[4,4,3,64,128]{4,3,2,1,0:T(8,128)(2,1)} custom-call(bf16[8,128,128]{2,1,0:T(8,128)(2,1)} %get-tuple-element.20.left_ref, bf16[4,4,7,64,128]{4,3,2,1,0:T(8,128)(2,1)} %bitcast.19), custom_call_target="tpu_custom_call" | custom-call | flops 1000000000 | bytes 4000000 | tf_op jit(solution)/shard_map/outer_left/pallas_call | solution.py:610
  21.2 0.0 collective-permute-done.2.ylow_hbm
  21.2 0.6 %collective-permute-done.3.yhigh_hbm = bf16[2,128,128]{2,1,0:T(8,128)(2,1)} collective-permute-done((bf16[2,128,128]{2,1,0:T(8,128)(2,1)}, bf16[2,128,128]{2,1,0:T(8,128)(2,1)}, u32[]{:S(2)}, u32[]{:S(2)}) %collective-permute-start.3) | collective-permute-done | bytes 65568 | tf_op jit(solution)/shard_map/ppermute | solution.py:605
  21.8 0.0 collective-permute-done.4.zlow_hbm
  21.8 0.0 collective-permute-done.5.zhigh_hbm
  21.8 4.5 %outer_blocks.1 = (bf16[1536,128]{1,0:T(8,128)(2,1)}, bf16[768,128]{1,0:T(8,128)(2,1)}, bf16[1536,128]{1,0:T(8,128)(2,1)}, bf16[768,128]{1,0:T(8,128)(2,1)}) custom-call(s32[1,16]{1,0:T(1,128)} %bitcast.22, s32[2,2,2]{2,1,0:T(2,128)} %pair_ref.3, bf16[4,4,3,64,128]{4,3,2,1,0:T(8,128)(2,1)} %outer_left.1.part_ref, ...), custom_call_target="tpu_custom_call" | custom-call | flops 1000000000 | bytes 4000000 | tf_op jit(solution)/shard_map/outer_blocks/pallas_call | solution.py:620
  26.2 0.9 %collective-permute-start.7 = (bf16[1536,128]{1,0:T(8,128)(2,1)}, bf16[1536,128]{1,0:T(8,128)(2,1)}, u32[]{:S(2)}, u32[]{:S(2)}) collective-permute-start(bf16[1536,128]{1,0:T(8,128)(2,1)} %get-tuple-element.31), channel_id=1, source_target_pairs={{0,16},{16,0},{1,17},{17,1},{2,18},{18,2},{3,19},{19,3},{4,20},{20... | collective-permute-start | bytes 1179656 | tf_op jit(solution)/shard_map/ppermute | solution.py:640
  27.2 1.2 %collective-permute-start.6 = (bf16[768,128]{1,0:T(8,128)(2,1)}, bf16[768,128]{1,0:T(8,128)(2,1)}, u32[]{:S(2)}, u32[]{:S(2)}) collective-permute-start(bf16[768,128]{1,0:T(8,128)(2,1)} %get-tuple-element.26), channel_id=1, source_target_pairs={{0,16},{16,0},{1,17},{17,1},{2,18},{18,2},{3,19},{19,3},{4,20},{20... | collective-permute-start | bytes 589832 | tf_op jit(solution)/shard_map/ppermute | solution.py:641
  28.3 2.9 %place_kept.1 = (bf16[11,128,128]{2,1,0:T(8,128)(2,1)}, bf16[11,768,128]{2,1,0:T(8,128)(2,1)}) custom-call(bf16[1936,128]{1,0:T(8,128)(2,1)} %get-tuple-element.27.early_ref, bf16[1536,128]{1,0:T(8,128)(2,1)} %get-tuple-element.28.xy_ref, bf16[768,128]{1,0:T(8,128)(2,1)} %get-tuple-element.29.z_ref), custom_call_target="tpu_custom_call" | custom-call | flops 1000000000 | bytes 4000000 | tf_op jit(solution)/shard_map/place_kept/pallas_call | solution.py:645
  31.2 0.0 collective-permute-done.early_ref
  31.2 7.5 %collective-permute-done.7.late_ref = bf16[1536,128]{1,0:T(8,128)(2,1)} collective-permute-done((bf16[1536,128]{1,0:T(8,128)(2,1)}, bf16[1536,128]{1,0:T(8,128)(2,1)}, u32[]{:S(2)}, u32[]{:S(2)}) %collective-permute-start.7) | collective-permute-done | bytes 393248 | tf_op jit(solution)/shard_map/ppermute | solution.py:640
  38.8 2.4 %place_xy.1._ = bf16[11,768,128]{2,1,0:T(8,128)(2,1)} custom-call(bf16[1936,128]{1,0:T(8,128)(2,1)} %collective-permute-done.early_ref, bf16[1536,128]{1,0:T(8,128)(2,1)} %collective-permute-done.7.late_ref, bf16[11,128,128]{2,1,0:T(8,128)(2,1)} %get-tuple-element.30.half_ref, bf16[11,768,128]{2,1,0:T(8,128)(2,1)} %get-tuple-element.32._), custom_call_target="tpu_custom_call", output_to_operand_aliasing={{}: (3, {})} | custom-call | flops 1000000000 | bytes 4000000 | tf_op jit(solution)/shard_map/place_xy/pallas_call | solution.py:656
  41.2 1.8 %collective-permute-done.6.late_ref = bf16[768,128]{1,0:T(8,128)(2,1)} collective-permute-done((bf16[768,128]{1,0:T(8,128)(2,1)}, bf16[768,128]{1,0:T(8,128)(2,1)}, u32[]{:S(2)}, u32[]{:S(2)}) %collective-permute-start.6) | collective-permute-done | bytes 196640 | tf_op jit(solution)/shard_map/ppermute | solution.py:641
  43.0 2.2 %place_z.1 = bf16[11,768,128]{2,1,0:T(8,128)(2,1)} custom-call(bf16[1936,128]{1,0:T(8,128)(2,1)} %collective-permute-done.early_ref, bf16[768,128]{1,0:T(8,128)(2,1)} %collective-permute-done.6.late_ref, bf16[11,128,128]{2,1,0:T(8,128)(2,1)} %get-tuple-element.30.half_ref, bf16[11,768,128]{2,1,0:T(8,128)(2,1)} %place_xy.1._), custom_call_target="tpu_custom_call", output_to_operand_aliasing={{}: (3, {})} | custom-call | flops 1000000000 | bytes 4000000 | tf_op jit(solution)/shard_map/place_z/pallas_call | solution.py:656
Async XLA Ops:
  4.8 11.8 %collective-permute-start.1 = (bf16[2,128,128]{2,1,0:T(8,128)(2,1)}, bf16[2,128,128]{2,1,0:T(8,128)(2,1)}, u32[]{:S(2)}, u32[]{:S(2)}) collective-permute-start(bf16[2,128,128]{2,1,0:T(8,128)(2,1)} %get-tuple-element.23), channel_id=1, source_target_pairs={{0,16},{16,0},{1,17},{17,1},{2,18},{18,2},{3,19},{19,3},{4,20},{20... | collective-permute-start | bytes 196616 | tf_op jit(solution)/shard_map/ppermute | solution.py:601
  7.8 14.0 %collective-permute-start.4 = (bf16[8,64,128]{2,1,0:T(8,128)(2,1)}, bf16[8,64,128]{2,1,0:T(8,128)(2,1)}, u32[]{:S(2)}, u32[]{:S(2)}) collective-permute-start(bf16[8,64,128]{2,1,0:T(8,128)(2,1)} %get-tuple-element.21.zup_ref), channel_id=1, source_target_pairs={{0,1},{1,2},{2,3},{4,5},{5,6},{6,7},{8,9},{9,10},{10,11},{12,13},{... | collective-permute-start | bytes 393224 | tf_op jit(solution)/shard_map/ppermute | solution.py:607
  9.9 11.9 %collective-permute-start.5 = (bf16[8,64,128]{2,1,0:T(8,128)(2,1)}, bf16[8,64,128]{2,1,0:T(8,128)(2,1)}, u32[]{:S(2)}, u32[]{:S(2)}) collective-permute-start(bf16[8,64,128]{2,1,0:T(8,128)(2,1)} %get-tuple-element.22.zdn_ref), channel_id=1, source_target_pairs={{1,0},{2,1},{3,2},{5,4},{6,5},{7,6},{9,8},{10,9},{11,10},{13,12},{... | collective-permute-start | bytes 393224 | tf_op jit(solution)/shard_map/ppermute | solution.py:608
  11.2 10.0 %collective-permute-start.2 = (bf16[2,128,128]{2,1,0:T(8,128)(2,1)}, bf16[2,128,128]{2,1,0:T(8,128)(2,1)}, u32[]{:S(2)}, u32[]{:S(2)}) collective-permute-start(bf16[2,128,128]{2,1,0:T(8,128)(2,1)} %get-tuple-element.24), channel_id=1, source_target_pairs={{0,4},{4,8},{8,12},{1,5},{5,9},{9,13},{2,6},{6,10},{10,14},{3,7},{... | collective-permute-start | bytes 196616 | tf_op jit(solution)/shard_map/ppermute | solution.py:604
  15.3 6.5 %collective-permute-start.3 = (bf16[2,128,128]{2,1,0:T(8,128)(2,1)}, bf16[2,128,128]{2,1,0:T(8,128)(2,1)}, u32[]{:S(2)}, u32[]{:S(2)}) collective-permute-start(bf16[2,128,128]{2,1,0:T(8,128)(2,1)} %get-tuple-element.25), channel_id=1, source_target_pairs={{4,0},{8,4},{12,8},{5,1},{9,5},{13,9},{6,2},{10,6},{14,10},{7,3},{... | collective-permute-start | bytes 196616 | tf_op jit(solution)/shard_map/ppermute | solution.py:605
  16.6 14.6 %collective-permute-start = (bf16[1936,128]{1,0:T(8,128)(2,1)}, bf16[1936,128]{1,0:T(8,128)(2,1)}, u32[]{:S(2)}, u32[]{:S(2)}) collective-permute-start(bf16[1936,128]{1,0:T(8,128)(2,1)} %get-tuple-element.19), channel_id=1, source_target_pairs={{0,16},{16,0},{1,17},{17,1},{2,18},{18,2},{3,19},{19,3},{4,20},{20... | collective-permute-start | bytes 1486856 | tf_op jit(solution)/shard_map/ppermute | solution.py:602
  26.2 12.5 %collective-permute-start.7 = (bf16[1536,128]{1,0:T(8,128)(2,1)}, bf16[1536,128]{1,0:T(8,128)(2,1)}, u32[]{:S(2)}, u32[]{:S(2)}) collective-permute-start(bf16[1536,128]{1,0:T(8,128)(2,1)} %get-tuple-element.31), channel_id=1, source_target_pairs={{0,16},{16,0},{1,17},{17,1},{2,18},{18,2},{3,19},{19,3},{4,20},{20... | collective-permute-start | bytes 1179656 | tf_op jit(solution)/shard_map/ppermute | solution.py:640
  27.2 15.8 %collective-permute-start.6 = (bf16[768,128]{1,0:T(8,128)(2,1)}, bf16[768,128]{1,0:T(8,128)(2,1)}, u32[]{:S(2)}, u32[]{:S(2)}) collective-permute-start(bf16[768,128]{1,0:T(8,128)(2,1)} %get-tuple-element.26), channel_id=1, source_target_pairs={{0,16},{16,0},{1,17},{17,1},{2,18},{18,2},{3,19},{19,3},{4,20},{20... | collective-permute-start | bytes 589832 | tf_op jit(solution)/shard_map/ppermute | solution.py:641

commit v2 on v1

--- a/solution.py
+++ b/solution.py
@@ -263,9 +263,9 @@
 
 
 def inner_kernel(
-    dims, grid, route_ref, pair_ref, p_ref, a_hbm,
-    send_ref, keep_ref, xface_ref, yup_ref, ydn_ref, zup_ref, zdn_ref, left_ref,
-    a_ref, part_ref, total_ref, codes_ref, where_ref, table_ref, sems,
+    dims, grid, route_hbm, pair_hbm, p_hbm, a_hbm,
+    send_ref, keep_ref, xface_ref, yup_ref, ydn_ref, zup_ref, zdn_ref, left_ref, a_ref,
+    p_ref, route_ref, pair_ref, part_ref, total_ref, codes_ref, where_ref, table_ref, sems,
 ):
     px, py, nz = grid
     aggregates, _, rows = dims
@@ -273,12 +273,20 @@
     blk = p_ref.shape[2]
     q = blk // 2
     nb = 5
-    copy = pltpu.make_async_copy(a_hbm, a_ref, sems.at[0])
-    copy.start()
+    copies = [
+        pltpu.make_async_copy(one, two, sems.at[k])
+        for k, (one, two) in enumerate((
+            (p_hbm, p_ref), (route_hbm, route_ref), (pair_hbm, pair_ref), (a_hbm, a_ref),
+        ))
+    ]
+    for copy in copies:
+        copy.start()
     clean, spread = constants(blk)
     masks = even_lanes(q)
     first, second = even_rows(blk)
     me = lax.axis_index("gx")
+    for copy in copies[:3]:
+        copy.wait()
 
     pairs = [(x, b) for x in range(nx) for b in range(py)]
     both = {e: pair(p_ref[e[0], 2 * e[1]], p_ref[e[0], 2 * e[1] + 1]) for e in pairs}
@@ -295,7 +303,7 @@
     for b in range(py):
         for z, ref in enumerate((zdn_ref, zup_ref)):
             xface_ref[b, z * blk : (z + 1) * blk] = ref[jnp.where(me == 0, nx - 1, 0) * py + b]
-    copy.wait()
+    copies[3].wait()
 
     for x, y in [(x, y) for x in range(nx) for y in range(ny)]:
         here = a_ref.at[x, y]
@@ -362,15 +370,12 @@
         out[nb * rows :] = codes_ref[kind * 2 * SUB : (kind + 1) * 2 * SUB].astype(jnp.bfloat16)
 
 
-def outer_left_kernel(grid, left_ref, a_hbm, part_ref, a_ref, sems):
+def outer_left_kernel(grid, left_ref, a_ref, part_ref):
     px, py, _ = grid
     nx, ny = 2 * px, 2 * py
     blk = a_ref.shape[3]
-    copy = pltpu.make_async_copy(a_hbm, a_ref, sems.at[0])
-    copy.start()
     masks = even_lanes(blk // 2)
     first, second = even_rows(blk)
-    copy.wait()
     for x, y in [(x, y) for x in range(nx) for y in range(ny)]:
         here = a_ref.at[x, y]
         along_z = here[5] * first + here[6] * second
@@ -387,9 +392,9 @@
 
 def outer_kernel(
     dims, grid, route_ref, pair_ref, part_ref, zup_ref, zdn_ref,
-    xface_hbm, ylow_hbm, yhigh_hbm, zlow_hbm, zhigh_hbm,
+    xface_ref, ylow_ref, yhigh_ref, zlow_ref, zhigh_ref,
     send_xy_ref, send_z_ref, keep_xy_ref, keep_z_ref,
-    xface_ref, ylow_ref, yhigh_ref, zlow_ref, zhigh_ref, total_ref, where_ref, table_ref, sems,
+    total_ref, where_ref, table_ref,
 ):
     px, py, nz = grid
     _, _, rows = dims
@@ -397,20 +402,9 @@
     blk = part_ref.shape[3]
     q = blk // 2
     nb = 6
-    copies = [
-        pltpu.make_async_copy(one, two, sems.at[k])
-        for k, (one, two) in enumerate((
-            (xface_hbm, xface_ref), (ylow_hbm, ylow_ref), (yhigh_hbm, yhigh_ref),
-            (zlow_hbm, zlow_ref), (zhigh_hbm, zhigh_ref),
-        ))
-    ]
-    for copy in copies:
-        copy.start()
     sent, kept = places(route_ref, where_ref, table_ref, dims, nb)
     me = lax.axis_index("gx")
     above = (iota((blk, LANES), 0) * 0 + me) > 0
-    for copy in copies:
-        copy.wait()
 
     def beside_x(x, b, z, u):
         to = x - 1 if u == 0 else x + 1
@@ -530,6 +524,14 @@
     return jax.ShapeDtypeStruct(shape, jnp.bfloat16)
 
 
+def near(*shape):
+    return pltpu.VMEM(shape, jnp.bfloat16)
+
+
+def held(*arrays):
+    return [pltpu.with_memory_space_constraint(one, pltpu.VMEM) for one in arrays]
+
+
 def local(a_blocks, prolong, pairing, route):
     devices_gx = lax.axis_size("gx")
     aggregates = route.shape[0]
@@ -561,36 +563,39 @@
     half_type = jnp.bfloat16
     face_x, face_y, face_z = (py, 2 * blk, LANES), (px, 2 * blk, LANES), (nx * py, blk, LANES)
     parts = (nx, ny, 3, blk, LANES)
-    room = pltpu.CompilerParams(vmem_limit_bytes=67_043_328)
+    room = pltpu.CompilerParams(vmem_limit_bytes=24 * 2**20)
     cost = pl.CostEstimate(flops=10**9, bytes_accessed=4 * 10**6, transcendentals=0)
 
-    send_0, keep_0, xface, yup, ydn, zup, zdn, left = pl.pallas_call(
+    send_0, keep_0, xface, yup, ydn, zup, zdn, left, a_near = pl.pallas_call(
         functools.partial(inner_kernel, dims, grid),
         out_shape=(
-            bf16(5 * rows + 2 * SUB, LANES),
-            bf16(5 * rows + 2 * SUB, LANES),
-            bf16(*face_x),
-            bf16(*face_y),
-            bf16(*face_y),
-            bf16(*face_z),
-            bf16(*face_z),
-            bf16(nx * py, 2 * blk, LANES),
+            near(5 * rows + 2 * SUB, LANES),
+            near(5 * rows + 2 * SUB, LANES),
+            near(*face_x),
+            near(*face_y),
+            near(*face_y),
+            near(*face_z),
+            near(*face_z),
+            near(nx * py, 2 * blk, LANES),
+            near(*a_view.shape),
         ),
-        in_specs=[SMEM, SMEM, VMEM, ANY],
-        out_specs=[VMEM] * 8,
+        in_specs=[ANY] * 4,
+        out_specs=[VMEM] * 9,
         scratch_shapes=[
-            pltpu.VMEM(a_view.shape, half_type),
+            pltpu.VMEM(p_view.shape, half_type),
+            pltpu.SMEM(route_row.shape, jnp.int32),
+            pltpu.SMEM(pairing.shape, jnp.int32),
             pltpu.VMEM((nx, ny, 4, blk, LANES), half_type),
             pltpu.VMEM((10 * rows, LANES), f32),
             pltpu.VMEM((4 * SUB, LANES), f32),
             pltpu.SMEM((4, aggregates), jnp.int32),
             pltpu.SMEM((4, capacity), jnp.int32),
-            pltpu.SemaphoreType.DMA((1,)),
+            pltpu.SemaphoreType.DMA((4,)),
         ],
         compiler_params=room,
         cost_estimate=cost,
         name="inner_blocks",
-    )(route_row, pairing, p_view, a_view)
+    )(*[pltpu.with_memory_space_constraint(one, pltpu.HBM) for one in (route_row, pairing, p_view, a_view)])
 
     def chain(axis):
         n = lax.axis_size(axis)
@@ -609,34 +614,27 @@
 
     part = pl.pallas_call(
         functools.partial(outer_left_kernel, grid),
-        out_shape=bf16(*parts),
-        in_specs=[VMEM, ANY],
+        out_shape=near(*parts),
+        in_specs=[VMEM] * 2,
         out_specs=VMEM,
-        scratch_shapes=[pltpu.VMEM(a_view.shape, half_type), pltpu.SemaphoreType.DMA((1,))],
         compiler_params=room,
         cost_estimate=cost,
         name="outer_left",
-    )(left, a_view)
+    )(*held(left, a_near))
     send_xy, send_z, keep_xy, keep_z = pl.pallas_call(
         functools.partial(outer_kernel, dims, grid),
-        out_shape=(bf16(4 * rows, LANES), bf16(2 * rows, LANES)) * 2,
-        in_specs=[SMEM, SMEM, VMEM, VMEM, VMEM] + [ANY] * 5,
+        out_shape=(near(4 * rows, LANES), near(2 * rows, LANES)) * 2,
+        in_specs=[SMEM, SMEM] + [VMEM] * 8,
         out_specs=[VMEM] * 4,
         scratch_shapes=[
-            pltpu.VMEM(face_x, half_type),
-            pltpu.VMEM(face_y, half_type),
-            pltpu.VMEM(face_y, half_type),
-            pltpu.VMEM(face_z, half_type),
-            pltpu.VMEM(face_z, half_type),
             pltpu.VMEM((12 * rows, LANES), f32),
             pltpu.SMEM((4, aggregates), jnp.int32),
             pltpu.SMEM((4, capacity), jnp.int32),
-            pltpu.SemaphoreType.DMA((5,)),
         ],
-        compiler_params=pltpu.CompilerParams(vmem_limit_bytes=67_043_328 - 1400 * 1024),
+        compiler_params=room,
         cost_estimate=cost,
         name="outer_blocks",
-    )(route_row, pairing, part, zup, zdn, xface, ylow, yhigh, zlow, zhigh)
+    )(route_row, pairing, *held(part, zup, zdn, xface, ylow, yhigh, zlow, zhigh))
     got_xy = lax.ppermute(send_xy, "gx", swap)
     got_z = lax.ppermute(send_z, "gx", swap)
 
@@ -644,14 +642,14 @@
     whole = 2 * rows
     half, out = pl.pallas_call(
         functools.partial(keep_kernel, (capacity, rows)),
-        out_shape=(bf16(11, rows - full, LANES), bf16(11, whole, LANES)),
+        out_shape=(near(11, rows - full, LANES), bf16(11, whole, LANES)),
         in_specs=[VMEM] * 3,
         out_specs=[VMEM, ANY],
         scratch_shapes=[pltpu.VMEM((11, full, LANES), half_type), pltpu.SemaphoreType.DMA((11,))],
         compiler_params=room,
         cost_estimate=cost,
         name="place_kept",
-    )(keep_0, keep_xy, keep_z)
+    )(*held(keep_0, keep_xy, keep_z))
     for with_xy, late in ((True, got_xy), (False, got_z)):
         out = pl.pallas_call(
             functools.partial(take_kernel, (capacity, rows), with_xy),
@@ -667,7 +665,7 @@
             compiler_params=room,
             cost_estimate=cost,
             name="place_xy" if with_xy else "place_z",
-        )(got_0, late, half, out)
+        )(*held(got_0, late, half), out)
     out = out.reshape(11, whole // (SUB * lines), lines, SUB, LANES).transpose(1, 3, 0, 2, 4)
     return out.reshape(2 * capacity, 11, entries)
 

time: 46.1 us -> 41.3 us (0.90)
  the two profiles are of different devices: /device:TPU:0 before, /device:TPU:28 now
where the time goes in v2:
time: 41.3 us; the launch traced here: 41.1 us
  waiting for transfers between devices  16.9 us (41%)
  starting transfers between devices  15.6 us (38%)
  Pallas kernels  8.47 us (21%)
    ppermute x1, waiting for transfers between devices, local(): got_xy = lax.ppermute(send_xy, 'gx', swap)  7.78 us
    ppermute x1, waiting for transfers between devices, local(): got_0 = lax.ppermute(send_0, 'gx', swap)  7.42 us
    ppermute x1, starting transfers between devices, local(): yhigh = lax.ppermute(ydn, 'gy', down)  4.55 us
    ppermute x1, starting transfers between devices, local(): zhigh = lax.ppermute(zdn, 'gz', down)  3.64 us
    pallas_call x1, Pallas kernels, local(): pl.pallas_call(functools.partial(inner_kernel, dims, grid), out_shape=(ne...  2.95 us
    pallas_call x2, Pallas kernels, local(): pl.pallas_call(functools.partial(take_kernel, (capacity, rows), with_xy),...  2.12 us
    ppermute x1, starting transfers between devices, local(): zlow = lax.ppermute(zup, 'gz', up)  1.91 us
    pallas_call x1, Pallas kernels, local(): pl.pallas_call(functools.partial(outer_kernel, dims, grid), out_shape=(ne...  1.87 us
  transfers between devices with their start and end apart: 8, of which 4 were waited for; matrix products, arithmetic and copies ran while one was open for 0% of the time, Pallas kernels for 11%

profile of v2, /device:TPU:28, one launch (start us, length us, event | category | flops | bytes accessed | tf_op | source)
XLA Modules:
  0.0 41.1 jit_solution(1174821787140062988)
XLA Ops:
  0.0 2.9 %inner_blocks.1 = (bf16[1936,128]{1,0:T(8,128)(2,1)S(1)}, bf16[1936,128]{1,0:T(8,128)(2,1)S(1)}, bf16[2,128,128]{2,1,0:T(8,128)(2,1)S(1)}, bf16[2,128,128]{2,1,0...) custom-call(s32[1,16]{1,0:T(1,128)} %bitcast.18, ...), custom_call_target="tpu_custom_call" | custom-call | flops 1000000000 | bytes 4000000 | tf_op jit(solution)/shard_map/inner_blocks/pallas_call | solution.py:569
  3.0 0.0 copy-start
  3.0 0.0 copy-start.1
  3.0 1.6 %collective-permute-start.1 = (bf16[2,128,128]{2,1,0:T(8,128)(2,1)S(1)}, bf16[2,128,128]{2,1,0:T(8,128)(2,1)S(1)}, u32[]{:S(2)}, u32[]{:S(2)}) collective-permute-start(bf16[2,128,128]{2,1,0:T(8,128)(2,1)S(1)} %get-tuple-element.25), channel_id=1, source_target_pairs={{0,16},{16,0},{1,17},{17,1},{2,18},{18,2},{3,19},{19,3},{4,20},{20... | collective-permute-start | bytes 196616 | tf_op jit(solution)/shard_map/ppermute | solution.py:606
  4.5 1.9 %collective-permute-start.4 = (bf16[8,64,128]{2,1,0:T(8,128)(2,1)S(1)}, bf16[8,64,128]{2,1,0:T(8,128)(2,1)S(1)}, u32[]{:S(2)}, u32[]{:S(2)}) collective-permute-start(bf16[8,64,128]{2,1,0:T(8,128)(2,1)S(1)} %get-tuple-element.23.zup_ref), channel_id=1, source_target_pairs={{0,1},{1,2},{2,3},{4,5},{5,6},{6,7},{8,9},{9,10},{10,11},{12,13},{... | collective-permute-start | bytes 393224 | tf_op jit(solution)/shard_map/ppermute | solution.py:612
  6.5 3.6 %collective-permute-start.5 = (bf16[8,64,128]{2,1,0:T(8,128)(2,1)S(1)}, bf16[8,64,128]{2,1,0:T(8,128)(2,1)S(1)}, u32[]{:S(2)}, u32[]{:S(2)}) collective-permute-start(bf16[8,64,128]{2,1,0:T(8,128)(2,1)S(1)} %get-tuple-element.24.zdn_ref), channel_id=1, source_target_pairs={{1,0},{2,1},{3,2},{5,4},{6,5},{7,6},{9,8},{10,9},{11,10},{13,12},{... | collective-permute-start | bytes 393224 | tf_op jit(solution)/shard_map/ppermute | solution.py:613
  10.1 1.3 %collective-permute-start.2 = (bf16[2,128,128]{2,1,0:T(8,128)(2,1)S(1)}, bf16[2,128,128]{2,1,0:T(8,128)(2,1)S(1)}, u32[]{:S(2)}, u32[]{:S(2)}) collective-permute-start(bf16[2,128,128]{2,1,0:T(8,128)(2,1)S(1)} %get-tuple-element.26), channel_id=1, source_target_pairs={{0,4},{4,8},{8,12},{1,5},{5,9},{9,13},{2,6},{6,10},{10,14},{3,7},{... | collective-permute-start | bytes 196616 | tf_op jit(solution)/shard_map/ppermute | solution.py:609
  11.4 4.5 %collective-permute-start.3 = (bf16[2,128,128]{2,1,0:T(8,128)(2,1)S(1)}, bf16[2,128,128]{2,1,0:T(8,128)(2,1)S(1)}, u32[]{:S(2)}, u32[]{:S(2)}) collective-permute-start(bf16[2,128,128]{2,1,0:T(8,128)(2,1)S(1)} %get-tuple-element.27), channel_id=1, source_target_pairs={{4,0},{8,4},{12,8},{5,1},{9,5},{13,9},{6,2},{10,6},{14,10},{7,3},{... | collective-permute-start | bytes 196616 | tf_op jit(solution)/shard_map/ppermute | solution.py:610
  16.0 0.0 collective-permute-done.1.xface_ref
  16.0 0.6 %collective-permute-start = (bf16[1936,128]{1,0:T(8,128)(2,1)S(1)}, bf16[1936,128]{1,0:T(8,128)(2,1)S(1)}, u32[]{:S(2)}, u32[]{:S(2)}) collective-permute-start(bf16[1936,128]{1,0:T(8,128)(2,1)S(1)} %get-tuple-element.20), channel_id=1, source_target_pairs={{0,16},{16,0},{1,17},{17,1},{2,18},{18,2},{3,19},{19,3},{4,20},{20... | collective-permute-start | bytes 1486856 | tf_op jit(solution)/shard_map/ppermute | solution.py:607
  16.6 0.6 %outer_left.1.part_ref = bf16[4,4,3,64,128]{4,3,2,1,0:T(8,128)(2,1)S(1)} custom-call(bf16[8,128,128]{2,1,0:T(8,128)(2,1)S(1)} %get-tuple-element.21.left_ref, bf16[4,4,7,64,128]{4,3,2,1,0:T(8,128)(2,1)S(1)} %get-tuple-element.22.a_ref), custom_call_target="tpu_custom_call" | custom-call | flops 1000000000 | bytes 4000000 | tf_op jit(solution)/shard_map/outer_left/pallas_call | solution.py:615
  17.2 0.0 collective-permute-done.2.ylow_ref
  17.2 0.7 %collective-permute-done.3.yhigh_ref = bf16[2,128,128]{2,1,0:T(8,128)(2,1)S(1)} collective-permute-done((bf16[2,128,128]{2,1,0:T(8,128)(2,1)S(1)}, bf16[2,128,128]{2,1,0:T(8,128)(2,1)S(1)}, u32[]{:S(2)}, u32[]{:S(2)}) %collective-permute-start.3) | collective-permute-done | bytes 65568 | tf_op jit(solution)/shard_map/ppermute | solution.py:610
  17.9 0.0 collective-permute-done.4.zlow_ref
  17.9 0.0 collective-permute-done.5.zhigh_ref
  17.9 0.0 copy-done
  17.9 0.0 copy-done.1
  17.9 1.9 %outer_blocks.1 = (bf16[1536,128]{1,0:T(8,128)(2,1)S(1)}, bf16[768,128]{1,0:T(8,128)(2,1)S(1)}, bf16[1536,128]{1,0:T(8,128)(2,1)S(1)}, bf16[768,128]{1,0:T(8,128)(2,1)S(1)}) custom-call(s32[1,16]{1,0:T(1,128)S(1)} %bitcast.19, s32[2,2,2]{2,1,0:T(2,128)S(1)} %copy-done, bf16[4,4,3,64,128]{4,3,2,1,0:T(8,128)(2,1)S(1)} %outer_left.1.part_ref, ...), custom_call_target="tpu_custom_call" | custom-call | flops 1000000000 | bytes 4000000 | tf_op jit(solution)/shard_map/outer_blocks/pallas_call | solution.py:624
  19.7 0.9 %collective-permute-start.7 = (bf16[1536,128]{1,0:T(8,128)(2,1)S(1)}, bf16[1536,128]{1,0:T(8,128)(2,1)S(1)}, u32[]{:S(2)}, u32[]{:S(2)}) collective-permute-start(bf16[1536,128]{1,0:T(8,128)(2,1)S(1)} %get-tuple-element.33), channel_id=1, source_target_pairs={{0,16},{16,0},{1,17},{17,1},{2,18},{18,2},{3,19},{19,3},{4,20},{20... | collective-permute-start | bytes 1179656 | tf_op jit(solution)/shard_map/ppermute | solution.py:638
  20.6 1.2 %collective-permute-start.6 = (bf16[768,128]{1,0:T(8,128)(2,1)S(1)}, bf16[768,128]{1,0:T(8,128)(2,1)S(1)}, u32[]{:S(2)}, u32[]{:S(2)}) collective-permute-start(bf16[768,128]{1,0:T(8,128)(2,1)S(1)} %get-tuple-element.28), channel_id=1, source_target_pairs={{0,16},{16,0},{1,17},{17,1},{2,18},{18,2},{3,19},{19,3},{4,20},{20... | collective-permute-start | bytes 589832 | tf_op jit(solution)/shard_map/ppermute | solution.py:639
  21.8 0.9 %place_kept.1 = (bf16[11,128,128]{2,1,0:T(8,128)(2,1)S(1)}, bf16[11,768,128]{2,1,0:T(8,128)(2,1)}) custom-call(bf16[1936,128]{1,0:T(8,128)(2,1)S(1)} %get-tuple-element.29.early_ref, bf16[1536,128]{1,0:T(8,128)(2,1)S(1)} %get-tuple-element.30.xy_ref, bf16[768,128]{1,0:T(8,128)(2,1)S(1)} %get-tuple-element.31.z_ref), custom_call_target="tpu_custom_call" | custom-call | flops 1000000000 | bytes 4000000 | tf_op jit(solution)/shard_map/place_kept/pallas_call | solution.py:643
  22.8 7.4 %collective-permute-done.early_ref = bf16[1936,128]{1,0:T(8,128)(2,1)S(1)} collective-permute-done((bf16[1936,128]{1,0:T(8,128)(2,1)S(1)}, bf16[1936,128]{1,0:T(8,128)(2,1)S(1)}, u32[]{:S(2)}, u32[]{:S(2)}) %collective-permute-start) | collective-permute-done | bytes 495648 | tf_op jit(solution)/shard_map/ppermute | solution.py:607
  30.2 7.8 %collective-permute-done.7.late_ref = bf16[1536,128]{1,0:T(8,128)(2,1)S(1)} collective-permute-done((bf16[1536,128]{1,0:T(8,128)(2,1)S(1)}, bf16[1536,128]{1,0:T(8,128)(2,1)S(1)}, u32[]{:S(2)}, u32[]{:S(2)}) %collective-permute-start.7) | collective-permute-done | bytes 393248 | tf_op jit(solution)/shard_map/ppermute | solution.py:638
  38.0 1.1 %place_xy.1._ = bf16[11,768,128]{2,1,0:T(8,128)(2,1)} custom-call(bf16[1936,128]{1,0:T(8,128)(2,1)S(1)} %collective-permute-done.early_ref, bf16[1536,128]{1,0:T(8,128)(2,1)S(1)} %collective-permute-done.7.late_ref, bf16[11,128,128]{2,1,0:T(8,128)(2,1)S(1)} %get-tuple-element.32.half_ref, ...), custom_call_target="tpu_custom_call", output_to_operand_aliasing={{}: (3, {})} | custom-call | flops 1000000000 | bytes 4000000 | tf_op jit(solution)/shard_map/place_xy/pallas_call | solution.py:654
  39.1 1.0 %collective-permute-done.6.late_ref = bf16[768,128]{1,0:T(8,128)(2,1)S(1)} collective-permute-done((bf16[768,128]{1,0:T(8,128)(2,1)S(1)}, bf16[768,128]{1,0:T(8,128)(2,1)S(1)}, u32[]{:S(2)}, u32[]{:S(2)}) %collective-permute-start.6) | collective-permute-done | bytes 196640 | tf_op jit(solution)/shard_map/ppermute | solution.py:639
  40.1 1.0 %place_z.1 = bf16[11,768,128]{2,1,0:T(8,128)(2,1)} custom-call(bf16[1936,128]{1,0:T(8,128)(2,1)S(1)} %collective-permute-done.early_ref, bf16[768,128]{1,0:T(8,128)(2,1)S(1)} %collective-permute-done.6.late_ref, bf16[11,128,128]{2,1,0:T(8,128)(2,1)S(1)} %get-tuple-element.32.half_ref, bf16[11,768,128]{2,1,0:T(8,128)(2,1)} %place_xy.1._), custom_call_target="tpu_custom_call", output_to_operand_aliasing={{}: (3, {})} | custom-call | flops 1000000000 | bytes 4000000 | tf_op jit(solution)/shard_map/place_z/pallas_call | solution.py:654
Async XLA Ops:
  3.0 14.9 %copy-start = (s32[2,2,2]{2,1,0:T(2,128)S(1)}, s32[2,2,2]{2,1,0:T(2,128)}, u32[]{:S(2)}) copy-start(s32[2,2,2]{2,1,0:T(2,128)} %pair_ref.1) | copy-start | bytes 100
  3.0 14.9 %copy-start.1 = (s32[16,1]{0,1:T(1,128)S(1)}, s32[16,1]{0,1:T(1,128)}, u32[]{:S(2)}) copy-start(s32[16,1]{0,1:T(1,128)} %param.7) | copy-start | bytes 196
  3.0 13.0 %collective-permute-start.1 = (bf16[2,128,128]{2,1,0:T(8,128)(2,1)S(1)}, bf16[2,128,128]{2,1,0:T(8,128)(2,1)S(1)}, u32[]{:S(2)}, u32[]{:S(2)}) collective-permute-start(bf16[2,128,128]{2,1,0:T(8,128)(2,1)S(1)} %get-tuple-element.25), channel_id=1, source_target_pairs={{0,16},{16,0},{1,17},{17,1},{2,18},{18,2},{3,19},{19,3},{4,20},{20... | collective-permute-start | bytes 196616 | tf_op jit(solution)/shard_map/ppermute | solution.py:606
  4.5 13.3 %collective-permute-start.4 = (bf16[8,64,128]{2,1,0:T(8,128)(2,1)S(1)}, bf16[8,64,128]{2,1,0:T(8,128)(2,1)S(1)}, u32[]{:S(2)}, u32[]{:S(2)}) collective-permute-start(bf16[8,64,128]{2,1,0:T(8,128)(2,1)S(1)} %get-tuple-element.23.zup_ref), channel_id=1, source_target_pairs={{0,1},{1,2},{2,3},{4,5},{5,6},{6,7},{8,9},{9,10},{10,11},{12,13},{... | collective-permute-start | bytes 393224 | tf_op jit(solution)/shard_map/ppermute | solution.py:612
  6.5 11.4 %collective-permute-start.5 = (bf16[8,64,128]{2,1,0:T(8,128)(2,1)S(1)}, bf16[8,64,128]{2,1,0:T(8,128)(2,1)S(1)}, u32[]{:S(2)}, u32[]{:S(2)}) collective-permute-start(bf16[8,64,128]{2,1,0:T(8,128)(2,1)S(1)} %get-tuple-element.24.zdn_ref), channel_id=1, source_target_pairs={{1,0},{2,1},{3,2},{5,4},{6,5},{7,6},{9,8},{10,9},{11,10},{13,12},{... | collective-permute-start | bytes 393224 | tf_op jit(solution)/shard_map/ppermute | solution.py:613
  10.1 7.1 %collective-permute-start.2 = (bf16[2,128,128]{2,1,0:T(8,128)(2,1)S(1)}, bf16[2,128,128]{2,1,0:T(8,128)(2,1)S(1)}, u32[]{:S(2)}, u32[]{:S(2)}) collective-permute-start(bf16[2,128,128]{2,1,0:T(8,128)(2,1)S(1)} %get-tuple-element.26), channel_id=1, source_target_pairs={{0,4},{4,8},{8,12},{1,5},{5,9},{9,13},{2,6},{6,10},{10,14},{3,7},{... | collective-permute-start | bytes 196616 | tf_op jit(solution)/shard_map/ppermute | solution.py:609
  11.4 6.4 %collective-permute-start.3 = (bf16[2,128,128]{2,1,0:T(8,128)(2,1)S(1)}, bf16[2,128,128]{2,1,0:T(8,128)(2,1)S(1)}, u32[]{:S(2)}, u32[]{:S(2)}) collective-permute-start(bf16[2,128,128]{2,1,0:T(8,128)(2,1)S(1)} %get-tuple-element.27), channel_id=1, source_target_pairs={{4,0},{8,4},{12,8},{5,1},{9,5},{13,9},{6,2},{10,6},{14,10},{7,3},{... | collective-permute-start | bytes 196616 | tf_op jit(solution)/shard_map/ppermute | solution.py:610
  16.0 14.2 %collective-permute-start = (bf16[1936,128]{1,0:T(8,128)(2,1)S(1)}, bf16[1936,128]{1,0:T(8,128)(2,1)S(1)}, u32[]{:S(2)}, u32[]{:S(2)}) collective-permute-start(bf16[1936,128]{1,0:T(8,128)(2,1)S(1)} %get-tuple-element.20), channel_id=1, source_target_pairs={{0,16},{16,0},{1,17},{17,1},{2,18},{18,2},{3,19},{19,3},{4,20},{20... | collective-permute-start | bytes 1486856 | tf_op jit(solution)/shard_map/ppermute | solution.py:607
  19.7 18.3 %collective-permute-start.7 = (bf16[1536,128]{1,0:T(8,128)(2,1)S(1)}, bf16[1536,128]{1,0:T(8,128)(2,1)S(1)}, u32[]{:S(2)}, u32[]{:S(2)}) collective-permute-start(bf16[1536,128]{1,0:T(8,128)(2,1)S(1)} %get-tuple-element.33), channel_id=1, source_target_pairs={{0,16},{16,0},{1,17},{17,1},{2,18},{18,2},{3,19},{19,3},{4,20},{20... | collective-permute-start | bytes 1179656 | tf_op jit(solution)/shard_map/ppermute | solution.py:638
  20.6 19.5 %collective-permute-start.6 = (bf16[768,128]{1,0:T(8,128)(2,1)S(1)}, bf16[768,128]{1,0:T(8,128)(2,1)S(1)}, u32[]{:S(2)}, u32[]{:S(2)}) collective-permute-start(bf16[768,128]{1,0:T(8,128)(2,1)S(1)} %get-tuple-element.28), channel_id=1, source_target_pairs={{0,16},{16,0},{1,17},{17,1},{2,18},{18,2},{3,19},{19,3},{4,20},{20... | collective-permute-start | bytes 589832 | tf_op jit(solution)/shard_map/ppermute | solution.py:639

commit v3 on v2

--- a/solution.py
+++ b/solution.py
@@ -264,7 +264,7 @@
 
 def inner_kernel(
     dims, grid, route_hbm, pair_hbm, p_hbm, a_hbm,
-    send_ref, keep_ref, xface_ref, yup_ref, ydn_ref, zup_ref, zdn_ref, left_ref, a_ref,
+    send_ref, keep_ref, xface_ref, ya_ref, yb_ref, za_ref, zb_ref, zup_ref, zdn_ref, left_ref, a_ref,
     p_ref, route_ref, pair_ref, part_ref, total_ref, codes_ref, where_ref, table_ref, sems,
 ):
     px, py, nz = grid
@@ -295,11 +295,17 @@
         left_ref[x * py + b] = transposed_dot(spread, both[x, b]).astype(jnp.bfloat16)
         zdn_ref[x * py + b] = tidy[x, b][:blk]
         zup_ref[x * py + b] = tidy[x, b][blk:]
+    y_even, z_even = lax.axis_index("gy") % 2 == 0, lax.axis_index("gz") % 2 == 0
     for a in range(px):
         one, two = tidy[2 * a, 0], tidy[2 * a + 1, 0]
-        ydn_ref[a] = jnp.concatenate([one[:, :blk], two[:, :blk]], axis=1)
+        down = jnp.concatenate([one[:, :blk], two[:, :blk]], axis=1)
         one, two = tidy[2 * a, py - 1], tidy[2 * a + 1, py - 1]
-        yup_ref[a] = jnp.concatenate([one[:, blk:], two[:, blk:]], axis=1)
+        up = jnp.concatenate([one[:, blk:], two[:, blk:]], axis=1)
+        ya_ref[a], yb_ref[a] = jnp.where(y_even, up, down), jnp.where(y_even, down, up)
+    for x, b in pairs:
+        down, up = tidy[x, b][:blk], tidy[x, b][blk:]
+        za_ref[x * py + b] = jnp.where(z_even, up, down)
+        zb_ref[x * py + b] = jnp.where(z_even, down, up)
     for b in range(py):
         for z, ref in enumerate((zdn_ref, zup_ref)):
             xface_ref[b, z * blk : (z + 1) * blk] = ref[jnp.where(me == 0, nx - 1, 0) * py + b]
@@ -392,7 +398,7 @@
 
 def outer_kernel(
     dims, grid, route_ref, pair_ref, part_ref, zup_ref, zdn_ref,
-    xface_ref, ylow_ref, yhigh_ref, zlow_ref, zhigh_ref,
+    xface_ref, ya_ref, yb_ref, za_ref, zb_ref,
     send_xy_ref, send_z_ref, keep_xy_ref, keep_z_ref,
     total_ref, where_ref, table_ref,
 ):
@@ -404,7 +410,17 @@
     nb = 6
     sent, kept = places(route_ref, where_ref, table_ref, dims, nb)
     me = lax.axis_index("gx")
-    above = (iota((blk, LANES), 0) * 0 + me) > 0
+    line = iota((blk, LANES), 0) * 0
+    above = line + me > 0
+
+    def from_sides(axis, first_ref, second_ref, at, high):
+        index = lax.axis_index(axis)
+        last = index == lax.axis_size(axis) - 1 if high else index == 0
+        by_first = index % 2 == (0 if high else 1)
+        kept = line + jnp.where(by_first | ~last, 1, 0) > 0
+        value = jnp.where(by_first, first_ref[at], second_ref[at]).astype(jnp.float32)
+        return jnp.where(kept, value, 0.0).astype(jnp.bfloat16)
+
 
     def beside_x(x, b, z, u):
         to = x - 1 if u == 0 else x + 1
@@ -418,8 +434,8 @@
         to = y - 1 if v == 0 else y + 1
         if 0 <= to < ny:
             return (zdn_ref, zup_ref)[z][x * py + to // 2], to % 2
-        ref = ylow_ref if v == 0 else yhigh_ref
-        return ref[x // 2, z * blk : (z + 1) * blk], x % 2
+        at = (x // 2, slice(z * blk, (z + 1) * blk))
+        return from_sides("gy", ya_ref, yb_ref, at, v == 1), x % 2
 
     for x in range(nx):
         made = []
@@ -427,7 +443,7 @@
             zs = pl.ds(z * q, q)
             u, a = x % 2, x // 2
             along_x = weights_of(beside_x(x, b, z, u))
-            along_z = weights_of((zlow_ref, zhigh_ref)[z][x * py + b])
+            along_z = weights_of(from_sides("gz", za_ref, zb_ref, x * py + b, z == 1))
             flat = pair_ref[a, b, z] == 0
             for v in range(2):
                 y = 2 * b + v
@@ -532,6 +548,25 @@
     return [pltpu.with_memory_space_constraint(one, pltpu.VMEM) for one in arrays]
 
 
+def swaps(ny, nz):
+    def first(i):
+        return i + 1 if i % 2 == 0 else i - 1
+
+    def second(i, n):
+        j = i - 1 if i % 2 == 0 else i + 1
+        return j if 0 <= j < n else None
+
+    made = {"y_a": [], "y_b": [], "z_a": [], "z_b": []}
+    for j in range(ny):
+        for k in range(nz):
+            to_y, to_z = second(j, ny), second(k, nz)
+            made["y_a"].append((first(j), k))
+            made["z_a"].append((j, first(k)))
+            made["y_b"].append((j, first(k)) if to_y is None else (to_y, k))
+            made["z_b"].append((first(j), k) if to_z is None else (j, to_z))
+    return {name: [(i, j * nz + k) for i, (j, k) in enumerate(to)] for name, to in made.items()}
+
+
 def local(a_blocks, prolong, pairing, route):
     devices_gx = lax.axis_size("gx")
     aggregates = route.shape[0]
@@ -539,6 +574,8 @@
     nx, ny, nz, faces, entries = a_blocks.shape
     fits = (
         devices_gx == 2
+        and lax.axis_size("gy") % 2 == 0
+        and lax.axis_size("gz") % 2 == 0
         and nz == 2
         and nx % 2 == 0
         and ny % 2 == 0
@@ -566,7 +603,7 @@
     room = pltpu.CompilerParams(vmem_limit_bytes=24 * 2**20)
     cost = pl.CostEstimate(flops=10**9, bytes_accessed=4 * 10**6, transcendentals=0)
 
-    send_0, keep_0, xface, yup, ydn, zup, zdn, left, a_near = pl.pallas_call(
+    send_0, keep_0, xface, ya, yb, za, zb, zup, zdn, left, a_near = pl.pallas_call(
         functools.partial(inner_kernel, dims, grid),
         out_shape=(
             near(5 * rows + 2 * SUB, LANES),
@@ -576,11 +613,13 @@
             near(*face_y),
             near(*face_z),
             near(*face_z),
+            near(*face_z),
+            near(*face_z),
             near(nx * py, 2 * blk, LANES),
             near(*a_view.shape),
         ),
         in_specs=[ANY] * 4,
-        out_specs=[VMEM] * 9,
+        out_specs=[VMEM] * 11,
         scratch_shapes=[
             pltpu.VMEM(p_view.shape, half_type),
             pltpu.SMEM(route_row.shape, jnp.int32),
@@ -597,20 +636,13 @@
         name="inner_blocks",
     )(*[pltpu.with_memory_space_constraint(one, pltpu.HBM) for one in (route_row, pairing, p_view, a_view)])
 
-    def chain(axis):
-        n = lax.axis_size(axis)
-        up = [(i, i + 1) for i in range(n - 1)]
-        return up, [(j, i) for i, j in up]
-
     swap = [(0, 1), (1, 0)]
     xface = lax.ppermute(xface, "gx", swap)
     got_0 = lax.ppermute(send_0, "gx", swap)
-    up, down = chain("gy")
-    ylow = lax.ppermute(yup, "gy", up)
-    yhigh = lax.ppermute(ydn, "gy", down)
-    up, down = chain("gz")
-    zlow = lax.ppermute(zup, "gz", up)
-    zhigh = lax.ppermute(zdn, "gz", down)
+    rounds = swaps(lax.axis_size("gy"), lax.axis_size("gz"))
+    halos = []
+    for name, value in (("y_a", ya), ("y_b", yb), ("z_a", za), ("z_b", zb)):
+        halos.append(lax.ppermute(value, ("gy", "gz"), rounds[name]))
 
     part = pl.pallas_call(
         functools.partial(outer_left_kernel, grid),
@@ -634,7 +666,7 @@
         compiler_params=room,
         cost_estimate=cost,
         name="outer_blocks",
-    )(route_row, pairing, *held(part, zup, zdn, xface, ylow, yhigh, zlow, zhigh))
+    )(route_row, pairing, *held(part, zup, zdn, xface, *halos))
     got_xy = lax.ppermute(send_xy, "gx", swap)
     got_z = lax.ppermute(send_z, "gx", swap)
 

time: 41.3 us -> 36 us (0.87)
  the two profiles are of different devices: /device:TPU:28 before, /device:TPU:0 now
where the time goes in v3:
time: 36 us; the launch traced here: 35.8 us
  waiting for transfers between devices  17.8 us (49%)
  starting transfers between devices  9.35 us (26%)
  Pallas kernels  8.54 us (24%)
    ppermute x1, waiting for transfers between devices, local(): got_xy = lax.ppermute(send_xy, 'gx', swap)  8.43 us
    ppermute x1, waiting for transfers between devices, local(): got_0 = lax.ppermute(send_0, 'gx', swap)  5.74 us
    ppermute x1, starting transfers between devices, local(): xface = lax.ppermute(xface, 'gx', swap)  3 us
    pallas_call x1, Pallas kernels, local(): pl.pallas_call(functools.partial(inner_kernel, dims, grid), out_shape=(ne...  2.98 us
    ppermute x4, starting transfers between devices, local(): halos.append(lax.ppermute(value, ('gy', 'gz'), rounds[name]))  2.92 us
    ppermute x1, waiting for transfers between devices, local(): got_z = lax.ppermute(send_z, 'gx', swap)  2.12 us
    pallas_call x2, Pallas kernels, local(): pl.pallas_call(functools.partial(take_kernel, (capacity, rows), with_xy),...  2.12 us
    ppermute x1, starting transfers between devices, local(): got_z = lax.ppermute(send_z, 'gx', swap)  1.91 us
  transfers between devices with their start and end apart: 8, of which 4 were waited for; matrix products, arithmetic and copies ran while one was open for 0% of the time, Pallas kernels for 13%

profile of v3, /device:TPU:0, one launch (start us, length us, event | category | flops | bytes accessed | tf_op | source)
XLA Modules:
  0.0 35.8 jit_solution(16215335736603947256)
XLA Ops:
  0.0 3.0 %inner_blocks.1 = (bf16[1936,128]{1,0:T(8,128)(2,1)S(1)}, bf16[1936,128]{1,0:T(8,128)(2,1)S(1)}, bf16[2,128,128]{2,1,0:T(8,128)(2,1)S(1)}, bf16[2,128,128]{2,1,0...) custom-call(s32[1,16]{1,0:T(1,128)} %bitcast.18, ...), custom_call_target="tpu_custom_call" | custom-call | flops 1000000000 | bytes 4000000 | tf_op jit(solution)/shard_map/inner_blocks/pallas_call | solution.py:606
  3.0 0.0 copy-start
  3.0 0.0 copy-start.1
  3.0 3.0 %collective-permute-start.1 = (bf16[2,128,128]{2,1,0:T(8,128)(2,1)S(1)}, bf16[2,128,128]{2,1,0:T(8,128)(2,1)S(1)}, u32[]{:S(2)}, u32[]{:S(2)}) collective-permute-start(bf16[2,128,128]{2,1,0:T(8,128)(2,1)S(1)} %get-tuple-element.27), channel_id=1, source_target_pairs={{0,16},{16,0},{1,17},{17,1},{2,18},{18,2},{3,19},{19,3},{4,20},{20... | collective-permute-start | bytes 196616 | tf_op jit(solution)/shard_map/ppermute | solution.py:640
  6.0 0.0 collective-permute-start.4
  6.0 1.6 %collective-permute-start.5 = (bf16[8,64,128]{2,1,0:T(8,128)(2,1)S(1)}, bf16[8,64,128]{2,1,0:T(8,128)(2,1)S(1)}, u32[]{:S(2)}, u32[]{:S(2)}) collective-permute-start(bf16[8,64,128]{2,1,0:T(8,128)(2,1)S(1)} %get-tuple-element.31), channel_id=1, source_target_pairs={{0,4},{1,2},{2,1},{3,7},{4,0},{5,6},{6,5},{7,3},{8,12},{9,10},{10,... | collective-permute-start | bytes 393224 | tf_op jit(solution)/shard_map/ppermute | solution.py:645
  7.6 0.5 %collective-permute-start.2 = (bf16[2,128,128]{2,1,0:T(8,128)(2,1)S(1)}, bf16[2,128,128]{2,1,0:T(8,128)(2,1)S(1)}, u32[]{:S(2)}, u32[]{:S(2)}) collective-permute-start(bf16[2,128,128]{2,1,0:T(8,128)(2,1)S(1)} %get-tuple-element.28), channel_id=1, source_target_pairs={{0,4},{1,5},{2,6},{3,7},{4,0},{5,1},{6,2},{7,3},{8,12},{9,13},{10,... | collective-permute-start | bytes 196616 | tf_op jit(solution)/shard_map/ppermute | solution.py:645
  8.0 0.9 %collective-permute-start.3 = (bf16[2,128,128]{2,1,0:T(8,128)(2,1)S(1)}, bf16[2,128,128]{2,1,0:T(8,128)(2,1)S(1)}, u32[]{:S(2)}, u32[]{:S(2)}) collective-permute-start(bf16[2,128,128]{2,1,0:T(8,128)(2,1)S(1)} %get-tuple-element.29), channel_id=1, source_target_pairs={{0,1},{1,0},{2,3},{3,2},{4,8},{5,9},{6,10},{7,11},{8,4},{9,5},{10,... | collective-permute-start | bytes 196616 | tf_op jit(solution)/shard_map/ppermute | solution.py:645
  8.9 0.0 collective-permute-done.1.xface_ref
  8.9 1.3 %collective-permute-start = (bf16[1936,128]{1,0:T(8,128)(2,1)S(1)}, bf16[1936,128]{1,0:T(8,128)(2,1)S(1)}, u32[]{:S(2)}, u32[]{:S(2)}) collective-permute-start(bf16[1936,128]{1,0:T(8,128)(2,1)S(1)} %get-tuple-element.22), channel_id=1, source_target_pairs={{0,16},{16,0},{1,17},{17,1},{2,18},{18,2},{3,19},{19,3},{4,20},{20... | collective-permute-start | bytes 1486856 | tf_op jit(solution)/shard_map/ppermute | solution.py:641
  10.3 0.6 %outer_left.1.part_ref = bf16[4,4,3,64,128]{4,3,2,1,0:T(8,128)(2,1)S(1)} custom-call(bf16[8,128,128]{2,1,0:T(8,128)(2,1)S(1)} %get-tuple-element.23.left_ref, bf16[4,4,7,64,128]{4,3,2,1,0:T(8,128)(2,1)S(1)} %get-tuple-element.24.a_ref), custom_call_target="tpu_custom_call" | custom-call | flops 1000000000 | bytes 4000000 | tf_op jit(solution)/shard_map/outer_left/pallas_call | solution.py:647
  10.9 1.5 %collective-permute-done.2.ya_ref = bf16[2,128,128]{2,1,0:T(8,128)(2,1)S(1)} collective-permute-done((bf16[2,128,128]{2,1,0:T(8,128)(2,1)S(1)}, bf16[2,128,128]{2,1,0:T(8,128)(2,1)S(1)}, u32[]{:S(2)}, u32[]{:S(2)}) %collective-permute-start.2) | collective-permute-done | bytes 65568 | tf_op jit(solution)/shard_map/ppermute | solution.py:645
  12.4 0.0 collective-permute-done.3.yb_ref
  12.4 0.0 collective-permute-done.4.za_ref
  12.4 0.0 collective-permute-done.5.zb_ref
  12.4 0.0 copy-done
  12.4 0.0 copy-done.1
  12.4 1.9 %outer_blocks.1 = (bf16[1536,128]{1,0:T(8,128)(2,1)S(1)}, bf16[768,128]{1,0:T(8,128)(2,1)S(1)}, bf16[1536,128]{1,0:T(8,128)(2,1)S(1)}, bf16[768,128]{1,0:T(8,128)(2,1)S(1)}) custom-call(s32[1,16]{1,0:T(1,128)S(1)} %bitcast.19, s32[2,2,2]{2,1,0:T(2,128)S(1)} %copy-done, bf16[4,4,3,64,128]{4,3,2,1,0:T(8,128)(2,1)S(1)} %outer_left.1.part_ref, ...), custom_call_target="tpu_custom_call" | custom-call | flops 1000000000 | bytes 4000000 | tf_op jit(solution)/shard_map/outer_blocks/pallas_call | solution.py:656
  14.3 0.2 collective-permute-start.7
  14.5 1.9 %collective-permute-start.6 = (bf16[768,128]{1,0:T(8,128)(2,1)S(1)}, bf16[768,128]{1,0:T(8,128)(2,1)S(1)}, u32[]{:S(2)}, u32[]{:S(2)}) collective-permute-start(bf16[768,128]{1,0:T(8,128)(2,1)S(1)} %get-tuple-element.32), channel_id=1, source_target_pairs={{0,16},{16,0},{1,17},{17,1},{2,18},{18,2},{3,19},{19,3},{4,20},{20... | collective-permute-start | bytes 589832 | tf_op jit(solution)/shard_map/ppermute | solution.py:671
  16.4 0.9 %place_kept.1 = (bf16[11,128,128]{2,1,0:T(8,128)(2,1)S(1)}, bf16[11,768,128]{2,1,0:T(8,128)(2,1)}) custom-call(bf16[1936,128]{1,0:T(8,128)(2,1)S(1)} %get-tuple-element.33.early_ref, bf16[1536,128]{1,0:T(8,128)(2,1)S(1)} %get-tuple-element.34.xy_ref, bf16[768,128]{1,0:T(8,128)(2,1)S(1)} %get-tuple-element.35.z_ref), custom_call_target="tpu_custom_call" | custom-call | flops 1000000000 | bytes 4000000 | tf_op jit(solution)/shard_map/place_kept/pallas_call | solution.py:675
  17.4 5.7 %collective-permute-done.early_ref = bf16[1936,128]{1,0:T(8,128)(2,1)S(1)} collective-permute-done((bf16[1936,128]{1,0:T(8,128)(2,1)S(1)}, bf16[1936,128]{1,0:T(8,128)(2,1)S(1)}, u32[]{:S(2)}, u32[]{:S(2)}) %collective-permute-start) | collective-permute-done | bytes 495648 | tf_op jit(solution)/shard_map/ppermute | solution.py:641
  23.1 8.4 %collective-permute-done.7.late_ref = bf16[1536,128]{1,0:T(8,128)(2,1)S(1)} collective-permute-done((bf16[1536,128]{1,0:T(8,128)(2,1)S(1)}, bf16[1536,128]{1,0:T(8,128)(2,1)S(1)}, u32[]{:S(2)}, u32[]{:S(2)}) %collective-permute-start.7) | collective-permute-done | bytes 393248 | tf_op jit(solution)/shard_map/ppermute | solution.py:670
  31.6 1.1 %place_xy.1._ = bf16[11,768,128]{2,1,0:T(8,128)(2,1)} custom-call(bf16[1936,128]{1,0:T(8,128)(2,1)S(1)} %collective-permute-done.early_ref, bf16[1536,128]{1,0:T(8,128)(2,1)S(1)} %collective-permute-done.7.late_ref, bf16[11,128,128]{2,1,0:T(8,128)(2,1)S(1)} %get-tuple-element.36.half_ref, ...), custom_call_target="tpu_custom_call", output_to_operand_aliasing={{}: (3, {})} | custom-call | flops 1000000000 | bytes 4000000 | tf_op jit(solution)/shard_map/place_xy/pallas_call | solution.py:686
  32.7 2.1 %collective-permute-done.6.late_ref = bf16[768,128]{1,0:T(8,128)(2,1)S(1)} collective-permute-done((bf16[768,128]{1,0:T(8,128)(2,1)S(1)}, bf16[768,128]{1,0:T(8,128)(2,1)S(1)}, u32[]{:S(2)}, u32[]{:S(2)}) %collective-permute-start.6) | collective-permute-done | bytes 196640 | tf_op jit(solution)/shard_map/ppermute | solution.py:671
  34.8 1.0 %place_z.1 = bf16[11,768,128]{2,1,0:T(8,128)(2,1)} custom-call(bf16[1936,128]{1,0:T(8,128)(2,1)S(1)} %collective-permute-done.early_ref, bf16[768,128]{1,0:T(8,128)(2,1)S(1)} %collective-permute-done.6.late_ref, bf16[11,128,128]{2,1,0:T(8,128)(2,1)S(1)} %get-tuple-element.36.half_ref, bf16[11,768,128]{2,1,0:T(8,128)(2,1)} %place_xy.1._), custom_call_target="tpu_custom_call", output_to_operand_aliasing={{}: (3, {})} | custom-call | flops 1000000000 | bytes 4000000 | tf_op jit(solution)/shard_map/place_z/pallas_call | solution.py:686
Async XLA Ops:
  3.0 9.4 %copy-start = (s32[2,2,2]{2,1,0:T(2,128)S(1)}, s32[2,2,2]{2,1,0:T(2,128)}, u32[]{:S(2)}) copy-start(s32[2,2,2]{2,1,0:T(2,128)} %pair_ref.1) | copy-start | bytes 100
  3.0 9.4 %copy-start.1 = (s32[16,1]{0,1:T(1,128)S(1)}, s32[16,1]{0,1:T(1,128)}, u32[]{:S(2)}) copy-start(s32[16,1]{0,1:T(1,128)} %param.7) | copy-start | bytes 196
  3.0 5.9 %collective-permute-start.1 = (bf16[2,128,128]{2,1,0:T(8,128)(2,1)S(1)}, bf16[2,128,128]{2,1,0:T(8,128)(2,1)S(1)}, u32[]{:S(2)}, u32[]{:S(2)}) collective-permute-start(bf16[2,128,128]{2,1,0:T(8,128)(2,1)S(1)} %get-tuple-element.27), channel_id=1, source_target_pairs={{0,16},{16,0},{1,17},{17,1},{2,18},{18,2},{3,19},{19,3},{4,20},{20... | collective-permute-start | bytes 196616 | tf_op jit(solution)/shard_map/ppermute | solution.py:640
  6.0 6.4 %collective-permute-start.4 = (bf16[8,64,128]{2,1,0:T(8,128)(2,1)S(1)}, bf16[8,64,128]{2,1,0:T(8,128)(2,1)S(1)}, u32[]{:S(2)}, u32[]{:S(2)}) collective-permute-start(bf16[8,64,128]{2,1,0:T(8,128)(2,1)S(1)} %get-tuple-element.30), channel_id=1, source_target_pairs={{0,1},{1,0},{2,3},{3,2},{4,5},{5,4},{6,7},{7,6},{8,9},{9,8},{10,11... | collective-permute-start | bytes 393224 | tf_op jit(solution)/shard_map/ppermute | solution.py:645
  6.0 6.4 %collective-permute-start.5 = (bf16[8,64,128]{2,1,0:T(8,128)(2,1)S(1)}, bf16[8,64,128]{2,1,0:T(8,128)(2,1)S(1)}, u32[]{:S(2)}, u32[]{:S(2)}) collective-permute-start(bf16[8,64,128]{2,1,0:T(8,128)(2,1)S(1)} %get-tuple-element.31), channel_id=1, source_target_pairs={{0,4},{1,2},{2,1},{3,7},{4,0},{5,6},{6,5},{7,3},{8,12},{9,10},{10,... | collective-permute-start | bytes 393224 | tf_op jit(solution)/shard_map/ppermute | solution.py:645
  7.6 4.8 %collective-permute-start.2 = (bf16[2,128,128]{2,1,0:T(8,128)(2,1)S(1)}, bf16[2,128,128]{2,1,0:T(8,128)(2,1)S(1)}, u32[]{:S(2)}, u32[]{:S(2)}) collective-permute-start(bf16[2,128,128]{2,1,0:T(8,128)(2,1)S(1)} %get-tuple-element.28), channel_id=1, source_target_pairs={{0,4},{1,5},{2,6},{3,7},{4,0},{5,1},{6,2},{7,3},{8,12},{9,13},{10,... | collective-permute-start | bytes 196616 | tf_op jit(solution)/shard_map/ppermute | solution.py:645
  8.0 4.3 %collective-permute-start.3 = (bf16[2,128,128]{2,1,0:T(8,128)(2,1)S(1)}, bf16[2,128,128]{2,1,0:T(8,128)(2,1)S(1)}, u32[]{:S(2)}, u32[]{:S(2)}) collective-permute-start(bf16[2,128,128]{2,1,0:T(8,128)(2,1)S(1)} %get-tuple-element.29), channel_id=1, source_target_pairs={{0,1},{1,0},{2,3},{3,2},{4,8},{5,9},{6,10},{7,11},{8,4},{9,5},{10,... | collective-permute-start | bytes 196616 | tf_op jit(solution)/shard_map/ppermute | solution.py:645
  8.9 14.2 %collective-permute-start = (bf16[1936,128]{1,0:T(8,128)(2,1)S(1)}, bf16[1936,128]{1,0:T(8,128)(2,1)S(1)}, u32[]{:S(2)}, u32[]{:S(2)}) collective-permute-start(bf16[1936,128]{1,0:T(8,128)(2,1)S(1)} %get-tuple-element.22), channel_id=1, source_target_pairs={{0,16},{16,0},{1,17},{17,1},{2,18},{18,2},{3,19},{19,3},{4,20},{20... | collective-permute-start | bytes 1486856 | tf_op jit(solution)/shard_map/ppermute | solution.py:641
  14.3 17.2 %collective-permute-start.7 = (bf16[1536,128]{1,0:T(8,128)(2,1)S(1)}, bf16[1536,128]{1,0:T(8,128)(2,1)S(1)}, u32[]{:S(2)}, u32[]{:S(2)}) collective-permute-start(bf16[1536,128]{1,0:T(8,128)(2,1)S(1)} %get-tuple-element.37), channel_id=1, source_target_pairs={{0,16},{16,0},{1,17},{17,1},{2,18},{18,2},{3,19},{19,3},{4,20},{20... | collective-permute-start | bytes 1179656 | tf_op jit(solution)/shard_map/ppermute | solution.py:670
  14.5 20.3 %collective-permute-start.6 = (bf16[768,128]{1,0:T(8,128)(2,1)S(1)}, bf16[768,128]{1,0:T(8,128)(2,1)S(1)}, u32[]{:S(2)}, u32[]{:S(2)}) collective-permute-start(bf16[768,128]{1,0:T(8,128)(2,1)S(1)} %get-tuple-element.32), channel_id=1, source_target_pairs={{0,16},{16,0},{1,17},{17,1},{2,18},{18,2},{3,19},{19,3},{4,20},{20... | collective-permute-start | bytes 589832 | tf_op jit(solution)/shard_map/ppermute | solution.py:671

commit v4 on v3

--- a/solution.py
+++ b/solution.py
@@ -262,10 +262,18 @@
         done += n
 
 
+def face_kernel(p_hbm, face_ref, sem):
+    last = p_hbm.shape[0] - 1
+    at = jnp.where(lax.axis_index("gx") == 0, last, 0)
+    copy = pltpu.make_async_copy(p_hbm.at[at], face_ref, sem.at[0])
+    copy.start()
+    copy.wait()
+
+
 def inner_kernel(
-    dims, grid, route_hbm, pair_hbm, p_hbm, a_hbm,
-    send_ref, keep_ref, xface_ref, ya_ref, yb_ref, za_ref, zb_ref, zup_ref, zdn_ref, left_ref, a_ref,
-    p_ref, route_ref, pair_ref, part_ref, total_ref, codes_ref, where_ref, table_ref, sems,
+    dims, grid, route_hbm, pair_hbm, p_ref, a_ref,
+    send_ref, total_ref, keep_codes_ref, ya_ref, yb_ref, za_ref, zb_ref, zup_ref, zdn_ref, left_ref,
+    route_ref, pair_ref, part_ref, codes_ref, where_ref, table_ref, sems,
 ):
     px, py, nz = grid
     aggregates, _, rows = dims
@@ -275,18 +283,13 @@
     nb = 5
     copies = [
         pltpu.make_async_copy(one, two, sems.at[k])
-        for k, (one, two) in enumerate((
-            (p_hbm, p_ref), (route_hbm, route_ref), (pair_hbm, pair_ref), (a_hbm, a_ref),
-        ))
+        for k, (one, two) in enumerate(((route_hbm, route_ref), (pair_hbm, pair_ref)))
     ]
     for copy in copies:
         copy.start()
     clean, spread = constants(blk)
     masks = even_lanes(q)
     first, second = even_rows(blk)
-    me = lax.axis_index("gx")
-    for copy in copies[:3]:
-        copy.wait()
 
     pairs = [(x, b) for x in range(nx) for b in range(py)]
     both = {e: pair(p_ref[e[0], 2 * e[1]], p_ref[e[0], 2 * e[1] + 1]) for e in pairs}
@@ -306,11 +309,6 @@
         down, up = tidy[x, b][:blk], tidy[x, b][blk:]
         za_ref[x * py + b] = jnp.where(z_even, up, down)
         zb_ref[x * py + b] = jnp.where(z_even, down, up)
-    for b in range(py):
-        for z, ref in enumerate((zdn_ref, zup_ref)):
-            xface_ref[b, z * blk : (z + 1) * blk] = ref[jnp.where(me == 0, nx - 1, 0) * py + b]
-    copies[3].wait()
-
     for x, y in [(x, y) for x in range(nx) for y in range(ny)]:
         here = a_ref.at[x, y]
         along_z = here[6] * first + here[5] * second
@@ -323,8 +321,10 @@
         for k in range(4):
             part_ref[x, y, k] = parts[k]
 
-    sent, kept = places(route_ref, where_ref, table_ref, dims, nb)
-    codes_ref[...] = jnp.zeros_like(codes_ref)
+    for copy in copies:
+        copy.wait()
+    sent, _ = places(route_ref, where_ref, table_ref, dims, nb)
+    codes_ref[...] = jnp.full_like(codes_ref, -1.0)
     for i in range(aggregates):
         a, b, z, t = i // (py * nz * 2), (i // (nz * 2)) % py, (i // 2) % nz, i % 2
         code = (2 * (jnp.where(pair_ref[a, b, z] == 0, 2, 1) - t) + z).astype(jnp.float32)
@@ -371,15 +371,19 @@
             put(total_ref, where_ref, i, 0, rows, sums[0, 0] + jnp.where(flat, sums[1, 0], sums[0, 1]))
             put(total_ref, where_ref, i + 1, 0, rows, sums[1, 1] + jnp.where(flat, sums[0, 1], sums[1, 0]))
 
-    for kind, (out, count) in enumerate(((send_ref, sent), (keep_ref, kept))):
-        finish(((out, nb),), total_ref, kind, dims, count)
-        out[nb * rows :] = codes_ref[kind * 2 * SUB : (kind + 1) * 2 * SUB].astype(jnp.bfloat16)
-
-
-def outer_left_kernel(grid, left_ref, a_ref, part_ref):
+    finish(((send_ref, nb),), total_ref, 0, dims, sent)
+    send_ref[nb * rows :] = codes_ref[: 2 * SUB].astype(jnp.bfloat16)
+    keep_codes_ref[...] = codes_ref[2 * SUB :].astype(jnp.bfloat16)
+
+
+def outer_left_kernel(grid, left_ref, a_ref, face_ref, part_ref, xface_ref):
     px, py, _ = grid
     nx, ny = 2 * px, 2 * py
     blk = a_ref.shape[3]
+    clean, _ = constants(blk)
+    for b in range(py):
+        both = pair(face_ref[2 * b], face_ref[2 * b + 1])
+        xface_ref[b] = dot(clean, both).astype(jnp.bfloat16)
     masks = even_lanes(blk // 2)
     first, second = even_rows(blk)
     for x, y in [(x, y) for x in range(nx) for y in range(ny)]:
@@ -464,8 +468,14 @@
         finish(((xy, 4), (along, 2)), total_ref, kind, dims, count)
 
 
-def placed_blocks(early_ref, xy_ref, z_ref, codes, rows, at, size):
-    code = jnp.concatenate([codes, codes], axis=0)
+def received(early_ref, rows):
+    def early(k, at, size):
+        return early_ref[k * rows + at : k * rows + at + size].reshape(-1, 2 * SUB, LANES)
+
+    return early
+
+
+def placed_blocks(early, xy_ref, z_ref, code, rows, at, size):
     near_low, near_high = (code < 1.5)[None], (code > 3.5)[None]
     upper = ((code == 1.0) | (code == 3.0) | (code == 5.0))[None]
 
@@ -473,31 +483,47 @@
         return ref[k * rows + at : k * rows + at + size].reshape(-1, 2 * SUB, LANES)
 
     if xy_ref is not None:
-        yield 0, tiles(early_ref, 0)
+        yield 0, early(0, at, size)
         for m in range(2):
-            cross, x_out, y_out = tiles(early_ref, 1 + m), tiles(xy_ref, 2 * m), tiles(xy_ref, 2 * m + 1)
+            cross, x_out, y_out = early(1 + m, at, size), tiles(xy_ref, 2 * m), tiles(xy_ref, 2 * m + 1)
             yield 1 + 5 * m, jnp.where(near_low, cross, x_out)
             yield 2 + 5 * m, jnp.where(near_low, x_out, jnp.where(near_high, y_out, cross))
             yield 3 + 5 * m, jnp.where(near_high, cross, y_out)
     if z_ref is not None:
         for m in range(2):
-            z_in, z_out = tiles(early_ref, 3 + m), tiles(z_ref, m)
+            z_in, z_out = early(3 + m, at, size), tiles(z_ref, m)
             yield 4 + 5 * m, jnp.where(upper, z_in, z_out)
             yield 5 + 5 * m, jnp.where(upper, z_out, z_in)
 
 
-def keep_kernel(dims, early_ref, xy_ref, z_ref, half_ref, out_hbm, full_ref, sem):
+def twice(codes):
+    return jnp.concatenate([codes, codes], axis=0)
+
+
+def keep_kernel(dims, total_ref, codes_ref, xy_ref, z_ref, half_ref, out_hbm, full_ref, sem):
     cap, rows = dims
     full = (cap - cap % SUB) * (rows // cap)
     me = lax.axis_index("gx")
-    codes = early_ref[5 * rows :]
+
+    def rounded(code):
+        filled = (code > -0.5)[None]
+
+        def early(k, at, size):
+            value = total_ref[pl.ds((5 + k) * rows + at, size), :].astype(jnp.bfloat16)
+            value = value.reshape(-1, 2 * SUB, LANES)
+            return jnp.where(filled, value, jnp.zeros_like(value))
+
+        return early
+
     copies = []
-    for k, value in placed_blocks(early_ref, xy_ref, z_ref, codes[:SUB], rows, 0, full):
+    code = twice(codes_ref[:SUB])
+    for k, value in placed_blocks(rounded(code), xy_ref, z_ref, code, rows, 0, full):
         full_ref[k] = value.reshape(full, LANES)
         to = out_hbm.at[k, pl.ds(me * (2 * full), full), :]
         copies.append(pltpu.make_async_copy(full_ref.at[k], to, sem.at[k]))
         copies[-1].start()
-    for k, value in placed_blocks(early_ref, xy_ref, z_ref, codes[SUB:], rows, full, rows - full):
+    code = twice(codes_ref[SUB:])
+    for k, value in placed_blocks(rounded(code), xy_ref, z_ref, code, rows, full, rows - full):
         half_ref[k] = value.reshape(rows - full, LANES)
     for copy in copies:
         copy.wait()
@@ -509,15 +535,16 @@
     me = lax.axis_index("gx")
     codes = early_ref[5 * rows :]
     xy_ref, z_ref = (late_ref, None) if with_xy else (None, late_ref)
+    early = received(early_ref, rows)
     copies = []
-    for k, value in placed_blocks(early_ref, xy_ref, z_ref, codes[:SUB], rows, 0, full):
+    for k, value in placed_blocks(early, xy_ref, z_ref, twice(codes[:SUB]), rows, 0, full):
         full_ref[k] = value.reshape(full, LANES)
         to = out_hbm.at[k, pl.ds((1 - me) * (2 * full), full), :]
         copies.append(pltpu.make_async_copy(full_ref.at[k], to, sem.at[0, k]))
         copies[-1].start()
     first_half = (iota((SUB, LANES), 0) < SUB // 2)[None]
     pick = first_half == (me == 0)
-    for k, value in placed_blocks(early_ref, xy_ref, z_ref, codes[SUB:], rows, full, rows - full):
+    for k, value in placed_blocks(early, xy_ref, z_ref, twice(codes[SUB:]), rows, full, rows - full):
         theirs = value.reshape(rows - full, LANES).astype(jnp.float32).reshape(-1, SUB, LANES)
         mine = half_ref[k].astype(jnp.float32).reshape(-1, SUB, LANES)
         low = jnp.where(pick, mine, theirs)
@@ -603,12 +630,25 @@
     room = pltpu.CompilerParams(vmem_limit_bytes=24 * 2**20)
     cost = pl.CostEstimate(flops=10**9, bytes_accessed=4 * 10**6, transcendentals=0)
 
-    send_0, keep_0, xface, ya, yb, za, zb, zup, zdn, left, a_near = pl.pallas_call(
+    swap = [(0, 1), (1, 0)]
+    face = pl.pallas_call(
+        face_kernel,
+        out_shape=near(ny, blk, LANES),
+        in_specs=[ANY],
+        out_specs=VMEM,
+        scratch_shapes=[pltpu.SemaphoreType.DMA((1,))],
+        compiler_params=room,
+        cost_estimate=cost,
+        name="face",
+    )(pltpu.with_memory_space_constraint(p_view, pltpu.HBM))
+    face = lax.ppermute(face, "gx", swap)
+    p_near, a_near = held(p_view, a_view)
+    send_0, total, keep_codes, ya, yb, za, zb, zup, zdn, left = pl.pallas_call(
         functools.partial(inner_kernel, dims, grid),
         out_shape=(
             near(5 * rows + 2 * SUB, LANES),
-            near(5 * rows + 2 * SUB, LANES),
-            near(*face_x),
+            pltpu.VMEM((10 * rows, LANES), f32),
+            near(2 * SUB, LANES),
             near(*face_y),
             near(*face_y),
             near(*face_z),
@@ -616,43 +656,41 @@
             near(*face_z),
             near(*face_z),
             near(nx * py, 2 * blk, LANES),
-            near(*a_view.shape),
         ),
-        in_specs=[ANY] * 4,
-        out_specs=[VMEM] * 11,
+        in_specs=[ANY, ANY, VMEM, VMEM],
+        out_specs=[VMEM] * 10,
         scratch_shapes=[
-            pltpu.VMEM(p_view.shape, half_type),
             pltpu.SMEM(route_row.shape, jnp.int32),
             pltpu.SMEM(pairing.shape, jnp.int32),
             pltpu.VMEM((nx, ny, 4, blk, LANES), half_type),
-            pltpu.VMEM((10 * rows, LANES), f32),
             pltpu.VMEM((4 * SUB, LANES), f32),
             pltpu.SMEM((4, aggregates), jnp.int32),
             pltpu.SMEM((4, capacity), jnp.int32),
-            pltpu.SemaphoreType.DMA((4,)),
+            pltpu.SemaphoreType.DMA((2,)),
         ],
         compiler_params=room,
         cost_estimate=cost,
         name="inner_blocks",
-    )(*[pltpu.with_memory_space_constraint(one, pltpu.HBM) for one in (route_row, pairing, p_view, a_view)])
-
-    swap = [(0, 1), (1, 0)]
-    xface = lax.ppermute(xface, "gx", swap)
+    )(
+        *[pltpu.with_memory_space_constraint(one, pltpu.HBM) for one in (route_row, pairing)],
+        p_near,
+        a_near,
+    )
     got_0 = lax.ppermute(send_0, "gx", swap)
     rounds = swaps(lax.axis_size("gy"), lax.axis_size("gz"))
     halos = []
     for name, value in (("y_a", ya), ("y_b", yb), ("z_a", za), ("z_b", zb)):
         halos.append(lax.ppermute(value, ("gy", "gz"), rounds[name]))
 
-    part = pl.pallas_call(
+    part, xface = pl.pallas_call(
         functools.partial(outer_left_kernel, grid),
-        out_shape=near(*parts),
-        in_specs=[VMEM] * 2,
-        out_specs=VMEM,
+        out_shape=(near(*parts), near(*face_x)),
+        in_specs=[VMEM] * 3,
+        out_specs=[VMEM] * 2,
         compiler_params=room,
         cost_estimate=cost,
         name="outer_left",
-    )(*held(left, a_near))
+    )(*held(left), a_near, *held(face))
     send_xy, send_z, keep_xy, keep_z = pl.pallas_call(
         functools.partial(outer_kernel, dims, grid),
         out_shape=(near(4 * rows, LANES), near(2 * rows, LANES)) * 2,
@@ -675,13 +713,13 @@
     half, out = pl.pallas_call(
         functools.partial(keep_kernel, (capacity, rows)),
         out_shape=(near(11, rows - full, LANES), bf16(11, whole, LANES)),
-        in_specs=[VMEM] * 3,
+        in_specs=[VMEM] * 4,
         out_specs=[VMEM, ANY],
         scratch_shapes=[pltpu.VMEM((11, full, LANES), half_type), pltpu.SemaphoreType.DMA((11,))],
         compiler_params=room,
         cost_estimate=cost,
         name="place_kept",
-    )(*held(keep_0, keep_xy, keep_z))
+    )(*held(total, keep_codes, keep_xy, keep_z))
     for with_xy, late in ((True, got_xy), (False, got_z)):
         out = pl.pallas_call(
             functools.partial(take_kernel, (capacity, rows), with_xy),

time: 36 us -> 36.5 us (1.014)
  waiting for transfers between devices: 17.8 us -> 18.6 us
  starting transfers between devices: 9.35 us -> 8.68 us
    pallas_call x1 -> x2, Pallas kernels: 0.58 us -> 1.61 us  [the longest x1 1 us: local(): pl.pallas_call(face_kernel, out_shape=near(ny, blk, LANES), in_specs=[ANY...]
    ppermute x1, starting transfers between devices: 1.34 us -> 0.5 us  [local(): got_0 = lax.ppermute(send_0, 'gx', swap)]
    ppermute x4, waiting for transfers between devices: 1.53 us -> 2.34 us  [local(): halos.append(lax.ppermute(value, ('gy', 'gz'), rounds[name]))]
    pallas_call x1, Pallas kernels: 2.98 us -> 2.27 us  [local(): pl.pallas_call(functools.partial(inner_kernel, dims, grid), out_shape=(ne...]
  transfers between devices with their start and end apart: 8 -> 8, of which waited for: 4 -> 4; matrix products, arithmetic and copies ran while one was open for 0% -> 0% of each run, Pallas kernels for 13% -> 19%
where the time goes in v4:
time: 36.5 us; the launch traced here: 36.3 us
  waiting for transfers between devices  18.6 us (51%)
  Pallas kernels  8.86 us (24%)
  starting transfers between devices  8.68 us (24%)
    ppermute x1, waiting for transfers between devices, local(): got_xy = lax.ppermute(send_xy, 'gx', swap)  8.43 us
    ppermute x1, waiting for transfers between devices, local(): got_0 = lax.ppermute(send_0, 'gx', swap)  5.74 us
    ppermute x4, starting transfers between devices, local(): halos.append(lax.ppermute(value, ('gy', 'gz'), rounds[name]))  3.06 us
    ppermute x1, starting transfers between devices, local(): face = lax.ppermute(face, 'gx', swap)  3.03 us
    ppermute x4, waiting for transfers between devices, local(): halos.append(lax.ppermute(value, ('gy', 'gz'), rounds[name]))  2.34 us
    pallas_call x1, Pallas kernels, local(): pl.pallas_call(functools.partial(inner_kernel, dims, grid), out_shape=(ne...  2.27 us
    ppermute x1, waiting for transfers between devices, local(): got_z = lax.ppermute(send_z, 'gx', swap)  2.12 us
    pallas_call x2, Pallas kernels, local(): pl.pallas_call(functools.partial(take_kernel, (capacity, rows), with_xy),...  2.12 us
  transfers between devices with their start and end apart: 8, of which 4 were waited for; matrix products, arithmetic and copies ran while one was open for 0% of the time, Pallas kernels for 19%

profile of v4, /device:TPU:0, one launch (start us, length us, event | category | flops | bytes accessed | tf_op | source)
XLA Modules:
  0.0 36.3 jit_solution(8194535258167738786)
XLA Ops:
  0.0 0.0 copy-start.1
  0.0 0.0 copy-start
  0.0 1.0 %face.1 = bf16[4,64,128]{2,1,0:T(8,128)(2,1)S(1)} custom-call(bf16[4,4,64,128]{3,2,1,0:T(8,128)(2,1)} %bitcast.20), custom_call_target="tpu_custom_call" | custom-call | flops 1000000000 | bytes 4000000 | tf_op jit(solution)/shard_map/face/pallas_call | solution.py:634
  1.0 3.0 %collective-permute-start.1 = (bf16[4,64,128]{2,1,0:T(8,128)(2,1)S(1)}, bf16[4,64,128]{2,1,0:T(8,128)(2,1)S(1)}, u32[]{:S(2)}, u32[]{:S(2)}) collective-permute-start(bf16[4,64,128]{2,1,0:T(8,128)(2,1)S(1)} %face.1), channel_id=1, source_target_pairs={{0,16},{16,0},{1,17},{17,1},{2,18},{18,2},{3,19},{19,3},{4,20},{20... | collective-permute-start | bytes 196616 | tf_op jit(solution)/shard_map/ppermute | solution.py:644
  4.0 0.0 copy-done.1
  4.0 0.0 copy-done
  4.0 2.3 %inner_blocks.1 = (bf16[1936,128]{1,0:T(8,128)(2,1)S(1)}, f32[3840,128]{1,0:T(8,128)S(1)}, bf16[16,128]{1,0:T(8,128)(2,1)S(1)}, bf16[2,128,128]{2,1,0:T(8,128)(2...) custom-call(s32[1,16]{1,0:T(1,128)} %bitcast.22, ...), custom_call_target="tpu_custom_call" | custom-call | flops 1000000000 | bytes 4000000 | tf_op jit(solution)/shard_map/inner_blocks/pallas_call | solution.py:646
  6.3 0.0 copy-start.2
  6.3 0.0 copy-start.3
  6.4 0.1 collective-permute-start.4
  6.4 1.6 %collective-permute-start.5 = (bf16[8,64,128]{2,1,0:T(8,128)(2,1)S(1)}, bf16[8,64,128]{2,1,0:T(8,128)(2,1)S(1)}, u32[]{:S(2)}, u32[]{:S(2)}) collective-permute-start(bf16[8,64,128]{2,1,0:T(8,128)(2,1)S(1)} %get-tuple-element.32), channel_id=1, source_target_pairs={{0,4},{1,2},{2,1},{3,7},{4,0},{5,6},{6,5},{7,3},{8,12},{9,10},{10,... | collective-permute-start | bytes 393224 | tf_op jit(solution)/shard_map/ppermute | solution.py:683
  8.1 0.5 %collective-permute-start.2 = (bf16[2,128,128]{2,1,0:T(8,128)(2,1)S(1)}, bf16[2,128,128]{2,1,0:T(8,128)(2,1)S(1)}, u32[]{:S(2)}, u32[]{:S(2)}) collective-permute-start(bf16[2,128,128]{2,1,0:T(8,128)(2,1)S(1)} %get-tuple-element.29), channel_id=1, source_target_pairs={{0,4},{1,5},{2,6},{3,7},{4,0},{5,1},{6,2},{7,3},{8,12},{9,13},{10,... | collective-permute-start | bytes 196616 | tf_op jit(solution)/shard_map/ppermute | solution.py:683
  8.5 0.9 %collective-permute-start.3 = (bf16[2,128,128]{2,1,0:T(8,128)(2,1)S(1)}, bf16[2,128,128]{2,1,0:T(8,128)(2,1)S(1)}, u32[]{:S(2)}, u32[]{:S(2)}) collective-permute-start(bf16[2,128,128]{2,1,0:T(8,128)(2,1)S(1)} %get-tuple-element.30), channel_id=1, source_target_pairs={{0,1},{1,0},{2,3},{3,2},{4,8},{5,9},{6,10},{7,11},{8,4},{9,5},{10,... | collective-permute-start | bytes 196616 | tf_op jit(solution)/shard_map/ppermute | solution.py:683
  9.4 0.0 collective-permute-done.1.face_ref
  9.4 0.5 %collective-permute-start = (bf16[1936,128]{1,0:T(8,128)(2,1)S(1)}, bf16[1936,128]{1,0:T(8,128)(2,1)S(1)}, u32[]{:S(2)}, u32[]{:S(2)}) collective-permute-start(bf16[1936,128]{1,0:T(8,128)(2,1)S(1)} %get-tuple-element.23), channel_id=1, source_target_pairs={{0,16},{16,0},{1,17},{17,1},{2,18},{18,2},{3,19},{19,3},{4,20},{20... | collective-permute-start | bytes 1486856 | tf_op jit(solution)/shard_map/ppermute | solution.py:679
  9.9 0.6 %outer_left.1 = (bf16[4,4,3,64,128]{4,3,2,1,0:T(8,128)(2,1)S(1)}, bf16[2,128,128]{2,1,0:T(8,128)(2,1)S(1)}) custom-call(bf16[8,128,128]{2,1,0:T(8,128)(2,1)S(1)} %get-tuple-element.24.left_ref, bf16[4,4,7,64,128]{4,3,2,1,0:T(8,128)(2,1)S(1)} %bitcast.19, bf16[4,64,128]{2,1,0:T(8,128)(2,1)S(1)} %collective-permute-done.1.face_ref), custom_call_target="tpu_custom_call" | custom-call | flops 1000000000 | bytes 4000000 | tf_op jit(solution)/shard_map/outer_left/pallas_call | solution.py:685
  10.5 2.3 %collective-permute-done.2.ya_ref = bf16[2,128,128]{2,1,0:T(8,128)(2,1)S(1)} collective-permute-done((bf16[2,128,128]{2,1,0:T(8,128)(2,1)S(1)}, bf16[2,128,128]{2,1,0:T(8,128)(2,1)S(1)}, u32[]{:S(2)}, u32[]{:S(2)}) %collective-permute-start.2) | collective-permute-done | bytes 65568 | tf_op jit(solution)/shard_map/ppermute | solution.py:683
  12.9 0.0 collective-permute-done.3.yb_ref
  12.9 0.0 collective-permute-done.4.za_ref
  12.9 0.0 collective-permute-done.5.zb_ref
  12.9 0.0 copy-done.2
  12.9 0.0 copy-done.3
  12.9 1.9 %outer_blocks.1 = (bf16[1536,128]{1,0:T(8,128)(2,1)S(1)}, bf16[768,128]{1,0:T(8,128)(2,1)S(1)}, bf16[1536,128]{1,0:T(8,128)(2,1)S(1)}, bf16[768,128]{1,0:T(8,128)(2,1)S(1)}) custom-call(s32[1,16]{1,0:T(1,128)S(1)} %bitcast.23, s32[2,2,2]{2,1,0:T(2,128)S(1)} %copy-done.2, bf16[4,4,3,64,128]{4,3,2,1,0:T(8,128)(2,1)S(1)} %get-tuple-element.25.part_ref, ...), custom_call_target="tpu_custom_call" | custom-call | flops 1000000000 | bytes 4000000 | tf_op jit(solution)/shard_map/outer_blocks/pallas_call | solution.py:694
  14.8 0.5 %collective-permute-start.7 = (bf16[1536,128]{1,0:T(8,128)(2,1)S(1)}, bf16[1536,128]{1,0:T(8,128)(2,1)S(1)}, u32[]{:S(2)}, u32[]{:S(2)}) collective-permute-start(bf16[1536,128]{1,0:T(8,128)(2,1)S(1)} %get-tuple-element.39), channel_id=1, source_target_pairs={{0,16},{16,0},{1,17},{17,1},{2,18},{18,2},{3,19},{19,3},{4,20},{20... | collective-permute-start | bytes 1179656 | tf_op jit(solution)/shard_map/ppermute | solution.py:708
  15.3 1.6 %collective-permute-start.6 = (bf16[768,128]{1,0:T(8,128)(2,1)S(1)}, bf16[768,128]{1,0:T(8,128)(2,1)S(1)}, u32[]{:S(2)}, u32[]{:S(2)}) collective-permute-start(bf16[768,128]{1,0:T(8,128)(2,1)S(1)} %get-tuple-element.33), channel_id=1, source_target_pairs={{0,16},{16,0},{1,17},{17,1},{2,18},{18,2},{3,19},{19,3},{4,20},{20... | collective-permute-start | bytes 589832 | tf_op jit(solution)/shard_map/ppermute | solution.py:709
  16.9 1.0 %place_kept.1 = (bf16[11,128,128]{2,1,0:T(8,128)(2,1)S(1)}, bf16[11,768,128]{2,1,0:T(8,128)(2,1)}) custom-call(f32[3840,128]{1,0:T(8,128)S(1)} %get-tuple-element.34.total_ref, bf16[16,128]{1,0:T(8,128)(2,1)S(1)} %get-tuple-element.35.codes_ref, bf16[1536,128]{1,0:T(8,128)(2,1)S(1)} %get-tuple-element.36.xy_ref, bf16[768,128]{1,0:T(8,128)(2,1)S(1)} %get-tuple-element.37.z_ref), custom_call_target="tpu_custom_call" | custom-call | flops 1000000000 | bytes 4000000 | tf_op jit(solution)/shard_map/place_kept/pallas_call | solution.py:713
  17.9 5.7 %collective-permute-done.early_ref = bf16[1936,128]{1,0:T(8,128)(2,1)S(1)} collective-permute-done((bf16[1936,128]{1,0:T(8,128)(2,1)S(1)}, bf16[1936,128]{1,0:T(8,128)(2,1)S(1)}, u32[]{:S(2)}, u32[]{:S(2)}) %collective-permute-start) | collective-permute-done | bytes 495648 | tf_op jit(solution)/shard_map/ppermute | solution.py:679
  23.6 8.4 %collective-permute-done.7.late_ref = bf16[1536,128]{1,0:T(8,128)(2,1)S(1)} collective-permute-done((bf16[1536,128]{1,0:T(8,128)(2,1)S(1)}, bf16[1536,128]{1,0:T(8,128)(2,1)S(1)}, u32[]{:S(2)}, u32[]{:S(2)}) %collective-permute-start.7) | collective-permute-done | bytes 393248 | tf_op jit(solution)/shard_map/ppermute | solution.py:708
  32.0 1.1 %place_xy.1._ = bf16[11,768,128]{2,1,0:T(8,128)(2,1)} custom-call(bf16[1936,128]{1,0:T(8,128)(2,1)S(1)} %collective-permute-done.early_ref, bf16[1536,128]{1,0:T(8,128)(2,1)S(1)} %collective-permute-done.7.late_ref, bf16[11,128,128]{2,1,0:T(8,128)(2,1)S(1)} %get-tuple-element.38.half_ref, ...), custom_call_target="tpu_custom_call", output_to_operand_aliasing={{}: (3, {})} | custom-call | flops 1000000000 | bytes 4000000 | tf_op jit(solution)/shard_map/place_xy/pallas_call | solution.py:724
  33.2 2.1 %collective-permute-done.6.late_ref = bf16[768,128]{1,0:T(8,128)(2,1)S(1)} collective-permute-done((bf16[768,128]{1,0:T(8,128)(2,1)S(1)}, bf16[768,128]{1,0:T(8,128)(2,1)S(1)}, u32[]{:S(2)}, u32[]{:S(2)}) %collective-permute-start.6) | collective-permute-done | bytes 196640 | tf_op jit(solution)/shard_map/ppermute | solution.py:709
  35.3 1.0 %place_z.1 = bf16[11,768,128]{2,1,0:T(8,128)(2,1)} custom-call(bf16[1936,128]{1,0:T(8,128)(2,1)S(1)} %collective-permute-done.early_ref, bf16[768,128]{1,0:T(8,128)(2,1)S(1)} %collective-permute-done.6.late_ref, bf16[11,128,128]{2,1,0:T(8,128)(2,1)S(1)} %get-tuple-element.38.half_ref, bf16[11,768,128]{2,1,0:T(8,128)(2,1)} %place_xy.1._), custom_call_target="tpu_custom_call", output_to_operand_aliasing={{}: (3, {})} | custom-call | flops 1000000000 | bytes 4000000 | tf_op jit(solution)/shard_map/place_z/pallas_call | solution.py:724
Async XLA Ops:
  0.0 4.0 %copy-start.1 = (bf16[4,4,2,4096]{3,2,1,0:T(2,128)(2,1)S(1)}, bf16[4,4,2,4096]{3,2,1,0:T(2,128)(2,1)}, u32[]{:S(2)}) copy-start(bf16[4,4,2,4096]{3,2,1,0:T(2,128)(2,1)} %param.5) | copy-start | bytes 786436
  0.0 4.0 %copy-start = (bf16[4,4,2,7,4096]{4,2,3,1,0:T(2,128)(2,1)S(1)}, bf16[4,4,2,7,4096]{4,2,3,1,0:T(2,128)(2,1)}, u32[]{:S(2)}) copy-start(bf16[4,4,2,7,4096]{4,2,3,1,0:T(2,128)(2,1)} %param.4) | copy-start | bytes 5505028
  1.0 8.4 %collective-permute-start.1 = (bf16[4,64,128]{2,1,0:T(8,128)(2,1)S(1)}, bf16[4,64,128]{2,1,0:T(8,128)(2,1)S(1)}, u32[]{:S(2)}, u32[]{:S(2)}) collective-permute-start(bf16[4,64,128]{2,1,0:T(8,128)(2,1)S(1)} %face.1), channel_id=1, source_target_pairs={{0,16},{16,0},{1,17},{17,1},{2,18},{18,2},{3,19},{19,3},{4,20},{20... | collective-permute-start | bytes 196616 | tf_op jit(solution)/shard_map/ppermute | solution.py:644
  6.3 6.6 %copy-start.2 = (s32[2,2,2]{2,1,0:T(2,128)S(1)}, s32[2,2,2]{2,1,0:T(2,128)}, u32[]{:S(2)}) copy-start(s32[2,2,2]{2,1,0:T(2,128)} %pair_ref.1) | copy-start | bytes 100
  6.3 6.6 %copy-start.3 = (s32[16,1]{0,1:T(1,128)S(1)}, s32[16,1]{0,1:T(1,128)}, u32[]{:S(2)}) copy-start(s32[16,1]{0,1:T(1,128)} %param.7) | copy-start | bytes 196
  6.4 6.5 %collective-permute-start.4 = (bf16[8,64,128]{2,1,0:T(8,128)(2,1)S(1)}, bf16[8,64,128]{2,1,0:T(8,128)(2,1)S(1)}, u32[]{:S(2)}, u32[]{:S(2)}) collective-permute-start(bf16[8,64,128]{2,1,0:T(8,128)(2,1)S(1)} %get-tuple-element.31), channel_id=1, source_target_pairs={{0,1},{1,0},{2,3},{3,2},{4,5},{5,4},{6,7},{7,6},{8,9},{9,8},{10,11... | collective-permute-start | bytes 393224 | tf_op jit(solution)/shard_map/ppermute | solution.py:683
  6.4 6.4 %collective-permute-start.5 = (bf16[8,64,128]{2,1,0:T(8,128)(2,1)S(1)}, bf16[8,64,128]{2,1,0:T(8,128)(2,1)S(1)}, u32[]{:S(2)}, u32[]{:S(2)}) collective-permute-start(bf16[8,64,128]{2,1,0:T(8,128)(2,1)S(1)} %get-tuple-element.32), channel_id=1, source_target_pairs={{0,4},{1,2},{2,1},{3,7},{4,0},{5,6},{6,5},{7,3},{8,12},{9,10},{10,... | collective-permute-start | bytes 393224 | tf_op jit(solution)/shard_map/ppermute | solution.py:683
  8.1 4.8 %collective-permute-start.2 = (bf16[2,128,128]{2,1,0:T(8,128)(2,1)S(1)}, bf16[2,128,128]{2,1,0:T(8,128)(2,1)S(1)}, u32[]{:S(2)}, u32[]{:S(2)}) collective-permute-start(bf16[2,128,128]{2,1,0:T(8,128)(2,1)S(1)} %get-tuple-element.29), channel_id=1, source_target_pairs={{0,4},{1,5},{2,6},{3,7},{4,0},{5,1},{6,2},{7,3},{8,12},{9,13},{10,... | collective-permute-start | bytes 196616 | tf_op jit(solution)/shard_map/ppermute | solution.py:683
  8.5 4.3 %collective-permute-start.3 = (bf16[2,128,128]{2,1,0:T(8,128)(2,1)S(1)}, bf16[2,128,128]{2,1,0:T(8,128)(2,1)S(1)}, u32[]{:S(2)}, u32[]{:S(2)}) collective-permute-start(bf16[2,128,128]{2,1,0:T(8,128)(2,1)S(1)} %get-tuple-element.30), channel_id=1, source_target_pairs={{0,1},{1,0},{2,3},{3,2},{4,8},{5,9},{6,10},{7,11},{8,4},{9,5},{10,... | collective-permute-start | bytes 196616 | tf_op jit(solution)/shard_map/ppermute | solution.py:683
  9.4 14.2 %collective-permute-start = (bf16[1936,128]{1,0:T(8,128)(2,1)S(1)}, bf16[1936,128]{1,0:T(8,128)(2,1)S(1)}, u32[]{:S(2)}, u32[]{:S(2)}) collective-permute-start(bf16[1936,128]{1,0:T(8,128)(2,1)S(1)} %get-tuple-element.23), channel_id=1, source_target_pairs={{0,16},{16,0},{1,17},{17,1},{2,18},{18,2},{3,19},{19,3},{4,20},{20... | collective-permute-start | bytes 1486856 | tf_op jit(solution)/shard_map/ppermute | solution.py:679
  14.8 17.2 %collective-permute-start.7 = (bf16[1536,128]{1,0:T(8,128)(2,1)S(1)}, bf16[1536,128]{1,0:T(8,128)(2,1)S(1)}, u32[]{:S(2)}, u32[]{:S(2)}) collective-permute-start(bf16[1536,128]{1,0:T(8,128)(2,1)S(1)} %get-tuple-element.39), channel_id=1, source_target_pairs={{0,16},{16,0},{1,17},{17,1},{2,18},{18,2},{3,19},{19,3},{4,20},{20... | collective-permute-start | bytes 1179656 | tf_op jit(solution)/shard_map/ppermute | solution.py:708
  15.3 19.9 %collective-permute-start.6 = (bf16[768,128]{1,0:T(8,128)(2,1)S(1)}, bf16[768,128]{1,0:T(8,128)(2,1)S(1)}, u32[]{:S(2)}, u32[]{:S(2)}) collective-permute-start(bf16[768,128]{1,0:T(8,128)(2,1)S(1)} %get-tuple-element.33), channel_id=1, source_target_pairs={{0,16},{16,0},{1,17},{17,1},{2,18},{18,2},{3,19},{19,3},{4,20},{20... | collective-permute-start | bytes 589832 | tf_op jit(solution)/shard_map/ppermute | solution.py:709

commit v5 on v4

--- a/solution.py
+++ b/solution.py
@@ -270,17 +270,21 @@
     copy.wait()
 
 
-def inner_kernel(
+def in_groups(items, size):
+    return [items[k : k + size] for k in range(0, len(items), size)]
+
+
+def first_kernel(
     dims, grid, route_hbm, pair_hbm, p_ref, a_ref,
-    send_ref, total_ref, keep_codes_ref, ya_ref, yb_ref, za_ref, zb_ref, zup_ref, zdn_ref, left_ref,
-    route_ref, pair_ref, part_ref, codes_ref, where_ref, table_ref, sems,
+    send_ref, total_ref, zup_ref, zdn_ref, left_ref,
+    route_ref, pair_ref, where_ref, table_ref, sems,
 ):
     px, py, nz = grid
-    aggregates, _, rows = dims
-    nx, ny = 2 * px, 2 * py
+    _, _, rows = dims
+    nx = 2 * px
     blk = p_ref.shape[2]
     q = blk // 2
-    nb = 5
+    nb = 2
     copies = [
         pltpu.make_async_copy(one, two, sems.at[k])
         for k, (one, two) in enumerate(((route_hbm, route_ref), (pair_hbm, pair_ref)))
@@ -290,36 +294,97 @@
     clean, spread = constants(blk)
     masks = even_lanes(q)
     first, second = even_rows(blk)
-
+    lane = iota((blk, LANES), 1)
+    low, high = as_bf16(lane < LANES // 2), as_bf16(lane >= LANES // 2)
     pairs = [(x, b) for x in range(nx) for b in range(py)]
     both = {e: pair(p_ref[e[0], 2 * e[1]], p_ref[e[0], 2 * e[1] + 1]) for e in pairs}
-    tidy = {e: dot(clean, both[e]).astype(jnp.bfloat16) for e in pairs}
+    left, tidy = {}, {}
+    for e in pairs:
+        at = e[0] * py + e[1]
+        left[e] = transposed_dot(spread, both[e]).astype(jnp.bfloat16)
+        left_ref[at] = left[e]
+        got = dot(clean, both[e]).astype(jnp.bfloat16)
+        tidy[e] = got[:blk], got[blk:]
+        zdn_ref[at], zup_ref[at] = tidy[e]
+    mixed = {}
     for x, b in pairs:
-        left_ref[x * py + b] = transposed_dot(spread, both[x, b]).astype(jnp.bfloat16)
-        zdn_ref[x * py + b] = tidy[x, b][:blk]
-        zup_ref[x * py + b] = tidy[x, b][blk:]
+        right = pair(*[
+            a_ref[x, 2 * b + v, 6] * first + a_ref[x, 2 * b + v, 5] * second for v in range(2)
+        ])
+        lefts = jnp.concatenate([left_factors(left[x, b], v, masks) for v in range(2)], axis=0)
+        got = dot(lefts, right)
+        chosen = iota((2 * blk, LANES), 1) < LANES // 2
+        mixed[x, b] = jnp.where(chosen, got[: 2 * blk], got[2 * blk :]).astype(jnp.bfloat16)
+    for copy in copies:
+        copy.wait()
+    sent, _ = places(route_ref, where_ref, table_ref, dims, nb)
+    for group in in_groups(pairs, 4):
+        made = []
+        for x, b in group:
+            for z in range(nz):
+                stack = jnp.concatenate(
+                    [mixed[x, b][z * q : (z + 1) * q], mixed[x, b][(2 + z) * q : (3 + z) * q]], axis=0
+                )
+                other = tidy[x, b][1 - z]
+                weight = jnp.concatenate([other * low, other * high], axis=0)
+                made.append((x, b, z, unpair(dot(stack, weight))))
+        for x, b, z, parts in made:
+            flat = pair_ref[x // 2, b, z] == 0
+            i = ((x // 2 * py + b) * nz + z) * 2
+            for v in range(2):
+                u = x % 2
+                t = u if u == v else jnp.where(flat, v, u)
+                m = u if u == v else jnp.where(flat, u, v)
+                put(total_ref, where_ref, i + t, m, rows, parts[v])
+    finish(((send_ref, nb),), total_ref, 0, dims, sent)
+
+
+def inner_kernel(
+    dims, grid, route_hbm, pair_hbm, left_ref, zup_ref, zdn_ref, a_ref,
+    send_ref, total_ref, keep_codes_ref, ya_ref, yb_ref, za_ref, zb_ref,
+    route_ref, pair_ref, part_ref, codes_ref, where_ref, table_ref, sems,
+):
+    px, py, nz = grid
+    aggregates, _, rows = dims
+    nx, ny = 2 * px, 2 * py
+    blk = a_ref.shape[3]
+    q = blk // 2
+    nb = 3
+    copies = [
+        pltpu.make_async_copy(one, two, sems.at[k])
+        for k, (one, two) in enumerate(((route_hbm, route_ref), (pair_hbm, pair_ref)))
+    ]
+    for copy in copies:
+        copy.start()
+    masks = even_lanes(q)
+    pairs = [(x, b) for x in range(nx) for b in range(py)]
+    down_of = lambda x, b: zdn_ref[x * py + b]
+    up_of = lambda x, b: zup_ref[x * py + b]
+
+    def both_z(x, b, half):
+        part = slice(half * blk, (half + 1) * blk)
+        return jnp.concatenate([down_of(x, b)[:, part], up_of(x, b)[:, part]], axis=0)
+
     y_even, z_even = lax.axis_index("gy") % 2 == 0, lax.axis_index("gz") % 2 == 0
     for a in range(px):
-        one, two = tidy[2 * a, 0], tidy[2 * a + 1, 0]
-        down = jnp.concatenate([one[:, :blk], two[:, :blk]], axis=1)
-        one, two = tidy[2 * a, py - 1], tidy[2 * a + 1, py - 1]
-        up = jnp.concatenate([one[:, blk:], two[:, blk:]], axis=1)
+        down = jnp.concatenate([both_z(2 * a, 0, 0), both_z(2 * a + 1, 0, 0)], axis=1)
+        up = jnp.concatenate([both_z(2 * a, py - 1, 1), both_z(2 * a + 1, py - 1, 1)], axis=1)
         ya_ref[a], yb_ref[a] = jnp.where(y_even, up, down), jnp.where(y_even, down, up)
     for x, b in pairs:
-        down, up = tidy[x, b][:blk], tidy[x, b][blk:]
+        down, up = down_of(x, b), up_of(x, b)
         za_ref[x * py + b] = jnp.where(z_even, up, down)
         zb_ref[x * py + b] = jnp.where(z_even, down, up)
     for x, y in [(x, y) for x in range(nx) for y in range(ny)]:
         here = a_ref.at[x, y]
-        along_z = here[6] * first + here[5] * second
+        low, high = halves(here[4 - y % 2])
         right = jnp.concatenate(
-            [pair(here[0], here[2 - x % 2]), pair(here[4 - y % 2], along_z)], axis=1
+            [pair(here[0], here[2 - x % 2]), jnp.concatenate([low, high], axis=0)], axis=1
         )
         left = left_factors(left_ref[x * py + y // 2], y % 2, masks)
         got = dot(left, right).astype(jnp.bfloat16)
-        parts = unpair(got[:, : 2 * blk]) + unpair(got[:, 2 * blk :])
-        for k in range(4):
-            part_ref[x, y, k] = parts[k]
+        part_ref[x, y, 0], part_ref[x, y, 1] = unpair(got[:, : 2 * blk])
+        along = got[:, 2 * blk :]
+        part_ref[x, y, 2] = jnp.concatenate([along[:blk], along[blk:]], axis=1)
 
     for copy in copies:
         copy.wait()
@@ -333,9 +398,9 @@
         codes_ref[pl.ds(where_ref[3, i], 1), :] = line
 
     for a, b in [(a, b) for a in range(px) for b in range(py)]:
-        own, with_x, with_y, with_z = {}, {}, {}, {}
+        own, with_x, with_y = {}, {}, {}
         for z, ref in enumerate((zdn_ref, zup_ref)):
-            zs, zo = pl.ds(z * q, q), pl.ds((1 - z) * q, q)
+            zs = pl.ds(z * q, q)
             for u in range(2):
                 x = 2 * a + u
                 weight = weights_of(ref[x * py + b])
@@ -346,15 +411,13 @@
                             part_ref[x, y, 0, zs],
                             part_ref[2 * a + 1 - u, y, 1, zs],
                             part_ref[x, 2 * b + 1 - v, 2, zs],
-                            part_ref[x, y, 3, zo],
                         ],
                         axis=0,
                     )
                     got = dot(stack, weight[v])
                     own[u, v, z] = got[:q]
                     with_x[1 - u, v, z] = got[q : 2 * q]
-                    with_y[u, 1 - v, z] = got[2 * q : 3 * q]
-                    with_z[u, v, 1 - z] = got[3 * q :]
+                    with_y[u, 1 - v, z] = got[2 * q :]
         for z in range(nz):
             flat = pair_ref[a, b, z] == 0
             i = ((a * py + b) * nz + z) * 2
@@ -367,7 +430,6 @@
                     sums[u, v] = own[e] + jnp.where(flat, with_x[e], with_y[e])
                     cross = jnp.where(flat, with_y[e], with_x[e])
                     put(total_ref, where_ref, i + t, 1 + m, rows, cross)
-                    put(total_ref, where_ref, i + t, 3 + m, rows, with_z[e])
             put(total_ref, where_ref, i, 0, rows, sums[0, 0] + jnp.where(flat, sums[1, 0], sums[0, 1]))
             put(total_ref, where_ref, i + 1, 0, rows, sums[1, 1] + jnp.where(flat, sums[0, 1], sums[1, 0]))
 
@@ -468,9 +530,10 @@
         finish(((xy, 4), (along, 2)), total_ref, kind, dims, count)
 
 
-def received(early_ref, rows):
+def received(z_ref, rest_ref, rows):
     def early(k, at, size):
-        return early_ref[k * rows + at : k * rows + at + size].reshape(-1, 2 * SUB, LANES)
+        ref, k = (rest_ref, k) if k < 3 else (z_ref, k - 3)
+        return ref[k * rows + at : k * rows + at + size].reshape(-1, 2 * SUB, LANES)
 
     return early
 
@@ -500,7 +563,7 @@
     return jnp.concatenate([codes, codes], axis=0)
 
 
-def keep_kernel(dims, total_ref, codes_ref, xy_ref, z_ref, half_ref, out_hbm, full_ref, sem):
+def keep_kernel(dims, z_total_ref, total_ref, codes_ref, xy_ref, z_ref, half_ref, out_hbm, full_ref, sem):
     cap, rows = dims
     full = (cap - cap % SUB) * (rows // cap)
     me = lax.axis_index("gx")
@@ -509,7 +572,8 @@
         filled = (code > -0.5)[None]
 
         def early(k, at, size):
-            value = total_ref[pl.ds((5 + k) * rows + at, size), :].astype(jnp.bfloat16)
+            ref, k = (total_ref, 3 + k) if k < 3 else (z_total_ref, 2 + k - 3)
+            value = ref[pl.ds(k * rows + at, size), :].astype(jnp.bfloat16)
             value = value.reshape(-1, 2 * SUB, LANES)
             return jnp.where(filled, value, jnp.zeros_like(value))
 
@@ -529,13 +593,13 @@
         copy.wait()
 
 
-def take_kernel(dims, with_xy, early_ref, late_ref, half_ref, _, out_hbm, full_ref, mixed_ref, sem):
+def take_kernel(dims, with_xy, early_z_ref, early_ref, late_ref, half_ref, _, out_hbm, full_ref, mixed_ref, sem):
     cap, rows = dims
     full = (cap - cap % SUB) * (rows // cap)
     me = lax.axis_index("gx")
-    codes = early_ref[5 * rows :]
+    codes = early_ref[3 * rows :]
     xy_ref, z_ref = (late_ref, None) if with_xy else (None, late_ref)
-    early = received(early_ref, rows)
+    early = received(early_z_ref, early_ref, rows)
     copies = []
     for k, value in placed_blocks(early, xy_ref, z_ref, twice(codes[:SUB]), rows, 0, full):
         full_ref[k] = value.reshape(full, LANES)
@@ -643,39 +707,52 @@
     )(pltpu.with_memory_space_constraint(p_view, pltpu.HBM))
     face = lax.ppermute(face, "gx", swap)
     p_near, a_near = held(p_view, a_view)
-    send_0, total, keep_codes, ya, yb, za, zb, zup, zdn, left = pl.pallas_call(
+    scalars = [pltpu.with_memory_space_constraint(one, pltpu.HBM) for one in (route_row, pairing)]
+    tables = [
+        pltpu.SMEM(route_row.shape, jnp.int32),
+        pltpu.SMEM(pairing.shape, jnp.int32),
+        pltpu.SMEM((4, aggregates), jnp.int32),
+        pltpu.SMEM((4, capacity), jnp.int32),
+        pltpu.SemaphoreType.DMA((2,)),
+    ]
+    send_z, total_z, zup, zdn, left = pl.pallas_call(
+        functools.partial(first_kernel, dims, grid),
+        out_shape=(
+            near(2 * rows, LANES),
+            pltpu.VMEM((4 * rows, LANES), f32),
+            near(*face_z),
+            near(*face_z),
+            near(nx * py, 2 * blk, LANES),
+        ),
+        in_specs=[ANY, ANY, VMEM, VMEM],
+        out_specs=[VMEM] * 5,
+        scratch_shapes=tables,
+        compiler_params=room,
+        cost_estimate=cost,
+        name="first_blocks",
+    )(*scalars, p_near, a_near)
+    got_z = lax.ppermute(send_z, "gx", swap)
+    near_z, left = held(zup, zdn), held(left)[0]
+    send_0, total, keep_codes, ya, yb, za, zb = pl.pallas_call(
         functools.partial(inner_kernel, dims, grid),
         out_shape=(
-            near(5 * rows + 2 * SUB, LANES),
-            pltpu.VMEM((10 * rows, LANES), f32),
+            near(3 * rows + 2 * SUB, LANES),
+            pltpu.VMEM((6 * rows, LANES), f32),
             near(2 * SUB, LANES),
             near(*face_y),
             near(*face_y),
             near(*face_z),
             near(*face_z),
-            near(*face_z),
-            near(*face_z),
-            near(nx * py, 2 * blk, LANES),
         ),
-        in_specs=[ANY, ANY, VMEM, VMEM],
-        out_specs=[VMEM] * 10,
-        scratch_shapes=[
-            pltpu.SMEM(route_row.shape, jnp.int32),
-            pltpu.SMEM(pairing.shape, jnp.int32),
-            pltpu.VMEM((nx, ny, 4, blk, LANES), half_type),
-            pltpu.VMEM((4 * SUB, LANES), f32),
-            pltpu.SMEM((4, aggregates), jnp.int32),
-            pltpu.SMEM((4, capacity), jnp.int32),
-            pltpu.SemaphoreType.DMA((2,)),
-        ],
+        in_specs=[ANY, ANY] + [VMEM] * 4,
+        out_specs=[VMEM] * 7,
+        scratch_shapes=tables[:2]
+        + [pltpu.VMEM((nx, ny, 3, blk, LANES), half_type), pltpu.VMEM((4 * SUB, LANES), f32)]
+        + tables[2:],
         compiler_params=room,
         cost_estimate=cost,
         name="inner_blocks",
-    )(
-        *[pltpu.with_memory_space_constraint(one, pltpu.HBM) for one in (route_row, pairing)],
-        p_near,
-        a_near,
-    )
+    )(*scalars, left, *near_z, a_near)
     got_0 = lax.ppermute(send_0, "gx", swap)
     rounds = swaps(lax.axis_size("gy"), lax.axis_size("gz"))
     halos = []
@@ -690,8 +767,8 @@
         compiler_params=room,
         cost_estimate=cost,
         name="outer_left",
-    )(*held(left), a_near, *held(face))
-    send_xy, send_z, keep_xy, keep_z = pl.pallas_call(
+    )(left, a_near, *held(face))
+    send_xy, send_late, keep_xy, keep_z = pl.pallas_call(
         functools.partial(outer_kernel, dims, grid),
         out_shape=(near(4 * rows, LANES), near(2 * rows, LANES)) * 2,
         in_specs=[SMEM, SMEM] + [VMEM] * 8,
@@ -704,29 +781,29 @@
         compiler_params=room,
         cost_estimate=cost,
         name="outer_blocks",
-    )(route_row, pairing, *held(part, zup, zdn, xface, *halos))
+    )(route_row, pairing, *held(part), *near_z, *held(xface, *halos))
     got_xy = lax.ppermute(send_xy, "gx", swap)
-    got_z = lax.ppermute(send_z, "gx", swap)
+    got_late = lax.ppermute(send_late, "gx", swap)
 
     full = (capacity // SUB) * SUB * lines
     whole = 2 * rows
     half, out = pl.pallas_call(
         functools.partial(keep_kernel, (capacity, rows)),
         out_shape=(near(11, rows - full, LANES), bf16(11, whole, LANES)),
-        in_specs=[VMEM] * 4,
+        in_specs=[VMEM] * 5,
         out_specs=[VMEM, ANY],
         scratch_shapes=[pltpu.VMEM((11, full, LANES), half_type), pltpu.SemaphoreType.DMA((11,))],
         compiler_params=room,
         cost_estimate=cost,
         name="place_kept",
-    )(*held(total, keep_codes, keep_xy, keep_z))
-    for with_xy, late in ((True, got_xy), (False, got_z)):
+    )(*held(total_z, total, keep_codes, keep_xy, keep_z))
+    for with_xy, late in ((True, got_xy), (False, got_late)):
         out = pl.pallas_call(
             functools.partial(take_kernel, (capacity, rows), with_xy),
             out_shape=bf16(11, whole, LANES),
-            in_specs=[VMEM] * 3 + [ANY],
+            in_specs=[VMEM] * 4 + [ANY],
             out_specs=ANY,
-            input_output_aliases={3: 0},
+            input_output_aliases={4: 0},
             scratch_shapes=[
                 pltpu.VMEM((11, full, LANES), half_type),
                 pltpu.VMEM((11, full, LANES), half_type),
@@ -735,7 +812,7 @@
             compiler_params=room,
             cost_estimate=cost,
             name="place_xy" if with_xy else "place_z",
-        )(*held(got_0, late, half), out)
+        )(*held(got_z, got_0, late, half), out)
     out = out.reshape(11, whole // (SUB * lines), lines, SUB, LANES).transpose(1, 3, 0, 2, 4)
     return out.reshape(2 * capacity, 11, entries)
 

time: 36.5 us -> 42.5 us (1.16)
  waiting for transfers between devices: 18.6 us -> 21.9 us
  starting transfers between devices: 8.68 us -> 10.2 us
  Pallas kernels: 8.86 us -> 10.1 us
    ppermute x1, waiting for transfers between devices: 2.12 us -> 17.6 us  [local(): got_z = lax.ppermute(send_z, 'gx', swap)]
    ppermute x1, waiting for transfers between devices: 8.43 us -> 0.01 us  [local(): got_xy = lax.ppermute(send_xy, 'gx', swap)]
    ppermute x1, waiting for transfers between devices: 5.74 us -> 0.01 us  [local(): got_0 = lax.ppermute(send_0, 'gx', swap)]
    pallas_call x0 -> x1, Pallas kernels: none -> 1.7 us  [local(): pl.pallas_call(functools.partial(first_kernel, dims, grid), out_shape=(ne...]
    ppermute x0 -> x1, starting transfers between devices: none -> 1.55 us  [local(): got_late = lax.ppermute(send_late, 'gx', swap)]
    ppermute x0 -> x1, waiting for transfers between devices: none -> 1.46 us  [local(): got_late = lax.ppermute(send_late, 'gx', swap)]
    ppermute x1, starting transfers between devices: 1.56 us -> 0.48 us  [local(): got_z = lax.ppermute(send_z, 'gx', swap)]
    ppermute x1, starting transfers between devices: 0.5 us -> 1.55 us  [local(): got_0 = lax.ppermute(send_0, 'gx', swap)]
  transfers between devices with their start and end apart: 8 -> 9, of which waited for: 4 -> 3; matrix products, arithmetic and copies ran while one was open for 0% -> 0% of each run, Pallas kernels for 19% -> 15%
where the time goes in v5:
time: 42.5 us; the launch traced here: 42.3 us
  waiting for transfers between devices  21.9 us (52%)
  starting transfers between devices  10.2 us (24%)
  Pallas kernels  10.1 us (24%)
    ppermute x1, waiting for transfers between devices, local(): got_z = lax.ppermute(send_z, 'gx', swap)  17.6 us
    ppermute x4, starting transfers between devices, local(): halos.append(lax.ppermute(value, ('gy', 'gz'), rounds[name]))  3.06 us
    ppermute x1, starting transfers between devices, local(): face = lax.ppermute(face, 'gx', swap)  3.03 us
    ppermute x4, waiting for transfers between devices, local(): halos.append(lax.ppermute(value, ('gy', 'gz'), rounds[name]))  2.83 us
    pallas_call x2, Pallas kernels, local(): pl.pallas_call(functools.partial(take_kernel, (capacity, rows), with_xy),...  2.12 us
    pallas_call x1, Pallas kernels, local(): pl.pallas_call(functools.partial(outer_kernel, dims, grid), out_shape=(ne...  1.9 us
    pallas_call x1, Pallas kernels, local(): pl.pallas_call(functools.partial(inner_kernel, dims, grid), out_shape=(ne...  1.81 us
    pallas_call x1, Pallas kernels, local(): pl.pallas_call(functools.partial(first_kernel, dims, grid), out_shape=(ne...  1.7 us
  transfers between devices with their start and end apart: 9, of which 3 were waited for; matrix products, arithmetic and copies ran while one was open for 0% of the time, Pallas kernels for 15%

profile of v5, /device:TPU:0, one launch (start us, length us, event | category | flops | bytes accessed | tf_op | source)
XLA Modules:
  0.0 42.3 jit_solution(12843689637019330090)
XLA Ops:
  0.0 1.0 %face.1 = bf16[4,64,128]{2,1,0:T(8,128)(2,1)S(1)} custom-call(bf16[4,4,64,128]{3,2,1,0:T(8,128)(2,1)} %bitcast.21), custom_call_target="tpu_custom_call" | custom-call | flops 1000000000 | bytes 4000000 | tf_op jit(solution)/shard_map/face/pallas_call | solution.py:698
  1.0 3.0 %collective-permute-start.2 = (bf16[4,64,128]{2,1,0:T(8,128)(2,1)S(1)}, bf16[4,64,128]{2,1,0:T(8,128)(2,1)S(1)}, u32[]{:S(2)}, u32[]{:S(2)}) collective-permute-start(bf16[4,64,128]{2,1,0:T(8,128)(2,1)S(1)} %face.1), channel_id=1, source_target_pairs={{0,16},{16,0},{1,17},{17,1},{2,18},{18,2},{3,19},{19,3},{4,20},{20... | collective-permute-start | bytes 196616 | tf_op jit(solution)/shard_map/ppermute | solution.py:708
  4.0 0.0 copy-done.1
  4.0 0.0 copy-done
  4.0 1.7 %first_blocks.1 = (bf16[768,128]{1,0:T(8,128)(2,1)S(1)}, f32[1536,128]{1,0:T(8,128)S(1)}, bf16[8,64,128]{2,1,0:T(8,128)(2,1)S(1)}, bf16[8,64,128]{2,1,0:T(8,128)(2,1)S(1)}, bf16[8,128,128]{2,1,0:T(8,128)(2,1)S(1)}) custom-call(s32[1,16]{1,0:T(1,128)} %bitcast.23, s32[2,2,2]{2,1,0:T(2,128)} %pair_ref.1, bf16[4,4,64,128]{3,2,1,0:T(8,128)(2,1)S(1)} %bitcast.22, ...), custom_call_target="tpu_custom_call" | custom-call | flops 1000000000 | bytes 4000000 | tf_op jit(solution)/shard_map/first_blocks/pallas_call | solution.py:718
  5.8 1.8 %inner_blocks.1 = (bf16[1168,128]{1,0:T(8,128)(2,1)S(1)}, f32[2304,128]{1,0:T(8,128)S(1)}, bf16[16,128]{1,0:T(8,128)(2,1)S(1)}, bf16[2,128,128]{2,1,0:T(8,128)(2...) custom-call(s32[1,16]{1,0:T(1,128)} %bitcast.24, ...), custom_call_target="tpu_custom_call" | custom-call | flops 1000000000 | bytes 4000000 | tf_op jit(solution)/shard_map/inner_blocks/pallas_call | solution.py:736
  7.6 0.0 copy-start.2
  7.6 0.0 copy-start.3
  7.6 0.1 collective-permute-start.5
  7.7 1.6 %collective-permute-start.6 = (bf16[8,64,128]{2,1,0:T(8,128)(2,1)S(1)}, bf16[8,64,128]{2,1,0:T(8,128)(2,1)S(1)}, u32[]{:S(2)}, u32[]{:S(2)}) collective-permute-start(bf16[8,64,128]{2,1,0:T(8,128)(2,1)S(1)} %get-tuple-element.35), channel_id=1, source_target_pairs={{0,4},{1,2},{2,1},{3,7},{4,0},{5,6},{6,5},{7,3},{8,12},{9,10},{10,... | collective-permute-start | bytes 393224 | tf_op jit(solution)/shard_map/ppermute | solution.py:760
  9.3 0.4 %collective-permute-start.3 = (bf16[2,128,128]{2,1,0:T(8,128)(2,1)S(1)}, bf16[2,128,128]{2,1,0:T(8,128)(2,1)S(1)}, u32[]{:S(2)}, u32[]{:S(2)}) collective-permute-start(bf16[2,128,128]{2,1,0:T(8,128)(2,1)S(1)} %get-tuple-element.32), channel_id=1, source_target_pairs={{0,4},{1,5},{2,6},{3,7},{4,0},{5,1},{6,2},{7,3},{8,12},{9,13},{10,... | collective-permute-start | bytes 196616 | tf_op jit(solution)/shard_map/ppermute | solution.py:760
  9.8 0.9 %collective-permute-start.4 = (bf16[2,128,128]{2,1,0:T(8,128)(2,1)S(1)}, bf16[2,128,128]{2,1,0:T(8,128)(2,1)S(1)}, u32[]{:S(2)}, u32[]{:S(2)}) collective-permute-start(bf16[2,128,128]{2,1,0:T(8,128)(2,1)S(1)} %get-tuple-element.33), channel_id=1, source_target_pairs={{0,1},{1,0},{2,3},{3,2},{4,8},{5,9},{6,10},{7,11},{8,4},{9,5},{10,... | collective-permute-start | bytes 196616 | tf_op jit(solution)/shard_map/ppermute | solution.py:760
  10.7 0.0 collective-permute-done.2.face_ref
  10.7 0.6 %outer_left.1 = (bf16[4,4,3,64,128]{4,3,2,1,0:T(8,128)(2,1)S(1)}, bf16[2,128,128]{2,1,0:T(8,128)(2,1)S(1)}) custom-call(bf16[8,128,128]{2,1,0:T(8,128)(2,1)S(1)} %get-tuple-element.26.left_ref, bf16[4,4,7,64,128]{4,3,2,1,0:T(8,128)(2,1)S(1)} %bitcast.20, bf16[4,64,128]{2,1,0:T(8,128)(2,1)S(1)} %collective-permute-done.2.face_ref), custom_call_target="tpu_custom_call" | custom-call | flops 1000000000 | bytes 4000000 | tf_op jit(solution)/shard_map/outer_left/pallas_call | solution.py:762
  11.3 2.8 %collective-permute-done.3.ya_ref = bf16[2,128,128]{2,1,0:T(8,128)(2,1)S(1)} collective-permute-done((bf16[2,128,128]{2,1,0:T(8,128)(2,1)S(1)}, bf16[2,128,128]{2,1,0:T(8,128)(2,1)S(1)}, u32[]{:S(2)}, u32[]{:S(2)}) %collective-permute-start.3) | collective-permute-done | bytes 65568 | tf_op jit(solution)/shard_map/ppermute | solution.py:760
  14.1 0.0 collective-permute-done.4.yb_ref
  14.1 0.0 collective-permute-done.5.za_ref
  14.1 0.0 collective-permute-done.6.zb_ref
  14.1 0.0 copy-done.2
  14.1 0.0 copy-done.3
  14.2 1.9 %outer_blocks.1 = (bf16[1536,128]{1,0:T(8,128)(2,1)S(1)}, bf16[768,128]{1,0:T(8,128)(2,1)S(1)}, bf16[1536,128]{1,0:T(8,128)(2,1)S(1)}, bf16[768,128]{1,0:T(8,128)(2,1)S(1)}) custom-call(s32[1,16]{1,0:T(1,128)S(1)} %bitcast.25, s32[2,2,2]{2,1,0:T(2,128)S(1)} %copy-done.2, bf16[4,4,3,64,128]{4,3,2,1,0:T(8,128)(2,1)S(1)} %get-tuple-element.30.part_ref, ...), custom_call_target="tpu_custom_call" | custom-call | flops 1000000000 | bytes 4000000 | tf_op jit(solution)/shard_map/outer_blocks/pallas_call | solution.py:771
  16.1 0.5 %collective-permute-start.8 = (bf16[1536,128]{1,0:T(8,128)(2,1)S(1)}, bf16[1536,128]{1,0:T(8,128)(2,1)S(1)}, u32[]{:S(2)}, u32[]{:S(2)}) collective-permute-start(bf16[1536,128]{1,0:T(8,128)(2,1)S(1)} %get-tuple-element.43), channel_id=1, source_target_pairs={{0,16},{16,0},{1,17},{17,1},{2,18},{18,2},{3,19},{19,3},{4,20},{20... | collective-permute-start | bytes 1179656 | tf_op jit(solution)/shard_map/ppermute | solution.py:785
  16.6 1.5 %collective-permute-start.1 = (bf16[1168,128]{1,0:T(8,128)(2,1)S(1)}, bf16[1168,128]{1,0:T(8,128)(2,1)S(1)}, u32[]{:S(2)}, u32[]{:S(2)}) collective-permute-start(bf16[1168,128]{1,0:T(8,128)(2,1)S(1)} %get-tuple-element.29), channel_id=1, source_target_pairs={{0,16},{16,0},{1,17},{17,1},{2,18},{18,2},{3,19},{19,3},{4,20},{20... | collective-permute-start | bytes 897032 | tf_op jit(solution)/shard_map/ppermute | solution.py:756
  18.2 0.5 %collective-permute-start = (bf16[768,128]{1,0:T(8,128)(2,1)S(1)}, bf16[768,128]{1,0:T(8,128)(2,1)S(1)}, u32[]{:S(2)}, u32[]{:S(2)}) collective-permute-start(bf16[768,128]{1,0:T(8,128)(2,1)S(1)} %get-tuple-element.25), channel_id=1, source_target_pairs={{0,16},{16,0},{1,17},{17,1},{2,18},{18,2},{3,19},{19,3},{4,20},{20... | collective-permute-start | bytes 589832 | tf_op jit(solution)/shard_map/ppermute | solution.py:734
  18.6 1.5 %collective-permute-start.7 = (bf16[768,128]{1,0:T(8,128)(2,1)S(1)}, bf16[768,128]{1,0:T(8,128)(2,1)S(1)}, u32[]{:S(2)}, u32[]{:S(2)}) collective-permute-start(bf16[768,128]{1,0:T(8,128)(2,1)S(1)} %get-tuple-element.36), channel_id=1, source_target_pairs={{0,16},{16,0},{1,17},{17,1},{2,18},{18,2},{3,19},{19,3},{4,20},{20... | collective-permute-start | bytes 589832 | tf_op jit(solution)/shard_map/ppermute | solution.py:786
  20.2 1.0 %place_kept.1 = (bf16[11,128,128]{2,1,0:T(8,128)(2,1)S(1)}, bf16[11,768,128]{2,1,0:T(8,128)(2,1)}) custom-call(f32[1536,128]{1,0:T(8,128)S(1)} %get-tuple-element.37.z_total_ref, f32[2304,128]{1,0:T(8,128)S(1)} %get-tuple-element.38.total_ref, bf16[16,128]{1,0:T(8,128)(2,1)S(1)} %get-tuple-element.39.codes_ref, ...), custom_call_target="tpu_custom_call" | custom-call | flops 1000000000 | bytes 4000000 | tf_op jit(solution)/shard_map/place_kept/pallas_call | solution.py:790
  21.1 17.6 %collective-permute-done.early_z_ref = bf16[768,128]{1,0:T(8,128)(2,1)S(1)} collective-permute-done((bf16[768,128]{1,0:T(8,128)(2,1)S(1)}, bf16[768,128]{1,0:T(8,128)(2,1)S(1)}, u32[]{:S(2)}, u32[]{:S(2)}) %collective-permute-start) | collective-permute-done | bytes 196640 | tf_op jit(solution)/shard_map/ppermute | solution.py:734
  38.7 0.0 collective-permute-done.1.early_ref
  38.7 0.0 collective-permute-done.8.late_ref
  38.7 1.1 %place_xy.1._ = bf16[11,768,128]{2,1,0:T(8,128)(2,1)} custom-call(bf16[768,128]{1,0:T(8,128)(2,1)S(1)} %collective-permute-done.early_z_ref, bf16[1168,128]{1,0:T(8,128)(2,1)S(1)} %collective-permute-done.1.early_ref, bf16[1536,128]{1,0:T(8,128)(2,1)S(1)} %collective-permute-done.8.late_ref, ...), custom_call_target="tpu_custom_call", output_to_operand_aliasing={{}: (4, {})} | custom-call | flops 1000000000 | bytes 4000000 | tf_op jit(solution)/shard_map/place_xy/pallas_call | solution.py:801
  39.9 1.5 %collective-permute-done.7.late_ref = bf16[768,128]{1,0:T(8,128)(2,1)S(1)} collective-permute-done((bf16[768,128]{1,0:T(8,128)(2,1)S(1)}, bf16[768,128]{1,0:T(8,128)(2,1)S(1)}, u32[]{:S(2)}, u32[]{:S(2)}) %collective-permute-start.7) | collective-permute-done | bytes 196640 | tf_op jit(solution)/shard_map/ppermute | solution.py:786
  41.3 1.0 %place_z.1 = bf16[11,768,128]{2,1,0:T(8,128)(2,1)} custom-call(bf16[768,128]{1,0:T(8,128)(2,1)S(1)} %collective-permute-done.early_z_ref, bf16[1168,128]{1,0:T(8,128)(2,1)S(1)} %collective-permute-done.1.early_ref, bf16[768,128]{1,0:T(8,128)(2,1)S(1)} %collective-permute-done.7.late_ref, ...), custom_call_target="tpu_custom_call", output_to_operand_aliasing={{}: (4, {})} | custom-call | flops 1000000000 | bytes 4000000 | tf_op jit(solution)/shard_map/place_z/pallas_call | solution.py:801
  (2 shorter events, 0.0 us)
Async XLA Ops:
  0.0 4.0 %copy-start.1 = (bf16[4,4,2,4096]{3,2,1,0:T(2,128)(2,1)S(1)}, bf16[4,4,2,4096]{3,2,1,0:T(2,128)(2,1)}, u32[]{:S(2)}) copy-start(bf16[4,4,2,4096]{3,2,1,0:T(2,128)(2,1)} %param.5) | copy-start | bytes 786436
  0.0 4.0 %copy-start = (bf16[4,4,2,7,4096]{4,2,3,1,0:T(2,128)(2,1)S(1)}, bf16[4,4,2,7,4096]{4,2,3,1,0:T(2,128)(2,1)}, u32[]{:S(2)}) copy-start(bf16[4,4,2,7,4096]{4,2,3,1,0:T(2,128)(2,1)} %param.4) | copy-start | bytes 5505028
  1.0 9.7 %collective-permute-start.2 = (bf16[4,64,128]{2,1,0:T(8,128)(2,1)S(1)}, bf16[4,64,128]{2,1,0:T(8,128)(2,1)S(1)}, u32[]{:S(2)}, u32[]{:S(2)}) collective-permute-start(bf16[4,64,128]{2,1,0:T(8,128)(2,1)S(1)} %face.1), channel_id=1, source_target_pairs={{0,16},{16,0},{1,17},{17,1},{2,18},{18,2},{3,19},{19,3},{4,20},{20... | collective-permute-start | bytes 196616 | tf_op jit(solution)/shard_map/ppermute | solution.py:708
  7.6 6.6 %copy-start.2 = (s32[2,2,2]{2,1,0:T(2,128)S(1)}, s32[2,2,2]{2,1,0:T(2,128)}, u32[]{:S(2)}) copy-start(s32[2,2,2]{2,1,0:T(2,128)} %pair_ref.1) | copy-start | bytes 100
  7.6 6.6 %copy-start.3 = (s32[16,1]{0,1:T(1,128)S(1)}, s32[16,1]{0,1:T(1,128)}, u32[]{:S(2)}) copy-start(s32[16,1]{0,1:T(1,128)} %param.7) | copy-start | bytes 196
  7.6 6.5 %collective-permute-start.5 = (bf16[8,64,128]{2,1,0:T(8,128)(2,1)S(1)}, bf16[8,64,128]{2,1,0:T(8,128)(2,1)S(1)}, u32[]{:S(2)}, u32[]{:S(2)}) collective-permute-start(bf16[8,64,128]{2,1,0:T(8,128)(2,1)S(1)} %get-tuple-element.34), channel_id=1, source_target_pairs={{0,1},{1,0},{2,3},{3,2},{4,5},{5,4},{6,7},{7,6},{8,9},{9,8},{10,11... | collective-permute-start | bytes 393224 | tf_op jit(solution)/shard_map/ppermute | solution.py:760
  7.7 6.4 %collective-permute-start.6 = (bf16[8,64,128]{2,1,0:T(8,128)(2,1)S(1)}, bf16[8,64,128]{2,1,0:T(8,128)(2,1)S(1)}, u32[]{:S(2)}, u32[]{:S(2)}) collective-permute-start(bf16[8,64,128]{2,1,0:T(8,128)(2,1)S(1)} %get-tuple-element.35), channel_id=1, source_target_pairs={{0,4},{1,2},{2,1},{3,7},{4,0},{5,6},{6,5},{7,3},{8,12},{9,10},{10,... | collective-permute-start | bytes 393224 | tf_op jit(solution)/shard_map/ppermute | solution.py:760
  9.3 4.8 %collective-permute-start.3 = (bf16[2,128,128]{2,1,0:T(8,128)(2,1)S(1)}, bf16[2,128,128]{2,1,0:T(8,128)(2,1)S(1)}, u32[]{:S(2)}, u32[]{:S(2)}) collective-permute-start(bf16[2,128,128]{2,1,0:T(8,128)(2,1)S(1)} %get-tuple-element.32), channel_id=1, source_target_pairs={{0,4},{1,5},{2,6},{3,7},{4,0},{5,1},{6,2},{7,3},{8,12},{9,13},{10,... | collective-permute-start | bytes 196616 | tf_op jit(solution)/shard_map/ppermute | solution.py:760
  9.8 4.3 %collective-permute-start.4 = (bf16[2,128,128]{2,1,0:T(8,128)(2,1)S(1)}, bf16[2,128,128]{2,1,0:T(8,128)(2,1)S(1)}, u32[]{:S(2)}, u32[]{:S(2)}) collective-permute-start(bf16[2,128,128]{2,1,0:T(8,128)(2,1)S(1)} %get-tuple-element.33), channel_id=1, source_target_pairs={{0,1},{1,0},{2,3},{3,2},{4,8},{5,9},{6,10},{7,11},{8,4},{9,5},{10,... | collective-permute-start | bytes 196616 | tf_op jit(solution)/shard_map/ppermute | solution.py:760
  16.1 22.7 %collective-permute-start.8 = (bf16[1536,128]{1,0:T(8,128)(2,1)S(1)}, bf16[1536,128]{1,0:T(8,128)(2,1)S(1)}, u32[]{:S(2)}, u32[]{:S(2)}) collective-permute-start(bf16[1536,128]{1,0:T(8,128)(2,1)S(1)} %get-tuple-element.43), channel_id=1, source_target_pairs={{0,16},{16,0},{1,17},{17,1},{2,18},{18,2},{3,19},{19,3},{4,20},{20... | collective-permute-start | bytes 1179656 | tf_op jit(solution)/shard_map/ppermute | solution.py:785
  16.6 22.1 %collective-permute-start.1 = (bf16[1168,128]{1,0:T(8,128)(2,1)S(1)}, bf16[1168,128]{1,0:T(8,128)(2,1)S(1)}, u32[]{:S(2)}, u32[]{:S(2)}) collective-permute-start(bf16[1168,128]{1,0:T(8,128)(2,1)S(1)} %get-tuple-element.29), channel_id=1, source_target_pairs={{0,16},{16,0},{1,17},{17,1},{2,18},{18,2},{3,19},{19,3},{4,20},{20... | collective-permute-start | bytes 897032 | tf_op jit(solution)/shard_map/ppermute | solution.py:756
  18.2 20.6 %collective-permute-start = (bf16[768,128]{1,0:T(8,128)(2,1)S(1)}, bf16[768,128]{1,0:T(8,128)(2,1)S(1)}, u32[]{:S(2)}, u32[]{:S(2)}) collective-permute-start(bf16[768,128]{1,0:T(8,128)(2,1)S(1)} %get-tuple-element.25), channel_id=1, source_target_pairs={{0,16},{16,0},{1,17},{17,1},{2,18},{18,2},{3,19},{19,3},{4,20},{20... | collective-permute-start | bytes 589832 | tf_op jit(solution)/shard_map/ppermute | solution.py:734
  18.6 22.7 %collective-permute-start.7 = (bf16[768,128]{1,0:T(8,128)(2,1)S(1)}, bf16[768,128]{1,0:T(8,128)(2,1)S(1)}, u32[]{:S(2)}, u32[]{:S(2)}) collective-permute-start(bf16[768,128]{1,0:T(8,128)(2,1)S(1)} %get-tuple-element.36), channel_id=1, source_target_pairs={{0,16},{16,0},{1,17},{17,1},{2,18},{18,2},{3,19},{19,3},{4,20},{20... | collective-permute-start | bytes 589832 | tf_op jit(solution)/shard_map/ppermute | solution.py:786

commit v6 on v4

--- a/solution.py
+++ b/solution.py
@@ -272,7 +272,7 @@
 
 def inner_kernel(
     dims, grid, route_hbm, pair_hbm, p_ref, a_ref,
-    send_ref, total_ref, keep_codes_ref, ya_ref, yb_ref, za_ref, zb_ref, zup_ref, zdn_ref, left_ref,
+    send_ref, total_ref, keep_codes_ref, zup_ref, zdn_ref, left_ref,
     route_ref, pair_ref, part_ref, codes_ref, where_ref, table_ref, sems,
 ):
     px, py, nz = grid
@@ -287,6 +287,16 @@
     ]
     for copy in copies:
         copy.start()
+    for copy in copies:
+        copy.wait()
+    sent, _ = places(route_ref, where_ref, table_ref, dims, nb)
+    codes_ref[...] = jnp.full_like(codes_ref, -1.0)
+    for i in range(aggregates):
+        a, b, z, t = i // (py * nz * 2), (i // (nz * 2)) % py, (i // 2) % nz, i % 2
+        code = (2 * (jnp.where(pair_ref[a, b, z] == 0, 2, 1) - t) + z).astype(jnp.float32)
+        line = jnp.full((1, LANES), code, jnp.float32)
+        codes_ref[pl.ds(where_ref[2, i], 1), :] = line
+        codes_ref[pl.ds(where_ref[3, i], 1), :] = line
     clean, spread = constants(blk)
     masks = even_lanes(q)
     first, second = even_rows(blk)
@@ -298,17 +308,7 @@
         left_ref[x * py + b] = transposed_dot(spread, both[x, b]).astype(jnp.bfloat16)
         zdn_ref[x * py + b] = tidy[x, b][:blk]
         zup_ref[x * py + b] = tidy[x, b][blk:]
-    y_even, z_even = lax.axis_index("gy") % 2 == 0, lax.axis_index("gz") % 2 == 0
-    for a in range(px):
-        one, two = tidy[2 * a, 0], tidy[2 * a + 1, 0]
-        down = jnp.concatenate([one[:, :blk], two[:, :blk]], axis=1)
-        one, two = tidy[2 * a, py - 1], tidy[2 * a + 1, py - 1]
-        up = jnp.concatenate([one[:, blk:], two[:, blk:]], axis=1)
-        ya_ref[a], yb_ref[a] = jnp.where(y_even, up, down), jnp.where(y_even, down, up)
-    for x, b in pairs:
-        down, up = tidy[x, b][:blk], tidy[x, b][blk:]
-        za_ref[x * py + b] = jnp.where(z_even, up, down)
-        zb_ref[x * py + b] = jnp.where(z_even, down, up)
+
     for x, y in [(x, y) for x in range(nx) for y in range(ny)]:
         here = a_ref.at[x, y]
         along_z = here[6] * first + here[5] * second
@@ -320,17 +320,6 @@
         parts = unpair(got[:, : 2 * blk]) + unpair(got[:, 2 * blk :])
         for k in range(4):
             part_ref[x, y, k] = parts[k]
-
-    for copy in copies:
-        copy.wait()
-    sent, _ = places(route_ref, where_ref, table_ref, dims, nb)
-    codes_ref[...] = jnp.full_like(codes_ref, -1.0)
-    for i in range(aggregates):
-        a, b, z, t = i // (py * nz * 2), (i // (nz * 2)) % py, (i // 2) % nz, i % 2
-        code = (2 * (jnp.where(pair_ref[a, b, z] == 0, 2, 1) - t) + z).astype(jnp.float32)
-        line = jnp.full((1, LANES), code, jnp.float32)
-        codes_ref[pl.ds(where_ref[2, i], 1), :] = line
-        codes_ref[pl.ds(where_ref[3, i], 1), :] = line
 
     for a, b in [(a, b) for a in range(px) for b in range(py)]:
         own, with_x, with_y, with_z = {}, {}, {}, {}
@@ -376,6 +365,25 @@
     keep_codes_ref[...] = codes_ref[2 * SUB :].astype(jnp.bfloat16)
 
 
+def faces_kernel(grid, zup_ref, zdn_ref, ya_ref, yb_ref, za_ref, zb_ref):
+    px, py, _ = grid
+    blk = zup_ref.shape[1]
+    y_even, z_even = lax.axis_index("gy") % 2 == 0, lax.axis_index("gz") % 2 == 0
+
+    def plane(a, b, half):
+        part = slice(half * blk, (half + 1) * blk)
+        rows = [jnp.concatenate([zdn_ref[x * py + b], zup_ref[x * py + b]], axis=0) for x in (2 * a, 2 * a + 1)]
+        return jnp.concatenate([row[:, part] for row in rows], axis=1)
+
+    for a in range(px):
+        down, up = plane(a, 0, 0), plane(a, py - 1, 1)
+        ya_ref[a], yb_ref[a] = jnp.where(y_even, up, down), jnp.where(y_even, down, up)
+    for at in range(2 * px * py):
+        down, up = zdn_ref[at], zup_ref[at]
+        za_ref[at] = jnp.where(z_even, up, down)
+        zb_ref[at] = jnp.where(z_even, down, up)
+
+
 def outer_left_kernel(grid, left_ref, a_ref, face_ref, part_ref, xface_ref):
     px, py, _ = grid
     nx, ny = 2 * px, 2 * py
@@ -643,22 +651,18 @@
     )(pltpu.with_memory_space_constraint(p_view, pltpu.HBM))
     face = lax.ppermute(face, "gx", swap)
     p_near, a_near = held(p_view, a_view)
-    send_0, total, keep_codes, ya, yb, za, zb, zup, zdn, left = pl.pallas_call(
+    send_0, total, keep_codes, zup, zdn, left = pl.pallas_call(
         functools.partial(inner_kernel, dims, grid),
         out_shape=(
             near(5 * rows + 2 * SUB, LANES),
             pltpu.VMEM((10 * rows, LANES), f32),
             near(2 * SUB, LANES),
-            near(*face_y),
-            near(*face_y),
-            near(*face_z),
-            near(*face_z),
             near(*face_z),
             near(*face_z),
             near(nx * py, 2 * blk, LANES),
         ),
         in_specs=[ANY, ANY, VMEM, VMEM],
-        out_specs=[VMEM] * 10,
+        out_specs=[VMEM] * 6,
         scratch_shapes=[
             pltpu.SMEM(route_row.shape, jnp.int32),
             pltpu.SMEM(pairing.shape, jnp.int32),
@@ -671,12 +675,18 @@
         compiler_params=room,
         cost_estimate=cost,
         name="inner_blocks",
-    )(
-        *[pltpu.with_memory_space_constraint(one, pltpu.HBM) for one in (route_row, pairing)],
-        p_near,
-        a_near,
-    )
+    )(route_row, pairing, p_near, a_near)
     got_0 = lax.ppermute(send_0, "gx", swap)
+    zup, zdn = held(zup, zdn)
+    ya, yb, za, zb = pl.pallas_call(
+        functools.partial(faces_kernel, grid),
+        out_shape=(near(*face_y), near(*face_y), near(*face_z), near(*face_z)),
+        in_specs=[VMEM] * 2,
+        out_specs=[VMEM] * 4,
+        compiler_params=room,
+        cost_estimate=cost,
+        name="faces",
+    )(zup, zdn)
     rounds = swaps(lax.axis_size("gy"), lax.axis_size("gz"))
     halos = []
     for name, value in (("y_a", ya), ("y_b", yb), ("z_a", za), ("z_b", zb)):
@@ -704,7 +714,7 @@
         compiler_params=room,
         cost_estimate=cost,
         name="outer_blocks",
-    )(route_row, pairing, *held(part, zup, zdn, xface, *halos))
+    )(route_row, pairing, *held(part), zup, zdn, *held(xface, *halos))
     got_xy = lax.ppermute(send_xy, "gx", swap)
     got_z = lax.ppermute(send_z, "gx", swap)
 

time: 36.5 us -> 36.2 us (level)
  transfers between devices with their start and end apart: 8 -> 8, of which waited for: 4 -> 4; matrix products, arithmetic and copies ran while one was open for 0% -> 0% of each run, Pallas kernels for 19% -> 18%
where the time goes in v6:
time: 36.2 us; the launch traced here: 36.1 us
  waiting for transfers between devices  18.7 us (52%)
  starting transfers between devices  8.7 us (24%)
  Pallas kernels  8.62 us (24%)
    ppermute x1, waiting for transfers between devices, local(): got_xy = lax.ppermute(send_xy, 'gx', swap)  8.43 us
    ppermute x1, waiting for transfers between devices, local(): got_0 = lax.ppermute(send_0, 'gx', swap)  5.76 us
    ppermute x4, starting transfers between devices, local(): halos.append(lax.ppermute(value, ('gy', 'gz'), rounds[name]))  3.07 us
    ppermute x1, starting transfers between devices, local(): face = lax.ppermute(face, 'gx', swap)  3.04 us
    ppermute x4, waiting for transfers between devices, local(): halos.append(lax.ppermute(value, ('gy', 'gz'), rounds[name]))  2.34 us
    ppermute x1, waiting for transfers between devices, local(): got_z = lax.ppermute(send_z, 'gx', swap)  2.12 us
    pallas_call x2, Pallas kernels, local(): pl.pallas_call(functools.partial(take_kernel, (capacity, rows), with_xy),...  2.12 us
    pallas_call x1, Pallas kernels, local(): pl.pallas_call(functools.partial(inner_kernel, dims, grid), out_shape=(ne...  1.93 us
  transfers between devices with their start and end apart: 8, of which 4 were waited for; matrix products, arithmetic and copies ran while one was open for 0% of the time, Pallas kernels for 18%

profile of v6, /device:TPU:0, one launch (start us, length us, event | category | flops | bytes accessed | tf_op | source)
XLA Modules:
  0.0 36.1 jit_solution(17355743455894099183)
XLA Ops:
  0.0 0.0 copy-start.1
  0.0 0.0 copy-start.2
  0.0 0.0 copy-start.3
  0.0 0.0 copy-start
  0.0 1.0 %face.1 = bf16[4,64,128]{2,1,0:T(8,128)(2,1)S(1)} custom-call(bf16[4,4,64,128]{3,2,1,0:T(8,128)(2,1)} %bitcast.20), custom_call_target="tpu_custom_call" | custom-call | flops 1000000000 | bytes 4000000 | tf_op jit(solution)/shard_map/face/pallas_call | solution.py:642
  1.0 3.0 %collective-permute-start.1 = (bf16[4,64,128]{2,1,0:T(8,128)(2,1)S(1)}, bf16[4,64,128]{2,1,0:T(8,128)(2,1)S(1)}, u32[]{:S(2)}, u32[]{:S(2)}) collective-permute-start(bf16[4,64,128]{2,1,0:T(8,128)(2,1)S(1)} %face.1), channel_id=1, source_target_pairs={{0,16},{16,0},{1,17},{17,1},{2,18},{18,2},{3,19},{19,3},{4,20},{20... | collective-permute-start | bytes 196616 | tf_op jit(solution)/shard_map/ppermute | solution.py:652
  4.1 0.0 copy-done.1
  4.1 0.0 copy-done.2
  4.1 0.0 copy-done.3
  4.1 0.0 copy-done
  4.1 1.9 %inner_blocks.1 = (bf16[1936,128]{1,0:T(8,128)(2,1)S(1)}, f32[3840,128]{1,0:T(8,128)S(1)}, bf16[16,128]{1,0:T(8,128)(2,1)S(1)}, bf16[8,64,128]{2,1,0:T(8,128)(2,...) custom-call(s32[1,16]{1,0:T(1,128)S(1)} %bitcast.22, s32[2,2,2]{2,1,0:T(2,128)S(1)} %copy-done.2, ...), custom_call_target="tpu_custom_call" | custom-call | flops 1000000000 | bytes 4000000 | tf_op jit(solution)/shard_map/inner_blocks/pallas_call | solution.py:654
  6.0 0.1 faces.1
  6.1 0.1 collective-permute-start.4
  6.2 1.6 %collective-permute-start.5 = (bf16[8,64,128]{2,1,0:T(8,128)(2,1)S(1)}, bf16[8,64,128]{2,1,0:T(8,128)(2,1)S(1)}, u32[]{:S(2)}, u32[]{:S(2)}) collective-permute-start(bf16[8,64,128]{2,1,0:T(8,128)(2,1)S(1)} %get-tuple-element.32), channel_id=1, source_target_pairs={{0,4},{1,2},{2,1},{3,7},{4,0},{5,6},{6,5},{7,3},{8,12},{9,10},{10,... | collective-permute-start | bytes 393224 | tf_op jit(solution)/shard_map/ppermute | solution.py:693
  7.9 0.4 %collective-permute-start.2 = (bf16[2,128,128]{2,1,0:T(8,128)(2,1)S(1)}, bf16[2,128,128]{2,1,0:T(8,128)(2,1)S(1)}, u32[]{:S(2)}, u32[]{:S(2)}) collective-permute-start(bf16[2,128,128]{2,1,0:T(8,128)(2,1)S(1)} %get-tuple-element.29), channel_id=1, source_target_pairs={{0,4},{1,5},{2,6},{3,7},{4,0},{5,1},{6,2},{7,3},{8,12},{9,13},{10,... | collective-permute-start | bytes 196616 | tf_op jit(solution)/shard_map/ppermute | solution.py:693
  8.3 0.9 %collective-permute-start.3 = (bf16[2,128,128]{2,1,0:T(8,128)(2,1)S(1)}, bf16[2,128,128]{2,1,0:T(8,128)(2,1)S(1)}, u32[]{:S(2)}, u32[]{:S(2)}) collective-permute-start(bf16[2,128,128]{2,1,0:T(8,128)(2,1)S(1)} %get-tuple-element.30), channel_id=1, source_target_pairs={{0,1},{1,0},{2,3},{3,2},{4,8},{5,9},{6,10},{7,11},{8,4},{9,5},{10,... | collective-permute-start | bytes 196616 | tf_op jit(solution)/shard_map/ppermute | solution.py:693
  9.2 0.0 collective-permute-done.1.face_ref
  9.2 0.5 %collective-permute-start = (bf16[1936,128]{1,0:T(8,128)(2,1)S(1)}, bf16[1936,128]{1,0:T(8,128)(2,1)S(1)}, u32[]{:S(2)}, u32[]{:S(2)}) collective-permute-start(bf16[1936,128]{1,0:T(8,128)(2,1)S(1)} %get-tuple-element.23), channel_id=1, source_target_pairs={{0,16},{16,0},{1,17},{17,1},{2,18},{18,2},{3,19},{19,3},{4,20},{20... | collective-permute-start | bytes 1486856 | tf_op jit(solution)/shard_map/ppermute | solution.py:679
  9.7 0.6 %outer_left.1 = (bf16[4,4,3,64,128]{4,3,2,1,0:T(8,128)(2,1)S(1)}, bf16[2,128,128]{2,1,0:T(8,128)(2,1)S(1)}) custom-call(bf16[8,128,128]{2,1,0:T(8,128)(2,1)S(1)} %get-tuple-element.24.left_ref, bf16[4,4,7,64,128]{4,3,2,1,0:T(8,128)(2,1)S(1)} %bitcast.19, bf16[4,64,128]{2,1,0:T(8,128)(2,1)S(1)} %collective-permute-done.1.face_ref), custom_call_target="tpu_custom_call" | custom-call | flops 1000000000 | bytes 4000000 | tf_op jit(solution)/shard_map/outer_left/pallas_call | solution.py:695
  10.3 2.3 %collective-permute-done.2.ya_ref = bf16[2,128,128]{2,1,0:T(8,128)(2,1)S(1)} collective-permute-done((bf16[2,128,128]{2,1,0:T(8,128)(2,1)S(1)}, bf16[2,128,128]{2,1,0:T(8,128)(2,1)S(1)}, u32[]{:S(2)}, u32[]{:S(2)}) %collective-permute-start.2) | collective-permute-done | bytes 65568 | tf_op jit(solution)/shard_map/ppermute | solution.py:693
  12.6 0.0 collective-permute-done.3.yb_ref
  12.6 0.0 collective-permute-done.4.za_ref
  12.6 0.0 collective-permute-done.5.zb_ref
  12.7 1.9 %outer_blocks.1 = (bf16[1536,128]{1,0:T(8,128)(2,1)S(1)}, bf16[768,128]{1,0:T(8,128)(2,1)S(1)}, bf16[1536,128]{1,0:T(8,128)(2,1)S(1)}, bf16[768,128]{1,0:T(8,128)(2,1)S(1)}) custom-call(s32[1,16]{1,0:T(1,128)S(1)} %bitcast.23, s32[2,2,2]{2,1,0:T(2,128)S(1)} %copy-done.2, bf16[4,4,3,64,128]{4,3,2,1,0:T(8,128)(2,1)S(1)} %get-tuple-element.25.part_ref, ...), custom_call_target="tpu_custom_call" | custom-call | flops 1000000000 | bytes 4000000 | tf_op jit(solution)/shard_map/outer_blocks/pallas_call | solution.py:704
  14.6 0.5 %collective-permute-start.7 = (bf16[1536,128]{1,0:T(8,128)(2,1)S(1)}, bf16[1536,128]{1,0:T(8,128)(2,1)S(1)}, u32[]{:S(2)}, u32[]{:S(2)}) collective-permute-start(bf16[1536,128]{1,0:T(8,128)(2,1)S(1)} %get-tuple-element.39), channel_id=1, source_target_pairs={{0,16},{16,0},{1,17},{17,1},{2,18},{18,2},{3,19},{19,3},{4,20},{20... | collective-permute-start | bytes 1179656 | tf_op jit(solution)/shard_map/ppermute | solution.py:718
  15.1 1.6 %collective-permute-start.6 = (bf16[768,128]{1,0:T(8,128)(2,1)S(1)}, bf16[768,128]{1,0:T(8,128)(2,1)S(1)}, u32[]{:S(2)}, u32[]{:S(2)}) collective-permute-start(bf16[768,128]{1,0:T(8,128)(2,1)S(1)} %get-tuple-element.33), channel_id=1, source_target_pairs={{0,16},{16,0},{1,17},{17,1},{2,18},{18,2},{3,19},{19,3},{4,20},{20... | collective-permute-start | bytes 589832 | tf_op jit(solution)/shard_map/ppermute | solution.py:719
  16.7 1.0 %place_kept.1 = (bf16[11,128,128]{2,1,0:T(8,128)(2,1)S(1)}, bf16[11,768,128]{2,1,0:T(8,128)(2,1)}) custom-call(f32[3840,128]{1,0:T(8,128)S(1)} %get-tuple-element.34.total_ref, bf16[16,128]{1,0:T(8,128)(2,1)S(1)} %get-tuple-element.35.codes_ref, bf16[1536,128]{1,0:T(8,128)(2,1)S(1)} %get-tuple-element.36.xy_ref, bf16[768,128]{1,0:T(8,128)(2,1)S(1)} %get-tuple-element.37.z_ref), custom_call_target="tpu_custom_call" | custom-call | flops 1000000000 | bytes 4000000 | tf_op jit(solution)/shard_map/place_kept/pallas_call | solution.py:723
  17.6 5.8 %collective-permute-done.early_ref = bf16[1936,128]{1,0:T(8,128)(2,1)S(1)} collective-permute-done((bf16[1936,128]{1,0:T(8,128)(2,1)S(1)}, bf16[1936,128]{1,0:T(8,128)(2,1)S(1)}, u32[]{:S(2)}, u32[]{:S(2)}) %collective-permute-start) | collective-permute-done | bytes 495648 | tf_op jit(solution)/shard_map/ppermute | solution.py:679
  23.4 8.4 %collective-permute-done.7.late_ref = bf16[1536,128]{1,0:T(8,128)(2,1)S(1)} collective-permute-done((bf16[1536,128]{1,0:T(8,128)(2,1)S(1)}, bf16[1536,128]{1,0:T(8,128)(2,1)S(1)}, u32[]{:S(2)}, u32[]{:S(2)}) %collective-permute-start.7) | collective-permute-done | bytes 393248 | tf_op jit(solution)/shard_map/ppermute | solution.py:718
  31.8 1.1 %place_xy.1._ = bf16[11,768,128]{2,1,0:T(8,128)(2,1)} custom-call(bf16[1936,128]{1,0:T(8,128)(2,1)S(1)} %collective-permute-done.early_ref, bf16[1536,128]{1,0:T(8,128)(2,1)S(1)} %collective-permute-done.7.late_ref, bf16[11,128,128]{2,1,0:T(8,128)(2,1)S(1)} %get-tuple-element.38.half_ref, ...), custom_call_target="tpu_custom_call", output_to_operand_aliasing={{}: (3, {})} | custom-call | flops 1000000000 | bytes 4000000 | tf_op jit(solution)/shard_map/place_xy/pallas_call | solution.py:734
  32.9 2.1 %collective-permute-done.6.late_ref = bf16[768,128]{1,0:T(8,128)(2,1)S(1)} collective-permute-done((bf16[768,128]{1,0:T(8,128)(2,1)S(1)}, bf16[768,128]{1,0:T(8,128)(2,1)S(1)}, u32[]{:S(2)}, u32[]{:S(2)}) %collective-permute-start.6) | collective-permute-done | bytes 196640 | tf_op jit(solution)/shard_map/ppermute | solution.py:719
  35.1 1.0 %place_z.1 = bf16[11,768,128]{2,1,0:T(8,128)(2,1)} custom-call(bf16[1936,128]{1,0:T(8,128)(2,1)S(1)} %collective-permute-done.early_ref, bf16[768,128]{1,0:T(8,128)(2,1)S(1)} %collective-permute-done.6.late_ref, bf16[11,128,128]{2,1,0:T(8,128)(2,1)S(1)} %get-tuple-element.38.half_ref, bf16[11,768,128]{2,1,0:T(8,128)(2,1)} %place_xy.1._), custom_call_target="tpu_custom_call", output_to_operand_aliasing={{}: (3, {})} | custom-call | flops 1000000000 | bytes 4000000 | tf_op jit(solution)/shard_map/place_z/pallas_call | solution.py:734
Async XLA Ops:
  0.0 4.1 %copy-start.1 = (bf16[4,4,2,4096]{3,2,1,0:T(2,128)(2,1)S(1)}, bf16[4,4,2,4096]{3,2,1,0:T(2,128)(2,1)}, u32[]{:S(2)}) copy-start(bf16[4,4,2,4096]{3,2,1,0:T(2,128)(2,1)} %param.5) | copy-start | bytes 786436
  0.0 4.1 %copy-start.2 = (s32[2,2,2]{2,1,0:T(2,128)S(1)}, s32[2,2,2]{2,1,0:T(2,128)}, u32[]{:S(2)}) copy-start(s32[2,2,2]{2,1,0:T(2,128)} %pair_ref.1) | copy-start | bytes 100
  0.0 4.1 %copy-start.3 = (s32[16,1]{0,1:T(1,128)S(1)}, s32[16,1]{0,1:T(1,128)}, u32[]{:S(2)}) copy-start(s32[16,1]{0,1:T(1,128)} %param.7) | copy-start | bytes 196
  0.0 4.1 %copy-start = (bf16[4,4,2,7,4096]{4,2,3,1,0:T(2,128)(2,1)S(1)}, bf16[4,4,2,7,4096]{4,2,3,1,0:T(2,128)(2,1)}, u32[]{:S(2)}) copy-start(bf16[4,4,2,7,4096]{4,2,3,1,0:T(2,128)(2,1)} %param.4) | copy-start | bytes 5505028
  1.0 8.2 %collective-permute-start.1 = (bf16[4,64,128]{2,1,0:T(8,128)(2,1)S(1)}, bf16[4,64,128]{2,1,0:T(8,128)(2,1)S(1)}, u32[]{:S(2)}, u32[]{:S(2)}) collective-permute-start(bf16[4,64,128]{2,1,0:T(8,128)(2,1)S(1)} %face.1), channel_id=1, source_target_pairs={{0,16},{16,0},{1,17},{17,1},{2,18},{18,2},{3,19},{19,3},{4,20},{20... | collective-permute-start | bytes 196616 | tf_op jit(solution)/shard_map/ppermute | solution.py:652
  6.1 6.5 %collective-permute-start.4 = (bf16[8,64,128]{2,1,0:T(8,128)(2,1)S(1)}, bf16[8,64,128]{2,1,0:T(8,128)(2,1)S(1)}, u32[]{:S(2)}, u32[]{:S(2)}) collective-permute-start(bf16[8,64,128]{2,1,0:T(8,128)(2,1)S(1)} %get-tuple-element.31), channel_id=1, source_target_pairs={{0,1},{1,0},{2,3},{3,2},{4,5},{5,4},{6,7},{7,6},{8,9},{9,8},{10,11... | collective-permute-start | bytes 393224 | tf_op jit(solution)/shard_map/ppermute | solution.py:693
  6.2 6.4 %collective-permute-start.5 = (bf16[8,64,128]{2,1,0:T(8,128)(2,1)S(1)}, bf16[8,64,128]{2,1,0:T(8,128)(2,1)S(1)}, u32[]{:S(2)}, u32[]{:S(2)}) collective-permute-start(bf16[8,64,128]{2,1,0:T(8,128)(2,1)S(1)} %get-tuple-element.32), channel_id=1, source_target_pairs={{0,4},{1,2},{2,1},{3,7},{4,0},{5,6},{6,5},{7,3},{8,12},{9,10},{10,... | collective-permute-start | bytes 393224 | tf_op jit(solution)/shard_map/ppermute | solution.py:693
  7.9 4.8 %collective-permute-start.2 = (bf16[2,128,128]{2,1,0:T(8,128)(2,1)S(1)}, bf16[2,128,128]{2,1,0:T(8,128)(2,1)S(1)}, u32[]{:S(2)}, u32[]{:S(2)}) collective-permute-start(bf16[2,128,128]{2,1,0:T(8,128)(2,1)S(1)} %get-tuple-element.29), channel_id=1, source_target_pairs={{0,4},{1,5},{2,6},{3,7},{4,0},{5,1},{6,2},{7,3},{8,12},{9,13},{10,... | collective-permute-start | bytes 196616 | tf_op jit(solution)/shard_map/ppermute | solution.py:693
  8.3 4.3 %collective-permute-start.3 = (bf16[2,128,128]{2,1,0:T(8,128)(2,1)S(1)}, bf16[2,128,128]{2,1,0:T(8,128)(2,1)S(1)}, u32[]{:S(2)}, u32[]{:S(2)}) collective-permute-start(bf16[2,128,128]{2,1,0:T(8,128)(2,1)S(1)} %get-tuple-element.30), channel_id=1, source_target_pairs={{0,1},{1,0},{2,3},{3,2},{4,8},{5,9},{6,10},{7,11},{8,4},{9,5},{10,... | collective-permute-start | bytes 196616 | tf_op jit(solution)/shard_map/ppermute | solution.py:693
  9.2 14.2 %collective-permute-start = (bf16[1936,128]{1,0:T(8,128)(2,1)S(1)}, bf16[1936,128]{1,0:T(8,128)(2,1)S(1)}, u32[]{:S(2)}, u32[]{:S(2)}) collective-permute-start(bf16[1936,128]{1,0:T(8,128)(2,1)S(1)} %get-tuple-element.23), channel_id=1, source_target_pairs={{0,16},{16,0},{1,17},{17,1},{2,18},{18,2},{3,19},{19,3},{4,20},{20... | collective-permute-start | bytes 1486856 | tf_op jit(solution)/shard_map/ppermute | solution.py:679
  14.6 17.2 %collective-permute-start.7 = (bf16[1536,128]{1,0:T(8,128)(2,1)S(1)}, bf16[1536,128]{1,0:T(8,128)(2,1)S(1)}, u32[]{:S(2)}, u32[]{:S(2)}) collective-permute-start(bf16[1536,128]{1,0:T(8,128)(2,1)S(1)} %get-tuple-element.39), channel_id=1, source_target_pairs={{0,16},{16,0},{1,17},{17,1},{2,18},{18,2},{3,19},{19,3},{4,20},{20... | collective-permute-start | bytes 1179656 | tf_op jit(solution)/shard_map/ppermute | solution.py:718
  15.1 20.0 %collective-permute-start.6 = (bf16[768,128]{1,0:T(8,128)(2,1)S(1)}, bf16[768,128]{1,0:T(8,128)(2,1)S(1)}, u32[]{:S(2)}, u32[]{:S(2)}) collective-permute-start(bf16[768,128]{1,0:T(8,128)(2,1)S(1)} %get-tuple-element.33), channel_id=1, source_target_pairs={{0,16},{16,0},{1,17},{17,1},{2,18},{18,2},{3,19},{19,3},{4,20},{20... | collective-permute-start | bytes 589832 | tf_op jit(solution)/shard_map/ppermute | solution.py:719

commit v7 on v6

--- a/solution.py
+++ b/solution.py
@@ -262,18 +262,10 @@
         done += n
 
 
-def face_kernel(p_hbm, face_ref, sem):
-    last = p_hbm.shape[0] - 1
-    at = jnp.where(lax.axis_index("gx") == 0, last, 0)
-    copy = pltpu.make_async_copy(p_hbm.at[at], face_ref, sem.at[0])
-    copy.start()
-    copy.wait()
-
-
 def inner_kernel(
-    dims, grid, route_hbm, pair_hbm, p_ref, a_ref,
-    send_ref, total_ref, keep_codes_ref, zup_ref, zdn_ref, left_ref,
-    route_ref, pair_ref, part_ref, codes_ref, where_ref, table_ref, sems,
+    dims, grid, route_hbm, pair_hbm, p_hbm, a_hbm,
+    send_ref, total_ref, keep_codes_ref, zup_ref, zdn_ref, left_ref, a_ref,
+    p_ref, route_ref, pair_ref, part_ref, codes_ref, where_ref, table_ref, sems,
 ):
     px, py, nz = grid
     aggregates, _, rows = dims
@@ -283,11 +275,13 @@
     nb = 5
     copies = [
         pltpu.make_async_copy(one, two, sems.at[k])
-        for k, (one, two) in enumerate(((route_hbm, route_ref), (pair_hbm, pair_ref)))
+        for k, (one, two) in enumerate((
+            (p_hbm, p_ref), (route_hbm, route_ref), (pair_hbm, pair_ref), (a_hbm, a_ref),
+        ))
     ]
     for copy in copies:
         copy.start()
-    for copy in copies:
+    for copy in copies[:3]:
         copy.wait()
     sent, _ = places(route_ref, where_ref, table_ref, dims, nb)
     codes_ref[...] = jnp.full_like(codes_ref, -1.0)
@@ -308,6 +302,10 @@
         left_ref[x * py + b] = transposed_dot(spread, both[x, b]).astype(jnp.bfloat16)
         zdn_ref[x * py + b] = tidy[x, b][:blk]
         zup_ref[x * py + b] = tidy[x, b][blk:]
+
+    face = p_ref[jnp.where(lax.axis_index("gx") == 0, nx - 1, 0)]
+    send_ref[nb * rows + 2 * SUB :] = face.reshape(ny * blk, LANES)
+    copies[3].wait()
 
     for x, y in [(x, y) for x in range(nx) for y in range(ny)]:
         here = a_ref.at[x, y]
@@ -361,7 +359,7 @@
             put(total_ref, where_ref, i + 1, 0, rows, sums[1, 1] + jnp.where(flat, sums[0, 1], sums[1, 0]))
 
     finish(((send_ref, nb),), total_ref, 0, dims, sent)
-    send_ref[nb * rows :] = codes_ref[: 2 * SUB].astype(jnp.bfloat16)
+    send_ref[nb * rows : nb * rows + 2 * SUB] = codes_ref[: 2 * SUB].astype(jnp.bfloat16)
     keep_codes_ref[...] = codes_ref[2 * SUB :].astype(jnp.bfloat16)
 
 
@@ -384,14 +382,10 @@
         zb_ref[at] = jnp.where(z_even, down, up)
 
 
-def outer_left_kernel(grid, left_ref, a_ref, face_ref, part_ref, xface_ref):
+def outer_left_kernel(grid, left_ref, a_ref, part_ref):
     px, py, _ = grid
     nx, ny = 2 * px, 2 * py
     blk = a_ref.shape[3]
-    clean, _ = constants(blk)
-    for b in range(py):
-        both = pair(face_ref[2 * b], face_ref[2 * b + 1])
-        xface_ref[b] = dot(clean, both).astype(jnp.bfloat16)
     masks = even_lanes(blk // 2)
     first, second = even_rows(blk)
     for x, y in [(x, y) for x in range(nx) for y in range(ny)]:
@@ -408,22 +402,18 @@
         part_ref[x, y, 2] = jnp.concatenate([along[:blk], along[blk:]], axis=1)
 
 
-def outer_kernel(
-    dims, grid, route_ref, pair_ref, part_ref, zup_ref, zdn_ref,
-    xface_ref, ya_ref, yb_ref, za_ref, zb_ref,
-    send_xy_ref, send_z_ref, keep_xy_ref, keep_z_ref,
-    total_ref, where_ref, table_ref,
+def outer_yz_kernel(
+    dims, grid, route_ref, pair_ref, part_ref, zup_ref, zdn_ref, ya_ref, yb_ref, za_ref, zb_ref,
+    send_ref, keep_ref, total_ref, where_ref, table_ref,
 ):
     px, py, nz = grid
     _, _, rows = dims
     nx, ny = 2 * px, 2 * py
     blk = part_ref.shape[3]
     q = blk // 2
-    nb = 6
+    nb = 4
     sent, kept = places(route_ref, where_ref, table_ref, dims, nb)
-    me = lax.axis_index("gx")
     line = iota((blk, LANES), 0) * 0
-    above = line + me > 0
 
     def from_sides(axis, first_ref, second_ref, at, high):
         index = lax.axis_index(axis)
@@ -433,15 +423,6 @@
         value = jnp.where(by_first, first_ref[at], second_ref[at]).astype(jnp.float32)
         return jnp.where(kept, value, 0.0).astype(jnp.bfloat16)
 
-
-    def beside_x(x, b, z, u):
-        to = x - 1 if u == 0 else x + 1
-        if 0 <= to < nx:
-            return (zdn_ref, zup_ref)[z][to * py + b]
-        part = xface_ref[b, z * blk : (z + 1) * blk].astype(jnp.float32)
-        part = jnp.where(above, part, 0.0) if u == 0 else jnp.where(above, 0.0, part)
-        return part.astype(jnp.bfloat16)
-
     def beside_y(x, y, z, v):
         to = y - 1 if v == 0 else y + 1
         if 0 <= to < ny:
@@ -453,27 +434,69 @@
         made = []
         for b, z in [(b, z) for b in range(py) for z in range(nz)]:
             zs = pl.ds(z * q, q)
-            u, a = x % 2, x // 2
-            along_x = weights_of(beside_x(x, b, z, u))
             along_z = weights_of(from_sides("gz", za_ref, zb_ref, x * py + b, z == 1))
-            flat = pair_ref[a, b, z] == 0
             for v in range(2):
                 y = 2 * b + v
-                t = u if u == v else jnp.where(flat, v, u)
-                m = u if u == v else jnp.where(flat, u, v)
-                i = ((a * py + b) * nz + z) * 2 + t
+                i, m = of_element(pair_ref, grid, x, y, z)
                 other, k = beside_y(x, y, z, v)
                 along_y = weights_of(other)[k]
-                made.append((i, 2 * m, dot(part_ref[x, y, 0, zs], along_x[v])))
-                made.append((i, 2 * m + 1, dot(part_ref[x, y, 1, zs], along_y)))
-                made.append((i, 4 + m, dot(part_ref[x, y, 2, zs], along_z[v])))
+                made.append((i, m, dot(part_ref[x, y, 1, zs], along_y)))
+                made.append((i, 2 + m, dot(part_ref[x, y, 2, zs], along_z[v])))
         for i, block, got in made:
             put(total_ref, where_ref, i, block, rows, got)
 
-    for kind, (xy, along, count) in enumerate((
-        (send_xy_ref, send_z_ref, sent), (keep_xy_ref, keep_z_ref, kept),
-    )):
-        finish(((xy, 4), (along, 2)), total_ref, kind, dims, count)
+    for kind, (out, count) in enumerate(((send_ref, sent), (keep_ref, kept))):
+        finish(((out, nb),), total_ref, kind, dims, count)
+
+
+def outer_x_kernel(
+    dims, grid, route_ref, pair_ref, part_ref, zup_ref, zdn_ref, early_ref,
+    send_ref, keep_ref, total_ref, where_ref, table_ref,
+):
+    px, py, nz = grid
+    _, _, rows = dims
+    nx, ny = 2 * px, 2 * py
+    blk = part_ref.shape[3]
+    q = blk // 2
+    nb = 2
+    sent, kept = places(route_ref, where_ref, table_ref, dims, nb)
+    above = iota((2 * blk, LANES), 0) * 0 + lax.axis_index("gx") > 0
+    clean, _ = constants(blk)
+    face = early_ref.shape[0] - ny * blk
+    low, high = [], []
+    for b in range(py):
+        at = face + 2 * b * blk
+        tidy = dot(clean, pair(early_ref[at : at + blk], early_ref[at + blk : at + 2 * blk]))
+        low.append(jnp.where(above, tidy, 0.0).astype(jnp.bfloat16))
+        high.append(jnp.where(above, 0.0, tidy).astype(jnp.bfloat16))
+
+    for x in range(nx):
+        made = []
+        for b, z in [(b, z) for b in range(py) for z in range(nz)]:
+            zs = pl.ds(z * q, q)
+            to = x - 1 if x % 2 == 0 else x + 1
+            if 0 <= to < nx:
+                part = (zdn_ref, zup_ref)[z][to * py + b]
+            else:
+                part = (low if to < 0 else high)[b][z * blk : (z + 1) * blk]
+            along_x = weights_of(part)
+            for v in range(2):
+                i, m = of_element(pair_ref, grid, x, 2 * b + v, z)
+                made.append((i, m, dot(part_ref[x, 2 * b + v, 0, zs], along_x[v])))
+        for i, block, got in made:
+            put(total_ref, where_ref, i, block, rows, got)
+
+    for kind, (out, count) in enumerate(((send_ref, sent), (keep_ref, kept))):
+        finish(((out, nb),), total_ref, kind, dims, count)
+
+
+def of_element(pair_ref, grid, x, y, z):
+    _, py, nz = grid
+    a, b, u, v = x // 2, y // 2, x % 2, y % 2
+    flat = pair_ref[a, b, z] == 0
+    t = u if u == v else jnp.where(flat, v, u)
+    m = u if u == v else jnp.where(flat, u, v)
+    return ((a * py + b) * nz + z) * 2 + t, m
 
 
 def received(early_ref, rows):
@@ -483,23 +506,24 @@
     return early
 
 
-def placed_blocks(early, xy_ref, z_ref, code, rows, at, size):
+def placed_blocks(early, x_ref, yz_ref, code, rows, at, size, without_x=True):
     near_low, near_high = (code < 1.5)[None], (code > 3.5)[None]
     upper = ((code == 1.0) | (code == 3.0) | (code == 5.0))[None]
 
     def tiles(ref, k):
         return ref[k * rows + at : k * rows + at + size].reshape(-1, 2 * SUB, LANES)
 
-    if xy_ref is not None:
+    if without_x:
         yield 0, early(0, at, size)
-        for m in range(2):
-            cross, x_out, y_out = early(1 + m, at, size), tiles(xy_ref, 2 * m), tiles(xy_ref, 2 * m + 1)
+    for m in range(2):
+        cross, y_out = early(1 + m, at, size), tiles(yz_ref, m)
+        if x_ref is not None:
+            x_out = tiles(x_ref, m)
             yield 1 + 5 * m, jnp.where(near_low, cross, x_out)
             yield 2 + 5 * m, jnp.where(near_low, x_out, jnp.where(near_high, y_out, cross))
+        if without_x:
+            z_in, z_out = early(3 + m, at, size), tiles(yz_ref, 2 + m)
             yield 3 + 5 * m, jnp.where(near_high, cross, y_out)
-    if z_ref is not None:
-        for m in range(2):
-            z_in, z_out = early(3 + m, at, size), tiles(z_ref, m)
             yield 4 + 5 * m, jnp.where(upper, z_in, z_out)
             yield 5 + 5 * m, jnp.where(upper, z_out, z_in)
 
@@ -508,7 +532,7 @@
     return jnp.concatenate([codes, codes], axis=0)
 
 
-def keep_kernel(dims, total_ref, codes_ref, xy_ref, z_ref, half_ref, out_hbm, full_ref, sem):
+def keep_kernel(dims, total_ref, codes_ref, x_ref, yz_ref, half_ref, out_hbm, full_ref, sem):
     cap, rows = dims
     full = (cap - cap % SUB) * (rows // cap)
     me = lax.axis_index("gx")
@@ -525,34 +549,37 @@
 
     copies = []
     code = twice(codes_ref[:SUB])
-    for k, value in placed_blocks(rounded(code), xy_ref, z_ref, code, rows, 0, full):
+    for k, value in placed_blocks(rounded(code), x_ref, yz_ref, code, rows, 0, full):
         full_ref[k] = value.reshape(full, LANES)
         to = out_hbm.at[k, pl.ds(me * (2 * full), full), :]
         copies.append(pltpu.make_async_copy(full_ref.at[k], to, sem.at[k]))
         copies[-1].start()
     code = twice(codes_ref[SUB:])
-    for k, value in placed_blocks(rounded(code), xy_ref, z_ref, code, rows, full, rows - full):
+    for k, value in placed_blocks(rounded(code), x_ref, yz_ref, code, rows, full, rows - full):
         half_ref[k] = value.reshape(rows - full, LANES)
     for copy in copies:
         copy.wait()
 
 
-def take_kernel(dims, with_xy, early_ref, late_ref, half_ref, _, out_hbm, full_ref, mixed_ref, sem):
+def take_kernel(dims, with_x, early_ref, *refs):
+    late, (half_ref, _, out_hbm, full_ref, mixed_ref, sem) = refs[: -6], refs[-6:]
     cap, rows = dims
     full = (cap - cap % SUB) * (rows // cap)
     me = lax.axis_index("gx")
-    codes = early_ref[5 * rows :]
-    xy_ref, z_ref = (late_ref, None) if with_xy else (None, late_ref)
+    codes = early_ref[5 * rows : 5 * rows + 2 * SUB]
+    x_ref, yz_ref = late if with_x else (None, late[0])
     early = received(early_ref, rows)
     copies = []
-    for k, value in placed_blocks(early, xy_ref, z_ref, twice(codes[:SUB]), rows, 0, full):
+    for k, value in placed_blocks(early, x_ref, yz_ref, twice(codes[:SUB]), rows, 0, full, not with_x):
         full_ref[k] = value.reshape(full, LANES)
         to = out_hbm.at[k, pl.ds((1 - me) * (2 * full), full), :]
         copies.append(pltpu.make_async_copy(full_ref.at[k], to, sem.at[0, k]))
         copies[-1].start()
     first_half = (iota((SUB, LANES), 0) < SUB // 2)[None]
     pick = first_half == (me == 0)
-    for k, value in placed_blocks(early, xy_ref, z_ref, twice(codes[SUB:]), rows, full, rows - full):
+    for k, value in placed_blocks(
+        early, x_ref, yz_ref, twice(codes[SUB:]), rows, full, rows - full, not with_x
+    ):
         theirs = value.reshape(rows - full, LANES).astype(jnp.float32).reshape(-1, SUB, LANES)
         mine = half_ref[k].astype(jnp.float32).reshape(-1, SUB, LANES)
         low = jnp.where(pick, mine, theirs)
@@ -633,49 +660,39 @@
     dims, grid = (aggregates, capacity, rows), (px, py, nz)
     f32 = jnp.float32
     half_type = jnp.bfloat16
-    face_x, face_y, face_z = (py, 2 * blk, LANES), (px, 2 * blk, LANES), (nx * py, blk, LANES)
+    face_y, face_z = (px, 2 * blk, LANES), (nx * py, blk, LANES)
     parts = (nx, ny, 3, blk, LANES)
     room = pltpu.CompilerParams(vmem_limit_bytes=24 * 2**20)
     cost = pl.CostEstimate(flops=10**9, bytes_accessed=4 * 10**6, transcendentals=0)
 
     swap = [(0, 1), (1, 0)]
-    face = pl.pallas_call(
-        face_kernel,
-        out_shape=near(ny, blk, LANES),
-        in_specs=[ANY],
-        out_specs=VMEM,
-        scratch_shapes=[pltpu.SemaphoreType.DMA((1,))],
-        compiler_params=room,
-        cost_estimate=cost,
-        name="face",
-    )(pltpu.with_memory_space_constraint(p_view, pltpu.HBM))
-    face = lax.ppermute(face, "gx", swap)
-    p_near, a_near = held(p_view, a_view)
-    send_0, total, keep_codes, zup, zdn, left = pl.pallas_call(
+    send_0, total, keep_codes, zup, zdn, left, a_near = pl.pallas_call(
         functools.partial(inner_kernel, dims, grid),
         out_shape=(
-            near(5 * rows + 2 * SUB, LANES),
+            near(5 * rows + 2 * SUB + ny * blk, LANES),
             pltpu.VMEM((10 * rows, LANES), f32),
             near(2 * SUB, LANES),
             near(*face_z),
             near(*face_z),
             near(nx * py, 2 * blk, LANES),
+            near(*a_view.shape),
         ),
-        in_specs=[ANY, ANY, VMEM, VMEM],
-        out_specs=[VMEM] * 6,
+        in_specs=[ANY] * 4,
+        out_specs=[VMEM] * 7,
         scratch_shapes=[
+            pltpu.VMEM(p_view.shape, half_type),
             pltpu.SMEM(route_row.shape, jnp.int32),
             pltpu.SMEM(pairing.shape, jnp.int32),
             pltpu.VMEM((nx, ny, 4, blk, LANES), half_type),
             pltpu.VMEM((4 * SUB, LANES), f32),
             pltpu.SMEM((4, aggregates), jnp.int32),
             pltpu.SMEM((4, capacity), jnp.int32),
-            pltpu.SemaphoreType.DMA((2,)),
+            pltpu.SemaphoreType.DMA((4,)),
         ],
         compiler_params=room,
         cost_estimate=cost,
         name="inner_blocks",
-    )(route_row, pairing, p_near, a_near)
+    )(*[pltpu.with_memory_space_constraint(one, pltpu.HBM) for one in (route_row, pairing, p_view, a_view)])
     got_0 = lax.ppermute(send_0, "gx", swap)
     zup, zdn = held(zup, zdn)
     ya, yb, za, zb = pl.pallas_call(
@@ -692,31 +709,37 @@
     for name, value in (("y_a", ya), ("y_b", yb), ("z_a", za), ("z_b", zb)):
         halos.append(lax.ppermute(value, ("gy", "gz"), rounds[name]))
 
-    part, xface = pl.pallas_call(
+    left, a_near = held(left, a_near)
+    part = pl.pallas_call(
         functools.partial(outer_left_kernel, grid),
-        out_shape=(near(*parts), near(*face_x)),
-        in_specs=[VMEM] * 3,
-        out_specs=[VMEM] * 2,
+        out_shape=near(*parts),
+        in_specs=[VMEM] * 2,
+        out_specs=VMEM,
         compiler_params=room,
         cost_estimate=cost,
         name="outer_left",
-    )(*held(left), a_near, *held(face))
-    send_xy, send_z, keep_xy, keep_z = pl.pallas_call(
-        functools.partial(outer_kernel, dims, grid),
-        out_shape=(near(4 * rows, LANES), near(2 * rows, LANES)) * 2,
-        in_specs=[SMEM, SMEM] + [VMEM] * 8,
-        out_specs=[VMEM] * 4,
-        scratch_shapes=[
-            pltpu.VMEM((12 * rows, LANES), f32),
-            pltpu.SMEM((4, aggregates), jnp.int32),
-            pltpu.SMEM((4, capacity), jnp.int32),
-        ],
-        compiler_params=room,
-        cost_estimate=cost,
-        name="outer_blocks",
-    )(route_row, pairing, *held(part), zup, zdn, *held(xface, *halos))
-    got_xy = lax.ppermute(send_xy, "gx", swap)
-    got_z = lax.ppermute(send_z, "gx", swap)
+    )(left, a_near)
+    part = held(part)[0]
+
+    def outer(kernel, blocks, *arrays):
+        return pl.pallas_call(
+            functools.partial(kernel, dims, grid),
+            out_shape=(near(blocks * rows, LANES),) * 2,
+            in_specs=[SMEM, SMEM] + [VMEM] * (3 + len(arrays)),
+            out_specs=[VMEM] * 2,
+            scratch_shapes=[
+                pltpu.VMEM((2 * blocks * rows, LANES), f32),
+                pltpu.SMEM((4, aggregates), jnp.int32),
+                pltpu.SMEM((4, capacity), jnp.int32),
+            ],
+            compiler_params=room,
+            cost_estimate=cost,
+        )(route_row, pairing, part, zup, zdn, *held(*arrays))
+
+    send_yz, keep_yz = outer(outer_yz_kernel, 4, *halos)
+    got_yz = lax.ppermute(send_yz, "gx", swap)
+    send_x, keep_x = outer(outer_x_kernel, 2, got_0)
+    got_x = lax.ppermute(send_x, "gx", swap)
 
     full = (capacity // SUB) * SUB * lines
     whole = 2 * rows
@@ -729,14 +752,14 @@
         compiler_params=room,
         cost_estimate=cost,
         name="place_kept",
-    )(*held(total, keep_codes, keep_xy, keep_z))
-    for with_xy, late in ((True, got_xy), (False, got_z)):
+    )(*held(total, keep_codes, keep_x, keep_yz))
+    for with_x, late in ((False, (got_yz,)), (True, (got_x, got_yz))):
         out = pl.pallas_call(
-            functools.partial(take_kernel, (capacity, rows), with_xy),
+            functools.partial(take_kernel, (capacity, rows), with_x),
             out_shape=bf16(11, whole, LANES),
-            in_specs=[VMEM] * 3 + [ANY],
+            in_specs=[VMEM] * (2 + len(late)) + [ANY],
             out_specs=ANY,
-            input_output_aliases={3: 0},
+            input_output_aliases={2 + len(late): 0},
             scratch_shapes=[
                 pltpu.VMEM((11, full, LANES), half_type),
                 pltpu.VMEM((11, full, LANES), half_type),
@@ -744,8 +767,8 @@
             ],
             compiler_params=room,
             cost_estimate=cost,
-            name="place_xy" if with_xy else "place_z",
-        )(*held(got_0, late, half), out)
+            name="place_x" if with_x else "place_yz",
+        )(*held(got_0, *late, half), out)
     out = out.reshape(11, whole // (SUB * lines), lines, SUB, LANES).transpose(1, 3, 0, 2, 4)
     return out.reshape(2 * capacity, 11, entries)
 

time: 36.2 us -> 32.3 us (0.89)
  waiting for transfers between devices: 18.7 us -> 14.3 us
  Pallas kernels: 8.62 us -> 9.46 us
  starting transfers between devices: 8.7 us -> 8.31 us
    ppermute x3 -> x2, waiting for transfers between devices: 10.6 us -> 6.31 us  [the longest x1 4.08 us: local(): got_yz = lax.ppermute(send_yz, 'gx', swap)]
    ppermute x3 -> x2, starting transfers between devices: 5.14 us -> 2.26 us  [the longest x1 2.08 us: local(): got_x = lax.ppermute(send_x, 'gx', swap)]
    ppermute x1, starting transfers between devices: 0.5 us -> 2.99 us  [local(): got_0 = lax.ppermute(send_0, 'gx', swap)]
    pallas_call x1, Pallas kernels: 1.93 us -> 2.84 us  [local(): pl.pallas_call(functools.partial(inner_kernel, dims, grid), out_shape=(ne...]
    ppermute x1, waiting for transfers between devices: 5.76 us -> 5.12 us  [local(): got_0 = lax.ppermute(send_0, 'gx', swap)]
    ppermute x4, waiting for transfers between devices: 2.34 us -> 2.87 us  [local(): halos.append(lax.ppermute(value, ('gy', 'gz'), rounds[name]))]
  transfers between devices with their start and end apart: 8 -> 7, of which waited for: 4 -> 4; matrix products, arithmetic and copies ran while one was open for 0% -> 0% of each run, Pallas kernels for 18% -> 17%
where the time goes in v7:
time: 32.3 us; the launch traced here: 32.2 us
  waiting for transfers between devices  14.3 us (44%)
  Pallas kernels  9.46 us (29%)
  starting transfers between devices  8.31 us (26%)
    ppermute x1, waiting for transfers between devices, local(): got_0 = lax.ppermute(send_0, 'gx', swap)  5.12 us
    ppermute x1, waiting for transfers between devices, local(): got_yz = lax.ppermute(send_yz, 'gx', swap)  4.08 us
    ppermute x4, starting transfers between devices, local(): halos.append(lax.ppermute(value, ('gy', 'gz'), rounds[name]))  3.06 us
    ppermute x1, starting transfers between devices, local(): got_0 = lax.ppermute(send_0, 'gx', swap)  2.99 us
    pallas_call x2, Pallas kernels, outer(): pl.pallas_call(functools.partial(kernel, dims, grid), out_shape=(near(blo...  2.87 us
    ppermute x4, waiting for transfers between devices, local(): halos.append(lax.ppermute(value, ('gy', 'gz'), rounds[name]))  2.87 us
    pallas_call x1, Pallas kernels, local(): pl.pallas_call(functools.partial(inner_kernel, dims, grid), out_shape=(ne...  2.84 us
    ppermute x1, waiting for transfers between devices, local(): got_x = lax.ppermute(send_x, 'gx', swap)  2.24 us
  transfers between devices with their start and end apart: 7, of which 4 were waited for; matrix products, arithmetic and copies ran while one was open for 0% of the time, Pallas kernels for 17%

profile of v7, /device:TPU:0, one launch (start us, length us, event | category | flops | bytes accessed | tf_op | source)
XLA Modules:
  0.0 32.2 jit_solution(303540684028032021)
XLA Ops:
  0.0 2.8 %inner_blocks.1 = (bf16[2192,128]{1,0:T(8,128)(2,1)S(1)}, f32[3840,128]{1,0:T(8,128)S(1)}, bf16[16,128]{1,0:T(8,128)(2,1)S(1)}, bf16[8,64,128]{2,1,0:T(8,128)(2,...) custom-call(s32[1,16]{1,0:T(1,128)} %bitcast.18, ...), custom_call_target="tpu_custom_call" | custom-call | flops 1000000000 | bytes 4000000 | tf_op jit(solution)/shard_map/inner_blocks/pallas_call | solution.py:669
  2.8 3.0 %collective-permute-start = (bf16[2192,128]{1,0:T(8,128)(2,1)S(1)}, bf16[2192,128]{1,0:T(8,128)(2,1)S(1)}, u32[]{:S(2)}, u32[]{:S(2)}) collective-permute-start(bf16[2192,128]{1,0:T(8,128)(2,1)S(1)} %get-tuple-element.22), channel_id=1, source_target_pairs={{0,16},{16,0},{1,17},{17,1},{2,18},{18,2},{3,19},{19,3},{4,20},{20... | collective-permute-start | bytes 1683464 | tf_op jit(solution)/shard_map/ppermute | solution.py:696
  5.8 0.1 faces.1
  5.9 0.0 copy-start
  6.0 0.0 copy-start.1
  6.0 0.1 collective-permute-start.4
  6.1 1.6 %collective-permute-start.5 = (bf16[8,64,128]{2,1,0:T(8,128)(2,1)S(1)}, bf16[8,64,128]{2,1,0:T(8,128)(2,1)S(1)}, u32[]{:S(2)}, u32[]{:S(2)}) collective-permute-start(bf16[8,64,128]{2,1,0:T(8,128)(2,1)S(1)} %get-tuple-element.31), channel_id=1, source_target_pairs={{0,4},{1,2},{2,1},{3,7},{4,0},{5,6},{6,5},{7,3},{8,12},{9,10},{10,... | collective-permute-start | bytes 393224 | tf_op jit(solution)/shard_map/ppermute | solution.py:710
  7.7 0.5 %collective-permute-start.2 = (bf16[2,128,128]{2,1,0:T(8,128)(2,1)S(1)}, bf16[2,128,128]{2,1,0:T(8,128)(2,1)S(1)}, u32[]{:S(2)}, u32[]{:S(2)}) collective-permute-start(bf16[2,128,128]{2,1,0:T(8,128)(2,1)S(1)} %get-tuple-element.28), channel_id=1, source_target_pairs={{0,4},{1,5},{2,6},{3,7},{4,0},{5,1},{6,2},{7,3},{8,12},{9,13},{10,... | collective-permute-start | bytes 196616 | tf_op jit(solution)/shard_map/ppermute | solution.py:710
  8.1 0.9 %collective-permute-start.3 = (bf16[2,128,128]{2,1,0:T(8,128)(2,1)S(1)}, bf16[2,128,128]{2,1,0:T(8,128)(2,1)S(1)}, u32[]{:S(2)}, u32[]{:S(2)}) collective-permute-start(bf16[2,128,128]{2,1,0:T(8,128)(2,1)S(1)} %get-tuple-element.29), channel_id=1, source_target_pairs={{0,1},{1,0},{2,3},{3,2},{4,8},{5,9},{6,10},{7,11},{8,4},{9,5},{10,... | collective-permute-start | bytes 196616 | tf_op jit(solution)/shard_map/ppermute | solution.py:710
  9.0 0.6 %outer_left.1.part_ref = bf16[4,4,3,64,128]{4,3,2,1,0:T(8,128)(2,1)S(1)} custom-call(bf16[8,128,128]{2,1,0:T(8,128)(2,1)S(1)} %get-tuple-element.23.left_ref, bf16[4,4,7,64,128]{4,3,2,1,0:T(8,128)(2,1)S(1)} %get-tuple-element.24.a_ref), custom_call_target="tpu_custom_call" | custom-call | flops 1000000000 | bytes 4000000 | tf_op jit(solution)/shard_map/outer_left/pallas_call | solution.py:713
  9.6 2.9 %collective-permute-done.2.ya_ref = bf16[2,128,128]{2,1,0:T(8,128)(2,1)S(1)} collective-permute-done((bf16[2,128,128]{2,1,0:T(8,128)(2,1)S(1)}, bf16[2,128,128]{2,1,0:T(8,128)(2,1)S(1)}, u32[]{:S(2)}, u32[]{:S(2)}) %collective-permute-start.2) | collective-permute-done | bytes 65568 | tf_op jit(solution)/shard_map/ppermute | solution.py:710
  12.5 0.0 collective-permute-done.3.yb_ref
  12.5 0.0 collective-permute-done.4.za_ref
  12.5 0.0 collective-permute-done.5.zb_ref
  12.5 0.0 copy-done
  12.5 0.0 copy-done.1
  12.5 1.6 %shard_map.47 = (bf16[1536,128]{1,0:T(8,128)(2,1)S(1)}, bf16[1536,128]{1,0:T(8,128)(2,1)S(1)}) custom-call(s32[1,16]{1,0:T(1,128)S(1)} %bitcast.19, s32[2,2,2]{2,1,0:T(2,128)S(1)} %copy-done, bf16[4,4,3,64,128]{4,3,2,1,0:T(8,128)(2,1)S(1)} %outer_left.1.part_ref, bf16[8,64,128]{2,1,0:T(8,128)(2,1)S(1)} %get-tuple-element.25.zup_ref, ...), custom_call_target="tpu_custom_call" | custom-call | flops 1000000000 | bytes 4000000 | tf_op jit(solution)/shard_map/pallas_call | solution.py:725
  14.1 0.2 collective-permute-start.6
  14.3 5.1 %collective-permute-done.early_ref = bf16[2192,128]{1,0:T(8,128)(2,1)S(1)} collective-permute-done((bf16[2192,128]{1,0:T(8,128)(2,1)S(1)}, bf16[2192,128]{1,0:T(8,128)(2,1)S(1)}, u32[]{:S(2)}, u32[]{:S(2)}) %collective-permute-start) | collective-permute-done | bytes 561184 | tf_op jit(solution)/shard_map/ppermute | solution.py:696
  19.4 1.3 %shard_map.46 = (bf16[768,128]{1,0:T(8,128)(2,1)S(1)}, bf16[768,128]{1,0:T(8,128)(2,1)S(1)}) custom-call(s32[1,16]{1,0:T(1,128)S(1)} %bitcast.20, s32[2,2,2]{2,1,0:T(2,128)S(1)} %copy-done, bf16[4,4,3,64,128]{4,3,2,1,0:T(8,128)(2,1)S(1)} %outer_left.1.part_ref, bf16[8,64,128]{2,1,0:T(8,128)(2,1)S(1)} %get-tuple-element.25.zup_ref, ...), custom_call_target="tpu_custom_call" | custom-call | flops 1000000000 | bytes 4000000 | tf_op jit(solution)/shard_map/pallas_call | solution.py:725
  20.7 2.1 %collective-permute-start.1 = (bf16[768,128]{1,0:T(8,128)(2,1)S(1)}, bf16[768,128]{1,0:T(8,128)(2,1)S(1)}, u32[]{:S(2)}, u32[]{:S(2)}) collective-permute-start(bf16[768,128]{1,0:T(8,128)(2,1)S(1)} %get-tuple-element.27), channel_id=1, source_target_pairs={{0,16},{16,0},{1,17},{17,1},{2,18},{18,2},{3,19},{19,3},{4,20},{20... | collective-permute-start | bytes 589832 | tf_op jit(solution)/shard_map/ppermute | solution.py:742
  22.8 1.0 %place_kept.1 = (bf16[11,128,128]{2,1,0:T(8,128)(2,1)S(1)}, bf16[11,768,128]{2,1,0:T(8,128)(2,1)}) custom-call(f32[3840,128]{1,0:T(8,128)S(1)} %get-tuple-element.33.total_ref, bf16[16,128]{1,0:T(8,128)(2,1)S(1)} %get-tuple-element.34.codes_ref, bf16[768,128]{1,0:T(8,128)(2,1)S(1)} %get-tuple-element.35.x_ref, bf16[1536,128]{1,0:T(8,128)(2,1)S(1)} %get-tuple-element.36.yz_ref), custom_call_target="tpu_custom_call" | custom-call | flops 1000000000 | bytes 4000000 | tf_op jit(solution)/shard_map/place_kept/pallas_call | solution.py:746
  23.8 4.1 %collective-permute-done.6.refs_0_.refs_1_ = bf16[1536,128]{1,0:T(8,128)(2,1)S(1)} collective-permute-done((bf16[1536,128]{1,0:T(8,128)(2,1)S(1)}, bf16[1536,128]{1,0:T(8,128)(2,1)S(1)}, u32[]{:S(2)}, u32[]{:S(2)}) %collective-permute-start.6) | collective-permute-done | bytes 393248 | tf_op jit(solution)/shard_map/ppermute | solution.py:740
  27.8 1.1 %place_yz.1.refs_3_ = bf16[11,768,128]{2,1,0:T(8,128)(2,1)} custom-call(bf16[2192,128]{1,0:T(8,128)(2,1)S(1)} %collective-permute-done.early_ref, bf16[1536,128]{1,0:T(8,128)(2,1)S(1)} %collective-permute-done.6.refs_0_.refs_1_, bf16[11,128,128]{2,1,0:T(8,128)(2,1)S(1)} %get-tuple-element.37.refs_1_.refs_2_, ...), custom_call_target="tpu_custom_call", output_to_operand_aliasing={{}: (3, {})} | custom-call | flops 1000000000 | bytes 4000000 | tf_op jit(solution)/shard_map/place_yz/pallas_call | solution.py:757
  29.0 2.2 %collective-permute-done.1.refs_0_ = bf16[768,128]{1,0:T(8,128)(2,1)S(1)} collective-permute-done((bf16[768,128]{1,0:T(8,128)(2,1)S(1)}, bf16[768,128]{1,0:T(8,128)(2,1)S(1)}, u32[]{:S(2)}, u32[]{:S(2)}) %collective-permute-start.1) | collective-permute-done | bytes 196640 | tf_op jit(solution)/shard_map/ppermute | solution.py:742
  31.2 1.0 %place_x.1 = bf16[11,768,128]{2,1,0:T(8,128)(2,1)} custom-call(bf16[2192,128]{1,0:T(8,128)(2,1)S(1)} %collective-permute-done.early_ref, bf16[768,128]{1,0:T(8,128)(2,1)S(1)} %collective-permute-done.1.refs_0_, bf16[1536,128]{1,0:T(8,128)(2,1)S(1)} %collective-permute-done.6.refs_0_.refs_1_, ...), custom_call_target="tpu_custom_call", output_to_operand_aliasing={{}: (4, {})} | custom-call | flops 1000000000 | bytes 4000000 | tf_op jit(solution)/shard_map/place_x/pallas_call | solution.py:757
Async XLA Ops:
  2.8 16.6 %collective-permute-start = (bf16[2192,128]{1,0:T(8,128)(2,1)S(1)}, bf16[2192,128]{1,0:T(8,128)(2,1)S(1)}, u32[]{:S(2)}, u32[]{:S(2)}) collective-permute-start(bf16[2192,128]{1,0:T(8,128)(2,1)S(1)} %get-tuple-element.22), channel_id=1, source_target_pairs={{0,16},{16,0},{1,17},{17,1},{2,18},{18,2},{3,19},{19,3},{4,20},{20... | collective-permute-start | bytes 1683464 | tf_op jit(solution)/shard_map/ppermute | solution.py:696
  5.9 6.6 %copy-start = (s32[2,2,2]{2,1,0:T(2,128)S(1)}, s32[2,2,2]{2,1,0:T(2,128)}, u32[]{:S(2)}) copy-start(s32[2,2,2]{2,1,0:T(2,128)} %pair_ref.3) | copy-start | bytes 100
  6.0 6.6 %copy-start.1 = (s32[16,1]{0,1:T(1,128)S(1)}, s32[16,1]{0,1:T(1,128)}, u32[]{:S(2)}) copy-start(s32[16,1]{0,1:T(1,128)} %param.7) | copy-start | bytes 196
  6.0 6.5 %collective-permute-start.4 = (bf16[8,64,128]{2,1,0:T(8,128)(2,1)S(1)}, bf16[8,64,128]{2,1,0:T(8,128)(2,1)S(1)}, u32[]{:S(2)}, u32[]{:S(2)}) collective-permute-start(bf16[8,64,128]{2,1,0:T(8,128)(2,1)S(1)} %get-tuple-element.30), channel_id=1, source_target_pairs={{0,1},{1,0},{2,3},{3,2},{4,5},{5,4},{6,7},{7,6},{8,9},{9,8},{10,11... | collective-permute-start | bytes 393224 | tf_op jit(solution)/shard_map/ppermute | solution.py:710
  6.1 6.4 %collective-permute-start.5 = (bf16[8,64,128]{2,1,0:T(8,128)(2,1)S(1)}, bf16[8,64,128]{2,1,0:T(8,128)(2,1)S(1)}, u32[]{:S(2)}, u32[]{:S(2)}) collective-permute-start(bf16[8,64,128]{2,1,0:T(8,128)(2,1)S(1)} %get-tuple-element.31), channel_id=1, source_target_pairs={{0,4},{1,2},{2,1},{3,7},{4,0},{5,6},{6,5},{7,3},{8,12},{9,10},{10,... | collective-permute-start | bytes 393224 | tf_op jit(solution)/shard_map/ppermute | solution.py:710
  7.7 4.8 %collective-permute-start.2 = (bf16[2,128,128]{2,1,0:T(8,128)(2,1)S(1)}, bf16[2,128,128]{2,1,0:T(8,128)(2,1)S(1)}, u32[]{:S(2)}, u32[]{:S(2)}) collective-permute-start(bf16[2,128,128]{2,1,0:T(8,128)(2,1)S(1)} %get-tuple-element.28), channel_id=1, source_target_pairs={{0,4},{1,5},{2,6},{3,7},{4,0},{5,1},{6,2},{7,3},{8,12},{9,13},{10,... | collective-permute-start | bytes 196616 | tf_op jit(solution)/shard_map/ppermute | solution.py:710
  8.1 4.3 %collective-permute-start.3 = (bf16[2,128,128]{2,1,0:T(8,128)(2,1)S(1)}, bf16[2,128,128]{2,1,0:T(8,128)(2,1)S(1)}, u32[]{:S(2)}, u32[]{:S(2)}) collective-permute-start(bf16[2,128,128]{2,1,0:T(8,128)(2,1)S(1)} %get-tuple-element.29), channel_id=1, source_target_pairs={{0,1},{1,0},{2,3},{3,2},{4,8},{5,9},{6,10},{7,11},{8,4},{9,5},{10,... | collective-permute-start | bytes 196616 | tf_op jit(solution)/shard_map/ppermute | solution.py:710
  14.1 13.7 %collective-permute-start.6 = (bf16[1536,128]{1,0:T(8,128)(2,1)S(1)}, bf16[1536,128]{1,0:T(8,128)(2,1)S(1)}, u32[]{:S(2)}, u32[]{:S(2)}) collective-permute-start(bf16[1536,128]{1,0:T(8,128)(2,1)S(1)} %get-tuple-element.32), channel_id=1, source_target_pairs={{0,16},{16,0},{1,17},{17,1},{2,18},{18,2},{3,19},{19,3},{4,20},{20... | collective-permute-start | bytes 1179656 | tf_op jit(solution)/shard_map/ppermute | solution.py:740
  20.7 10.5 %collective-permute-start.1 = (bf16[768,128]{1,0:T(8,128)(2,1)S(1)}, bf16[768,128]{1,0:T(8,128)(2,1)S(1)}, u32[]{:S(2)}, u32[]{:S(2)}) collective-permute-start(bf16[768,128]{1,0:T(8,128)(2,1)S(1)} %get-tuple-element.27), channel_id=1, source_target_pairs={{0,16},{16,0},{1,17},{17,1},{2,18},{18,2},{3,19},{19,3},{4,20},{20... | collective-permute-start | bytes 589832 | tf_op jit(solution)/shard_map/ppermute | solution.py:742

commit v8 on v7

--- a/solution.py
+++ b/solution.py
@@ -199,8 +199,8 @@
     return part[:, :h], part[:, h:]
 
 
-def places(route_ref, where_ref, table_ref, dims, blocks):
-    aggregates, cap, rows = dims
+def make_table(table_ref, dims):
+    _, cap, rows = dims
     me = lax.axis_index("gx")
     lines = rows // cap
     rest = cap % SUB
@@ -219,6 +219,11 @@
             one = (h, h + half // 2, h, h)
         for k in range(4):
             table_ref[k, c] = jnp.where(at_zero, zero[k], one[k])
+
+
+def places(route_ref, where_ref, table_ref, dims, blocks):
+    aggregates, _, rows = dims
+    me = lax.axis_index("gx")
     sent, kept = jnp.int32(0), jnp.int32(0)
     for i in range(aggregates):
         away = route_ref[0, i] != me
@@ -276,24 +281,28 @@
     copies = [
         pltpu.make_async_copy(one, two, sems.at[k])
         for k, (one, two) in enumerate((
-            (p_hbm, p_ref), (route_hbm, route_ref), (pair_hbm, pair_ref), (a_hbm, a_ref),
+            (p_hbm, p_ref), (route_hbm, route_ref), (pair_hbm, pair_ref),
         ))
     ]
+    blocks = [
+        pltpu.make_async_copy(a_hbm.at[x], a_ref.at[x], sems.at[3 + x]) for x in range(nx)
+    ]
+    for copy in copies + blocks:
+        copy.start()
+    clean, spread = constants(blk)
+    masks = even_lanes(q)
+    first, second = even_rows(blk)
+    codes_ref[...] = jnp.full_like(codes_ref, -1.0)
+    make_table(table_ref, dims)
     for copy in copies:
-        copy.start()
-    for copy in copies[:3]:
         copy.wait()
     sent, _ = places(route_ref, where_ref, table_ref, dims, nb)
-    codes_ref[...] = jnp.full_like(codes_ref, -1.0)
     for i in range(aggregates):
         a, b, z, t = i // (py * nz * 2), (i // (nz * 2)) % py, (i // 2) % nz, i % 2
         code = (2 * (jnp.where(pair_ref[a, b, z] == 0, 2, 1) - t) + z).astype(jnp.float32)
         line = jnp.full((1, LANES), code, jnp.float32)
         codes_ref[pl.ds(where_ref[2, i], 1), :] = line
         codes_ref[pl.ds(where_ref[3, i], 1), :] = line
-    clean, spread = constants(blk)
-    masks = even_lanes(q)
-    first, second = even_rows(blk)
 
     pairs = [(x, b) for x in range(nx) for b in range(py)]
     both = {e: pair(p_ref[e[0], 2 * e[1]], p_ref[e[0], 2 * e[1] + 1]) for e in pairs}
@@ -305,7 +314,8 @@
 
     face = p_ref[jnp.where(lax.axis_index("gx") == 0, nx - 1, 0)]
     send_ref[nb * rows + 2 * SUB :] = face.reshape(ny * blk, LANES)
-    copies[3].wait()
+    for copy in blocks:
+        copy.wait()
 
     for x, y in [(x, y) for x in range(nx) for y in range(ny)]:
         here = a_ref.at[x, y]
@@ -412,6 +422,7 @@
     blk = part_ref.shape[3]
     q = blk // 2
     nb = 4
+    make_table(table_ref, dims)
     sent, kept = places(route_ref, where_ref, table_ref, dims, nb)
     line = iota((blk, LANES), 0) * 0
 
@@ -451,7 +462,7 @@
 
 def outer_x_kernel(
     dims, grid, route_ref, pair_ref, part_ref, zup_ref, zdn_ref, early_ref,
-    send_ref, keep_ref, total_ref, where_ref, table_ref,
+    send_one_ref, send_two_ref, keep_ref, total_ref, where_ref, table_ref,
 ):
     px, py, nz = grid
     _, _, rows = dims
@@ -459,6 +470,7 @@
     blk = part_ref.shape[3]
     q = blk // 2
     nb = 2
+    make_table(table_ref, dims)
     sent, kept = places(route_ref, where_ref, table_ref, dims, nb)
     above = iota((2 * blk, LANES), 0) * 0 + lax.axis_index("gx") > 0
     clean, _ = constants(blk)
@@ -486,8 +498,8 @@
         for i, block, got in made:
             put(total_ref, where_ref, i, block, rows, got)
 
-    for kind, (out, count) in enumerate(((send_ref, sent), (keep_ref, kept))):
-        finish(((out, nb),), total_ref, kind, dims, count)
+    finish(((send_one_ref, 1), (send_two_ref, 1)), total_ref, 0, dims, sent)
+    finish(((keep_ref, nb),), total_ref, 1, dims, kept)
 
 
 def of_element(pair_ref, grid, x, y, z):
@@ -506,7 +518,7 @@
     return early
 
 
-def placed_blocks(early, x_ref, yz_ref, code, rows, at, size, without_x=True):
+def placed_blocks(early, x_refs, yz_ref, code, rows, at, size, without_x=True):
     near_low, near_high = (code < 1.5)[None], (code > 3.5)[None]
     upper = ((code == 1.0) | (code == 3.0) | (code == 5.0))[None]
 
@@ -516,9 +528,11 @@
     if without_x:
         yield 0, early(0, at, size)
     for m in range(2):
+        if m not in x_refs and not without_x:
+            continue
         cross, y_out = early(1 + m, at, size), tiles(yz_ref, m)
-        if x_ref is not None:
-            x_out = tiles(x_ref, m)
+        if m in x_refs:
+            x_out = tiles(*x_refs[m])
             yield 1 + 5 * m, jnp.where(near_low, cross, x_out)
             yield 2 + 5 * m, jnp.where(near_low, x_out, jnp.where(near_high, y_out, cross))
         if without_x:
@@ -549,28 +563,30 @@
 
     copies = []
     code = twice(codes_ref[:SUB])
-    for k, value in placed_blocks(rounded(code), x_ref, yz_ref, code, rows, 0, full):
+    for k, value in placed_blocks(rounded(code), {0: (x_ref, 0), 1: (x_ref, 1)}, yz_ref, code, rows, 0, full):
         full_ref[k] = value.reshape(full, LANES)
         to = out_hbm.at[k, pl.ds(me * (2 * full), full), :]
         copies.append(pltpu.make_async_copy(full_ref.at[k], to, sem.at[k]))
         copies[-1].start()
     code = twice(codes_ref[SUB:])
-    for k, value in placed_blocks(rounded(code), x_ref, yz_ref, code, rows, full, rows - full):
+    for k, value in placed_blocks(rounded(code), {0: (x_ref, 0), 1: (x_ref, 1)}, yz_ref, code, rows, full, rows - full):
         half_ref[k] = value.reshape(rows - full, LANES)
     for copy in copies:
         copy.wait()
 
 
-def take_kernel(dims, with_x, early_ref, *refs):
+def take_kernel(dims, member, early_ref, yz_ref, *refs):
     late, (half_ref, _, out_hbm, full_ref, mixed_ref, sem) = refs[: -6], refs[-6:]
     cap, rows = dims
     full = (cap - cap % SUB) * (rows // cap)
     me = lax.axis_index("gx")
     codes = early_ref[5 * rows : 5 * rows + 2 * SUB]
-    x_ref, yz_ref = late if with_x else (None, late[0])
+    x_refs = {} if member is None else {member: (late[0], 0)}
     early = received(early_ref, rows)
     copies = []
-    for k, value in placed_blocks(early, x_ref, yz_ref, twice(codes[:SUB]), rows, 0, full, not with_x):
+    for k, value in placed_blocks(
+        early, x_refs, yz_ref, twice(codes[:SUB]), rows, 0, full, member is None
+    ):
         full_ref[k] = value.reshape(full, LANES)
         to = out_hbm.at[k, pl.ds((1 - me) * (2 * full), full), :]
         copies.append(pltpu.make_async_copy(full_ref.at[k], to, sem.at[0, k]))
@@ -578,7 +594,7 @@
     first_half = (iota((SUB, LANES), 0) < SUB // 2)[None]
     pick = first_half == (me == 0)
     for k, value in placed_blocks(
-        early, x_ref, yz_ref, twice(codes[SUB:]), rows, full, rows - full, not with_x
+        early, x_refs, yz_ref, twice(codes[SUB:]), rows, full, rows - full, member is None
     ):
         theirs = value.reshape(rows - full, LANES).astype(jnp.float32).reshape(-1, SUB, LANES)
         mine = half_ref[k].astype(jnp.float32).reshape(-1, SUB, LANES)
@@ -687,7 +703,7 @@
             pltpu.VMEM((4 * SUB, LANES), f32),
             pltpu.SMEM((4, aggregates), jnp.int32),
             pltpu.SMEM((4, capacity), jnp.int32),
-            pltpu.SemaphoreType.DMA((4,)),
+            pltpu.SemaphoreType.DMA((3 + nx,)),
         ],
         compiler_params=room,
         cost_estimate=cost,
@@ -721,12 +737,13 @@
     )(left, a_near)
     part = held(part)[0]
 
-    def outer(kernel, blocks, *arrays):
+    def outer(kernel, blocks, sends, *arrays):
         return pl.pallas_call(
             functools.partial(kernel, dims, grid),
-            out_shape=(near(blocks * rows, LANES),) * 2,
+            out_shape=(near(blocks // sends * rows, LANES),) * sends
+            + (near(blocks * rows, LANES),),
             in_specs=[SMEM, SMEM] + [VMEM] * (3 + len(arrays)),
-            out_specs=[VMEM] * 2,
+            out_specs=[VMEM] * (sends + 1),
             scratch_shapes=[
                 pltpu.VMEM((2 * blocks * rows, LANES), f32),
                 pltpu.SMEM((4, aggregates), jnp.int32),
@@ -736,10 +753,11 @@
             cost_estimate=cost,
         )(route_row, pairing, part, zup, zdn, *held(*arrays))
 
-    send_yz, keep_yz = outer(outer_yz_kernel, 4, *halos)
+    send_yz, keep_yz = outer(outer_yz_kernel, 4, 1, *halos)
     got_yz = lax.ppermute(send_yz, "gx", swap)
-    send_x, keep_x = outer(outer_x_kernel, 2, got_0)
-    got_x = lax.ppermute(send_x, "gx", swap)
+    send_one, send_two, keep_x = outer(outer_x_kernel, 2, 2, got_0)
+    got_one = lax.ppermute(send_one, "gx", swap)
+    got_two = lax.ppermute(send_two, "gx", swap)
 
     full = (capacity // SUB) * SUB * lines
     whole = 2 * rows
@@ -753,9 +771,9 @@
         cost_estimate=cost,
         name="place_kept",
     )(*held(total, keep_codes, keep_x, keep_yz))
-    for with_x, late in ((False, (got_yz,)), (True, (got_x, got_yz))):
+    for member, late in ((None, (got_yz,)), (0, (got_yz, got_one)), (1, (got_yz, got_two))):
         out = pl.pallas_call(
-            functools.partial(take_kernel, (capacity, rows), with_x),
+            functools.partial(take_kernel, (capacity, rows), member),
             out_shape=bf16(11, whole, LANES),
             in_specs=[VMEM] * (2 + len(late)) + [ANY],
             out_specs=ANY,
@@ -767,7 +785,6 @@
             ],
             compiler_params=room,
             cost_estimate=cost,
-            name="place_x" if with_x else "place_yz",
         )(*held(got_0, *late, half), out)
     out = out.reshape(11, whole // (SUB * lines), lines, SUB, LANES).transpose(1, 3, 0, 2, 4)
     return out.reshape(2 * capacity, 11, entries)

time: 32.3 us -> 33.1 us (1.025)
  Pallas kernels: 9.46 us -> 10.3 us
    pallas_call x2 -> x3, Pallas kernels: 2.11 us -> 2.95 us  [local(): pl.pallas_call(functools.partial(take_kernel, (capacity, rows), member),...]
    ppermute x1 -> x2, starting transfers between devices: 2.08 us -> 2.16 us  [the longest x1 2.08 us: local(): got_two = lax.ppermute(send_two, 'gx', swap)]
    ppermute x1 -> x2, waiting for transfers between devices: 2.24 us -> 2.24 us  [the longest x1 2.24 us: local(): got_one = lax.ppermute(send_one, 'gx', swap)]
  transfers between devices with their start and end apart: 7 -> 8, of which waited for: 4 -> 4; matrix products, arithmetic and copies ran while one was open for 0% -> 0% of each run, Pallas kernels for 17% -> 20%
where the time goes in v8:
time: 33.1 us; the launch traced here: 33 us
  waiting for transfers between devices  14.2 us (43%)
  Pallas kernels  10.3 us (31%)
  starting transfers between devices  8.38 us (25%)
    ppermute x1, waiting for transfers between devices, local(): got_0 = lax.ppermute(send_0, 'gx', swap)  5.13 us
    ppermute x1, waiting for transfers between devices, local(): got_yz = lax.ppermute(send_yz, 'gx', swap)  3.99 us
    ppermute x4, starting transfers between devices, local(): halos.append(lax.ppermute(value, ('gy', 'gz'), rounds[name]))  3.06 us
    ppermute x1, starting transfers between devices, local(): got_0 = lax.ppermute(send_0, 'gx', swap)  3 us
    pallas_call x3, Pallas kernels, local(): pl.pallas_call(functools.partial(take_kernel, (capacity, rows), member),...  2.95 us
    pallas_call x2, Pallas kernels, outer(): pl.pallas_call(functools.partial(kernel, dims, grid), out_shape=(near(blo...  2.87 us
    ppermute x4, waiting for transfers between devices, local(): halos.append(lax.ppermute(value, ('gy', 'gz'), rounds[name]))  2.87 us
    pallas_call x1, Pallas kernels, local(): pl.pallas_call(functools.partial(inner_kernel, dims, grid), out_shape=(ne...  2.79 us
  transfers between devices with their start and end apart: 8, of which 4 were waited for; matrix products, arithmetic and copies ran while one was open for 0% of the time, Pallas kernels for 20%

profile of v8, /device:TPU:0, one launch (start us, length us, event | category | flops | bytes accessed | tf_op | source)
XLA Modules:
  0.0 33.0 jit_solution(13096792845939597439)
XLA Ops:
  0.0 2.8 %inner_blocks.1 = (bf16[2192,128]{1,0:T(8,128)(2,1)S(1)}, f32[3840,128]{1,0:T(8,128)S(1)}, bf16[16,128]{1,0:T(8,128)(2,1)S(1)}, bf16[8,64,128]{2,1,0:T(8,128)(2,...) custom-call(s32[1,16]{1,0:T(1,128)} %bitcast.18, ...), custom_call_target="tpu_custom_call" | custom-call | flops 1000000000 | bytes 4000000 | tf_op jit(solution)/shard_map/inner_blocks/pallas_call | solution.py:685
  2.8 3.0 %collective-permute-start = (bf16[2192,128]{1,0:T(8,128)(2,1)S(1)}, bf16[2192,128]{1,0:T(8,128)(2,1)S(1)}, u32[]{:S(2)}, u32[]{:S(2)}) collective-permute-start(bf16[2192,128]{1,0:T(8,128)(2,1)S(1)} %get-tuple-element.23), channel_id=1, source_target_pairs={{0,16},{16,0},{1,17},{17,1},{2,18},{18,2},{3,19},{19,3},{4,20},{20... | collective-permute-start | bytes 1683464 | tf_op jit(solution)/shard_map/ppermute | solution.py:712
  5.8 0.1 faces.1
  5.9 0.0 copy-start
  5.9 0.0 copy-start.1
  5.9 0.1 collective-permute-start.3
  6.0 1.6 %collective-permute-start.4 = (bf16[8,64,128]{2,1,0:T(8,128)(2,1)S(1)}, bf16[8,64,128]{2,1,0:T(8,128)(2,1)S(1)}, u32[]{:S(2)}, u32[]{:S(2)}) collective-permute-start(bf16[8,64,128]{2,1,0:T(8,128)(2,1)S(1)} %get-tuple-element.31), channel_id=1, source_target_pairs={{0,4},{1,2},{2,1},{3,7},{4,0},{5,6},{6,5},{7,3},{8,12},{9,10},{10,... | collective-permute-start | bytes 393224 | tf_op jit(solution)/shard_map/ppermute | solution.py:726
  7.6 0.5 %collective-permute-start.1 = (bf16[2,128,128]{2,1,0:T(8,128)(2,1)S(1)}, bf16[2,128,128]{2,1,0:T(8,128)(2,1)S(1)}, u32[]{:S(2)}, u32[]{:S(2)}) collective-permute-start(bf16[2,128,128]{2,1,0:T(8,128)(2,1)S(1)} %get-tuple-element.28), channel_id=1, source_target_pairs={{0,4},{1,5},{2,6},{3,7},{4,0},{5,1},{6,2},{7,3},{8,12},{9,13},{10,... | collective-permute-start | bytes 196616 | tf_op jit(solution)/shard_map/ppermute | solution.py:726
  8.1 0.9 %collective-permute-start.2 = (bf16[2,128,128]{2,1,0:T(8,128)(2,1)S(1)}, bf16[2,128,128]{2,1,0:T(8,128)(2,1)S(1)}, u32[]{:S(2)}, u32[]{:S(2)}) collective-permute-start(bf16[2,128,128]{2,1,0:T(8,128)(2,1)S(1)} %get-tuple-element.29), channel_id=1, source_target_pairs={{0,1},{1,0},{2,3},{3,2},{4,8},{5,9},{6,10},{7,11},{8,4},{9,5},{10,... | collective-permute-start | bytes 196616 | tf_op jit(solution)/shard_map/ppermute | solution.py:726
  9.0 0.6 %outer_left.1.part_ref = bf16[4,4,3,64,128]{4,3,2,1,0:T(8,128)(2,1)S(1)} custom-call(bf16[8,128,128]{2,1,0:T(8,128)(2,1)S(1)} %get-tuple-element.24.left_ref, bf16[4,4,7,64,128]{4,3,2,1,0:T(8,128)(2,1)S(1)} %get-tuple-element.25.a_ref), custom_call_target="tpu_custom_call" | custom-call | flops 1000000000 | bytes 4000000 | tf_op jit(solution)/shard_map/outer_left/pallas_call | solution.py:729
  9.6 2.9 %collective-permute-done.1.ya_ref = bf16[2,128,128]{2,1,0:T(8,128)(2,1)S(1)} collective-permute-done((bf16[2,128,128]{2,1,0:T(8,128)(2,1)S(1)}, bf16[2,128,128]{2,1,0:T(8,128)(2,1)S(1)}, u32[]{:S(2)}, u32[]{:S(2)}) %collective-permute-start.1) | collective-permute-done | bytes 65568 | tf_op jit(solution)/shard_map/ppermute | solution.py:726
  12.4 0.0 collective-permute-done.2.yb_ref
  12.4 0.0 collective-permute-done.3.za_ref
  12.5 0.0 collective-permute-done.4.zb_ref
  12.5 0.0 copy-done
  12.5 0.0 copy-done.1
  12.5 1.6 %shard_map.46 = (bf16[1536,128]{1,0:T(8,128)(2,1)S(1)}, bf16[1536,128]{1,0:T(8,128)(2,1)S(1)}) custom-call(s32[1,16]{1,0:T(1,128)S(1)} %bitcast.19, s32[2,2,2]{2,1,0:T(2,128)S(1)} %copy-done, bf16[4,4,3,64,128]{4,3,2,1,0:T(8,128)(2,1)S(1)} %outer_left.1.part_ref, bf16[8,64,128]{2,1,0:T(8,128)(2,1)S(1)} %get-tuple-element.26.zup_ref, ...), custom_call_target="tpu_custom_call" | custom-call | flops 1000000000 | bytes 4000000 | tf_op jit(solution)/shard_map/pallas_call | solution.py:741
  14.1 0.2 collective-permute-start.5
  14.2 5.1 %collective-permute-done.early_ref = bf16[2192,128]{1,0:T(8,128)(2,1)S(1)} collective-permute-done((bf16[2192,128]{1,0:T(8,128)(2,1)S(1)}, bf16[2192,128]{1,0:T(8,128)(2,1)S(1)}, u32[]{:S(2)}, u32[]{:S(2)}) %collective-permute-start) | collective-permute-done | bytes 561184 | tf_op jit(solution)/shard_map/ppermute | solution.py:712
  19.4 1.3 %shard_map.47 = (bf16[384,128]{1,0:T(8,128)(2,1)S(1)}, bf16[384,128]{1,0:T(8,128)(2,1)S(1)}, bf16[768,128]{1,0:T(8,128)(2,1)S(1)}) custom-call(s32[1,16]{1,0:T(1,128)S(1)} %bitcast.20, s32[2,2,2]{2,1,0:T(2,128)S(1)} %copy-done, bf16[4,4,3,64,128]{4,3,2,1,0:T(8,128)(2,1)S(1)} %outer_left.1.part_ref, bf16[8,64,128]{2,1,0:T(8,128)(2,1)S(1)} %get-tuple-element.26.zup_ref, ...), custom_call_target="tpu_custom_call" | custom-call | flops 1000000000 | bytes 4000000 | tf_op jit(solution)/shard_map/pallas_call | solution.py:741
  20.7 2.1 %collective-permute-start.6 = (bf16[384,128]{1,0:T(8,128)(2,1)S(1)}, bf16[384,128]{1,0:T(8,128)(2,1)S(1)}, u32[]{:S(2)}, u32[]{:S(2)}) collective-permute-start(bf16[384,128]{1,0:T(8,128)(2,1)S(1)} %get-tuple-element.33), channel_id=1, source_target_pairs={{0,16},{16,0},{1,17},{17,1},{2,18},{18,2},{3,19},{19,3},{4,20},{20... | collective-permute-start | bytes 294920 | tf_op jit(solution)/shard_map/ppermute | solution.py:760
  22.7 0.1 collective-permute-start.7
  22.8 1.0 %place_kept.1 = (bf16[11,128,128]{2,1,0:T(8,128)(2,1)S(1)}, bf16[11,768,128]{2,1,0:T(8,128)(2,1)}) custom-call(f32[3840,128]{1,0:T(8,128)S(1)} %get-tuple-element.34.total_ref, bf16[16,128]{1,0:T(8,128)(2,1)S(1)} %get-tuple-element.35.codes_ref, bf16[768,128]{1,0:T(8,128)(2,1)S(1)} %get-tuple-element.36.x_ref, bf16[1536,128]{1,0:T(8,128)(2,1)S(1)} %get-tuple-element.37.yz_ref), custom_call_target="tpu_custom_call" | custom-call | flops 1000000000 | bytes 4000000 | tf_op jit(solution)/shard_map/place_kept/pallas_call | solution.py:764
  23.8 4.0 %collective-permute-done.5.yz_ref = bf16[1536,128]{1,0:T(8,128)(2,1)S(1)} collective-permute-done((bf16[1536,128]{1,0:T(8,128)(2,1)S(1)}, bf16[1536,128]{1,0:T(8,128)(2,1)S(1)}, u32[]{:S(2)}, u32[]{:S(2)}) %collective-permute-start.5) | collective-permute-done | bytes 393248 | tf_op jit(solution)/shard_map/ppermute | solution.py:757
  27.8 1.1 %shard_map.48.refs_2_ = bf16[11,768,128]{2,1,0:T(8,128)(2,1)} custom-call(bf16[2192,128]{1,0:T(8,128)(2,1)S(1)} %collective-permute-done.early_ref, bf16[1536,128]{1,0:T(8,128)(2,1)S(1)} %collective-permute-done.5.yz_ref, bf16[11,128,128]{2,1,0:T(8,128)(2,1)S(1)} %get-tuple-element.38.refs_0_.refs_1_, ...), custom_call_target="tpu_custom_call", output_to_operand_aliasing={{}: (3, {})} | custom-call | flops 1000000000 | bytes 4000000 | tf_op jit(solution)/shard_map/pallas_call | solution.py:775
  28.9 2.2 %collective-permute-done.7.refs_0_ = bf16[384,128]{1,0:T(8,128)(2,1)S(1)} collective-permute-done((bf16[384,128]{1,0:T(8,128)(2,1)S(1)}, bf16[384,128]{1,0:T(8,128)(2,1)S(1)}, u32[]{:S(2)}, u32[]{:S(2)}) %collective-permute-start.7) | collective-permute-done | bytes 98336 | tf_op jit(solution)/shard_map/ppermute | solution.py:759
  31.1 0.9 %shard_map.49.refs_2_ = bf16[11,768,128]{2,1,0:T(8,128)(2,1)} custom-call(bf16[2192,128]{1,0:T(8,128)(2,1)S(1)} %collective-permute-done.early_ref, bf16[1536,128]{1,0:T(8,128)(2,1)S(1)} %collective-permute-done.5.yz_ref, bf16[384,128]{1,0:T(8,128)(2,1)S(1)} %collective-permute-done.7.refs_0_, ...), custom_call_target="tpu_custom_call", output_to_operand_aliasing={{}: (4, {})} | custom-call | flops 1000000000 | bytes 4000000 | tf_op jit(solution)/shard_map/pallas_call | solution.py:775
  32.1 0.0 collective-permute-done.6.refs_0_
  32.1 0.9 %shard_map.50 = bf16[11,768,128]{2,1,0:T(8,128)(2,1)} custom-call(bf16[2192,128]{1,0:T(8,128)(2,1)S(1)} %collective-permute-done.early_ref, bf16[1536,128]{1,0:T(8,128)(2,1)S(1)} %collective-permute-done.5.yz_ref, bf16[384,128]{1,0:T(8,128)(2,1)S(1)} %collective-permute-done.6.refs_0_, ...), custom_call_target="tpu_custom_call", output_to_operand_aliasing={{}: (4, {})} | custom-call | flops 1000000000 | bytes 4000000 | tf_op jit(solution)/shard_map/pallas_call | solution.py:775
Async XLA Ops:
  2.8 16.6 %collective-permute-start = (bf16[2192,128]{1,0:T(8,128)(2,1)S(1)}, bf16[2192,128]{1,0:T(8,128)(2,1)S(1)}, u32[]{:S(2)}, u32[]{:S(2)}) collective-permute-start(bf16[2192,128]{1,0:T(8,128)(2,1)S(1)} %get-tuple-element.23), channel_id=1, source_target_pairs={{0,16},{16,0},{1,17},{17,1},{2,18},{18,2},{3,19},{19,3},{4,20},{20... | collective-permute-start | bytes 1683464 | tf_op jit(solution)/shard_map/ppermute | solution.py:712
  5.9 6.6 %copy-start = (s32[2,2,2]{2,1,0:T(2,128)S(1)}, s32[2,2,2]{2,1,0:T(2,128)}, u32[]{:S(2)}) copy-start(s32[2,2,2]{2,1,0:T(2,128)} %pair_ref.3) | copy-start | bytes 100
  5.9 6.6 %copy-start.1 = (s32[16,1]{0,1:T(1,128)S(1)}, s32[16,1]{0,1:T(1,128)}, u32[]{:S(2)}) copy-start(s32[16,1]{0,1:T(1,128)} %param.7) | copy-start | bytes 196
  5.9 6.5 %collective-permute-start.3 = (bf16[8,64,128]{2,1,0:T(8,128)(2,1)S(1)}, bf16[8,64,128]{2,1,0:T(8,128)(2,1)S(1)}, u32[]{:S(2)}, u32[]{:S(2)}) collective-permute-start(bf16[8,64,128]{2,1,0:T(8,128)(2,1)S(1)} %get-tuple-element.30), channel_id=1, source_target_pairs={{0,1},{1,0},{2,3},{3,2},{4,5},{5,4},{6,7},{7,6},{8,9},{9,8},{10,11... | collective-permute-start | bytes 393224 | tf_op jit(solution)/shard_map/ppermute | solution.py:726
  6.0 6.4 %collective-permute-start.4 = (bf16[8,64,128]{2,1,0:T(8,128)(2,1)S(1)}, bf16[8,64,128]{2,1,0:T(8,128)(2,1)S(1)}, u32[]{:S(2)}, u32[]{:S(2)}) collective-permute-start(bf16[8,64,128]{2,1,0:T(8,128)(2,1)S(1)} %get-tuple-element.31), channel_id=1, source_target_pairs={{0,4},{1,2},{2,1},{3,7},{4,0},{5,6},{6,5},{7,3},{8,12},{9,10},{10,... | collective-permute-start | bytes 393224 | tf_op jit(solution)/shard_map/ppermute | solution.py:726
  7.6 4.8 %collective-permute-start.1 = (bf16[2,128,128]{2,1,0:T(8,128)(2,1)S(1)}, bf16[2,128,128]{2,1,0:T(8,128)(2,1)S(1)}, u32[]{:S(2)}, u32[]{:S(2)}) collective-permute-start(bf16[2,128,128]{2,1,0:T(8,128)(2,1)S(1)} %get-tuple-element.28), channel_id=1, source_target_pairs={{0,4},{1,5},{2,6},{3,7},{4,0},{5,1},{6,2},{7,3},{8,12},{9,13},{10,... | collective-permute-start | bytes 196616 | tf_op jit(solution)/shard_map/ppermute | solution.py:726
  8.1 4.3 %collective-permute-start.2 = (bf16[2,128,128]{2,1,0:T(8,128)(2,1)S(1)}, bf16[2,128,128]{2,1,0:T(8,128)(2,1)S(1)}, u32[]{:S(2)}, u32[]{:S(2)}) collective-permute-start(bf16[2,128,128]{2,1,0:T(8,128)(2,1)S(1)} %get-tuple-element.29), channel_id=1, source_target_pairs={{0,1},{1,0},{2,3},{3,2},{4,8},{5,9},{6,10},{7,11},{8,4},{9,5},{10,... | collective-permute-start | bytes 196616 | tf_op jit(solution)/shard_map/ppermute | solution.py:726
  14.1 13.7 %collective-permute-start.5 = (bf16[1536,128]{1,0:T(8,128)(2,1)S(1)}, bf16[1536,128]{1,0:T(8,128)(2,1)S(1)}, u32[]{:S(2)}, u32[]{:S(2)}) collective-permute-start(bf16[1536,128]{1,0:T(8,128)(2,1)S(1)} %get-tuple-element.32), channel_id=1, source_target_pairs={{0,16},{16,0},{1,17},{17,1},{2,18},{18,2},{3,19},{19,3},{4,20},{20... | collective-permute-start | bytes 1179656 | tf_op jit(solution)/shard_map/ppermute | solution.py:757
  20.7 11.4 %collective-permute-start.6 = (bf16[384,128]{1,0:T(8,128)(2,1)S(1)}, bf16[384,128]{1,0:T(8,128)(2,1)S(1)}, u32[]{:S(2)}, u32[]{:S(2)}) collective-permute-start(bf16[384,128]{1,0:T(8,128)(2,1)S(1)} %get-tuple-element.33), channel_id=1, source_target_pairs={{0,16},{16,0},{1,17},{17,1},{2,18},{18,2},{3,19},{19,3},{4,20},{20... | collective-permute-start | bytes 294920 | tf_op jit(solution)/shard_map/ppermute | solution.py:760
  22.7 8.4 %collective-permute-start.7 = (bf16[384,128]{1,0:T(8,128)(2,1)S(1)}, bf16[384,128]{1,0:T(8,128)(2,1)S(1)}, u32[]{:S(2)}, u32[]{:S(2)}) collective-permute-start(bf16[384,128]{1,0:T(8,128)(2,1)S(1)} %get-tuple-element.39), channel_id=1, source_target_pairs={{0,16},{16,0},{1,17},{17,1},{2,18},{18,2},{3,19},{19,3},{4,20},{20... | collective-permute-start | bytes 294920 | tf_op jit(solution)/shard_map/ppermute | solution.py:759

commit v9 on v7

--- a/solution.py
+++ b/solution.py
@@ -199,8 +199,8 @@
     return part[:, :h], part[:, h:]
 
 
-def places(route_ref, where_ref, table_ref, dims, blocks):
-    aggregates, cap, rows = dims
+def make_table(table_ref, dims):
+    _, cap, rows = dims
     me = lax.axis_index("gx")
     lines = rows // cap
     rest = cap % SUB
@@ -219,6 +219,11 @@
             one = (h, h + half // 2, h, h)
         for k in range(4):
             table_ref[k, c] = jnp.where(at_zero, zero[k], one[k])
+
+
+def places(route_ref, where_ref, table_ref, dims, blocks):
+    aggregates, _, rows = dims
+    me = lax.axis_index("gx")
     sent, kept = jnp.int32(0), jnp.int32(0)
     for i in range(aggregates):
         away = route_ref[0, i] != me
@@ -276,25 +281,20 @@
     copies = [
         pltpu.make_async_copy(one, two, sems.at[k])
         for k, (one, two) in enumerate((
-            (p_hbm, p_ref), (route_hbm, route_ref), (pair_hbm, pair_ref), (a_hbm, a_ref),
+            (p_hbm, p_ref), (route_hbm, route_ref), (pair_hbm, pair_ref),
         ))
     ]
-    for copy in copies:
+    blocks = [
+        pltpu.make_async_copy(a_hbm.at[x], a_ref.at[x], sems.at[3 + x]) for x in range(nx)
+    ]
+    for copy in copies + blocks:
         copy.start()
-    for copy in copies[:3]:
-        copy.wait()
-    sent, _ = places(route_ref, where_ref, table_ref, dims, nb)
-    codes_ref[...] = jnp.full_like(codes_ref, -1.0)
-    for i in range(aggregates):
-        a, b, z, t = i // (py * nz * 2), (i // (nz * 2)) % py, (i // 2) % nz, i % 2
-        code = (2 * (jnp.where(pair_ref[a, b, z] == 0, 2, 1) - t) + z).astype(jnp.float32)
-        line = jnp.full((1, LANES), code, jnp.float32)
-        codes_ref[pl.ds(where_ref[2, i], 1), :] = line
-        codes_ref[pl.ds(where_ref[3, i], 1), :] = line
     clean, spread = constants(blk)
     masks = even_lanes(q)
     first, second = even_rows(blk)
-
+    codes_ref[...] = jnp.full_like(codes_ref, -1.0)
+    make_table(table_ref, dims)
+    copies[0].wait()
     pairs = [(x, b) for x in range(nx) for b in range(py)]
     both = {e: pair(p_ref[e[0], 2 * e[1]], p_ref[e[0], 2 * e[1] + 1]) for e in pairs}
     tidy = {e: dot(clean, both[e]).astype(jnp.bfloat16) for e in pairs}
@@ -305,7 +305,15 @@
 
     face = p_ref[jnp.where(lax.axis_index("gx") == 0, nx - 1, 0)]
     send_ref[nb * rows + 2 * SUB :] = face.reshape(ny * blk, LANES)
-    copies[3].wait()
+    for copy in copies[1:] + blocks:
+        copy.wait()
+    sent, _ = places(route_ref, where_ref, table_ref, dims, nb)
+    for i in range(aggregates):
+        a, b, z, t = i // (py * nz * 2), (i // (nz * 2)) % py, (i // 2) % nz, i % 2
+        code = (2 * (jnp.where(pair_ref[a, b, z] == 0, 2, 1) - t) + z).astype(jnp.float32)
+        line = jnp.full((1, LANES), code, jnp.float32)
+        codes_ref[pl.ds(where_ref[2, i], 1), :] = line
+        codes_ref[pl.ds(where_ref[3, i], 1), :] = line
 
     for x, y in [(x, y) for x in range(nx) for y in range(ny)]:
         here = a_ref.at[x, y]
@@ -412,6 +420,7 @@
     blk = part_ref.shape[3]
     q = blk // 2
     nb = 4
+    make_table(table_ref, dims)
     sent, kept = places(route_ref, where_ref, table_ref, dims, nb)
     line = iota((blk, LANES), 0) * 0
 
@@ -459,6 +468,7 @@
     blk = part_ref.shape[3]
     q = blk // 2
     nb = 2
+    make_table(table_ref, dims)
     sent, kept = places(route_ref, where_ref, table_ref, dims, nb)
     above = iota((2 * blk, LANES), 0) * 0 + lax.axis_index("gx") > 0
     clean, _ = constants(blk)
@@ -687,7 +697,7 @@
             pltpu.VMEM((4 * SUB, LANES), f32),
             pltpu.SMEM((4, aggregates), jnp.int32),
             pltpu.SMEM((4, capacity), jnp.int32),
-            pltpu.SemaphoreType.DMA((4,)),
+            pltpu.SemaphoreType.DMA((3 + nx,)),
         ],
         compiler_params=room,
         cost_estimate=cost,

time: 32.3 us -> 32.3 us (level)
  no operation moved by 1% of the time
where the time goes in v9:
time: 32.3 us; the launch traced here: 32.2 us
  waiting for transfers between devices  14.3 us (44%)
  Pallas kernels  9.43 us (29%)
  starting transfers between devices  8.31 us (26%)
    ppermute x1, waiting for transfers between devices, local(): got_0 = lax.ppermute(send_0, 'gx', swap)  5.12 us
    ppermute x1, waiting for transfers between devices, local(): got_yz = lax.ppermute(send_yz, 'gx', swap)  4.07 us
    ppermute x4, starting transfers between devices, local(): halos.append(lax.ppermute(value, ('gy', 'gz'), rounds[name]))  3.06 us
    ppermute x1, starting transfers between devices, local(): got_0 = lax.ppermute(send_0, 'gx', swap)  2.99 us
    pallas_call x2, Pallas kernels, outer(): pl.pallas_call(functools.partial(kernel, dims, grid), out_shape=(near(blo...  2.87 us
    ppermute x4, waiting for transfers between devices, local(): halos.append(lax.ppermute(value, ('gy', 'gz'), rounds[name]))  2.86 us
    pallas_call x1, Pallas kernels, local(): pl.pallas_call(functools.partial(inner_kernel, dims, grid), out_shape=(ne...  2.81 us
    ppermute x1, waiting for transfers between devices, local(): got_x = lax.ppermute(send_x, 'gx', swap)  2.24 us
  transfers between devices with their start and end apart: 7, of which 4 were waited for; matrix products, arithmetic and copies ran while one was open for 0% of the time, Pallas kernels for 17%

profile of v9, /device:TPU:0, one launch (start us, length us, event | category | flops | bytes accessed | tf_op | source)
XLA Modules:
  0.0 32.2 jit_solution(12437699979051066840)
XLA Ops:
  0.0 2.8 %inner_blocks.1 = (bf16[2192,128]{1,0:T(8,128)(2,1)S(1)}, f32[3840,128]{1,0:T(8,128)S(1)}, bf16[16,128]{1,0:T(8,128)(2,1)S(1)}, bf16[8,64,128]{2,1,0:T(8,128)(2,...) custom-call(s32[1,16]{1,0:T(1,128)} %bitcast.18, ...), custom_call_target="tpu_custom_call" | custom-call | flops 1000000000 | bytes 4000000 | tf_op jit(solution)/shard_map/inner_blocks/pallas_call | solution.py:679
  2.8 3.0 %collective-permute-start = (bf16[2192,128]{1,0:T(8,128)(2,1)S(1)}, bf16[2192,128]{1,0:T(8,128)(2,1)S(1)}, u32[]{:S(2)}, u32[]{:S(2)}) collective-permute-start(bf16[2192,128]{1,0:T(8,128)(2,1)S(1)} %get-tuple-element.22), channel_id=1, source_target_pairs={{0,16},{16,0},{1,17},{17,1},{2,18},{18,2},{3,19},{19,3},{4,20},{20... | collective-permute-start | bytes 1683464 | tf_op jit(solution)/shard_map/ppermute | solution.py:706
  5.8 0.1 faces.1
  5.9 0.0 copy-start
  5.9 0.0 copy-start.1
  5.9 0.1 collective-permute-start.4
  6.0 1.6 %collective-permute-start.5 = (bf16[8,64,128]{2,1,0:T(8,128)(2,1)S(1)}, bf16[8,64,128]{2,1,0:T(8,128)(2,1)S(1)}, u32[]{:S(2)}, u32[]{:S(2)}) collective-permute-start(bf16[8,64,128]{2,1,0:T(8,128)(2,1)S(1)} %get-tuple-element.31), channel_id=1, source_target_pairs={{0,4},{1,2},{2,1},{3,7},{4,0},{5,6},{6,5},{7,3},{8,12},{9,10},{10,... | collective-permute-start | bytes 393224 | tf_op jit(solution)/shard_map/ppermute | solution.py:720
  7.7 0.5 %collective-permute-start.2 = (bf16[2,128,128]{2,1,0:T(8,128)(2,1)S(1)}, bf16[2,128,128]{2,1,0:T(8,128)(2,1)S(1)}, u32[]{:S(2)}, u32[]{:S(2)}) collective-permute-start(bf16[2,128,128]{2,1,0:T(8,128)(2,1)S(1)} %get-tuple-element.28), channel_id=1, source_target_pairs={{0,4},{1,5},{2,6},{3,7},{4,0},{5,1},{6,2},{7,3},{8,12},{9,13},{10,... | collective-permute-start | bytes 196616 | tf_op jit(solution)/shard_map/ppermute | solution.py:720
  8.1 0.9 %collective-permute-start.3 = (bf16[2,128,128]{2,1,0:T(8,128)(2,1)S(1)}, bf16[2,128,128]{2,1,0:T(8,128)(2,1)S(1)}, u32[]{:S(2)}, u32[]{:S(2)}) collective-permute-start(bf16[2,128,128]{2,1,0:T(8,128)(2,1)S(1)} %get-tuple-element.29), channel_id=1, source_target_pairs={{0,1},{1,0},{2,3},{3,2},{4,8},{5,9},{6,10},{7,11},{8,4},{9,5},{10,... | collective-permute-start | bytes 196616 | tf_op jit(solution)/shard_map/ppermute | solution.py:720
  9.0 0.6 %outer_left.1.part_ref = bf16[4,4,3,64,128]{4,3,2,1,0:T(8,128)(2,1)S(1)} custom-call(bf16[8,128,128]{2,1,0:T(8,128)(2,1)S(1)} %get-tuple-element.23.left_ref, bf16[4,4,7,64,128]{4,3,2,1,0:T(8,128)(2,1)S(1)} %get-tuple-element.24.a_ref), custom_call_target="tpu_custom_call" | custom-call | flops 1000000000 | bytes 4000000 | tf_op jit(solution)/shard_map/outer_left/pallas_call | solution.py:723
  9.6 2.9 %collective-permute-done.2.ya_ref = bf16[2,128,128]{2,1,0:T(8,128)(2,1)S(1)} collective-permute-done((bf16[2,128,128]{2,1,0:T(8,128)(2,1)S(1)}, bf16[2,128,128]{2,1,0:T(8,128)(2,1)S(1)}, u32[]{:S(2)}, u32[]{:S(2)}) %collective-permute-start.2) | collective-permute-done | bytes 65568 | tf_op jit(solution)/shard_map/ppermute | solution.py:720
  12.5 0.0 collective-permute-done.3.yb_ref
  12.5 0.0 collective-permute-done.4.za_ref
  12.5 0.0 collective-permute-done.5.zb_ref
  12.5 0.0 copy-done
  12.5 0.0 copy-done.1
  12.5 1.6 %shard_map.47 = (bf16[1536,128]{1,0:T(8,128)(2,1)S(1)}, bf16[1536,128]{1,0:T(8,128)(2,1)S(1)}) custom-call(s32[1,16]{1,0:T(1,128)S(1)} %bitcast.19, s32[2,2,2]{2,1,0:T(2,128)S(1)} %copy-done, bf16[4,4,3,64,128]{4,3,2,1,0:T(8,128)(2,1)S(1)} %outer_left.1.part_ref, bf16[8,64,128]{2,1,0:T(8,128)(2,1)S(1)} %get-tuple-element.25.zup_ref, ...), custom_call_target="tpu_custom_call" | custom-call | flops 1000000000 | bytes 4000000 | tf_op jit(solution)/shard_map/pallas_call | solution.py:735
  14.1 0.2 collective-permute-start.6
  14.3 5.1 %collective-permute-done.early_ref = bf16[2192,128]{1,0:T(8,128)(2,1)S(1)} collective-permute-done((bf16[2192,128]{1,0:T(8,128)(2,1)S(1)}, bf16[2192,128]{1,0:T(8,128)(2,1)S(1)}, u32[]{:S(2)}, u32[]{:S(2)}) %collective-permute-start) | collective-permute-done | bytes 561184 | tf_op jit(solution)/shard_map/ppermute | solution.py:706
  19.4 1.3 %shard_map.46 = (bf16[768,128]{1,0:T(8,128)(2,1)S(1)}, bf16[768,128]{1,0:T(8,128)(2,1)S(1)}) custom-call(s32[1,16]{1,0:T(1,128)S(1)} %bitcast.20, s32[2,2,2]{2,1,0:T(2,128)S(1)} %copy-done, bf16[4,4,3,64,128]{4,3,2,1,0:T(8,128)(2,1)S(1)} %outer_left.1.part_ref, bf16[8,64,128]{2,1,0:T(8,128)(2,1)S(1)} %get-tuple-element.25.zup_ref, ...), custom_call_target="tpu_custom_call" | custom-call | flops 1000000000 | bytes 4000000 | tf_op jit(solution)/shard_map/pallas_call | solution.py:735
  20.7 2.1 %collective-permute-start.1 = (bf16[768,128]{1,0:T(8,128)(2,1)S(1)}, bf16[768,128]{1,0:T(8,128)(2,1)S(1)}, u32[]{:S(2)}, u32[]{:S(2)}) collective-permute-start(bf16[768,128]{1,0:T(8,128)(2,1)S(1)} %get-tuple-element.27), channel_id=1, source_target_pairs={{0,16},{16,0},{1,17},{17,1},{2,18},{18,2},{3,19},{19,3},{4,20},{20... | collective-permute-start | bytes 589832 | tf_op jit(solution)/shard_map/ppermute | solution.py:752
  22.8 1.0 %place_kept.1 = (bf16[11,128,128]{2,1,0:T(8,128)(2,1)S(1)}, bf16[11,768,128]{2,1,0:T(8,128)(2,1)}) custom-call(f32[3840,128]{1,0:T(8,128)S(1)} %get-tuple-element.33.total_ref, bf16[16,128]{1,0:T(8,128)(2,1)S(1)} %get-tuple-element.34.codes_ref, bf16[768,128]{1,0:T(8,128)(2,1)S(1)} %get-tuple-element.35.x_ref, bf16[1536,128]{1,0:T(8,128)(2,1)S(1)} %get-tuple-element.36.yz_ref), custom_call_target="tpu_custom_call" | custom-call | flops 1000000000 | bytes 4000000 | tf_op jit(solution)/shard_map/place_kept/pallas_call | solution.py:756
  23.7 4.1 %collective-permute-done.6.refs_0_.refs_1_ = bf16[1536,128]{1,0:T(8,128)(2,1)S(1)} collective-permute-done((bf16[1536,128]{1,0:T(8,128)(2,1)S(1)}, bf16[1536,128]{1,0:T(8,128)(2,1)S(1)}, u32[]{:S(2)}, u32[]{:S(2)}) %collective-permute-start.6) | collective-permute-done | bytes 393248 | tf_op jit(solution)/shard_map/ppermute | solution.py:750
  27.8 1.1 %place_yz.1.refs_3_ = bf16[11,768,128]{2,1,0:T(8,128)(2,1)} custom-call(bf16[2192,128]{1,0:T(8,128)(2,1)S(1)} %collective-permute-done.early_ref, bf16[1536,128]{1,0:T(8,128)(2,1)S(1)} %collective-permute-done.6.refs_0_.refs_1_, bf16[11,128,128]{2,1,0:T(8,128)(2,1)S(1)} %get-tuple-element.37.refs_1_.refs_2_, ...), custom_call_target="tpu_custom_call", output_to_operand_aliasing={{}: (3, {})} | custom-call | flops 1000000000 | bytes 4000000 | tf_op jit(solution)/shard_map/place_yz/pallas_call | solution.py:767
  28.9 2.2 %collective-permute-done.1.refs_0_ = bf16[768,128]{1,0:T(8,128)(2,1)S(1)} collective-permute-done((bf16[768,128]{1,0:T(8,128)(2,1)S(1)}, bf16[768,128]{1,0:T(8,128)(2,1)S(1)}, u32[]{:S(2)}, u32[]{:S(2)}) %collective-permute-start.1) | collective-permute-done | bytes 196640 | tf_op jit(solution)/shard_map/ppermute | solution.py:752
  31.2 1.0 %place_x.1 = bf16[11,768,128]{2,1,0:T(8,128)(2,1)} custom-call(bf16[2192,128]{1,0:T(8,128)(2,1)S(1)} %collective-permute-done.early_ref, bf16[768,128]{1,0:T(8,128)(2,1)S(1)} %collective-permute-done.1.refs_0_, bf16[1536,128]{1,0:T(8,128)(2,1)S(1)} %collective-permute-done.6.refs_0_.refs_1_, ...), custom_call_target="tpu_custom_call", output_to_operand_aliasing={{}: (4, {})} | custom-call | flops 1000000000 | bytes 4000000 | tf_op jit(solution)/shard_map/place_x/pallas_call | solution.py:767
Async XLA Ops:
  2.8 16.6 %collective-permute-start = (bf16[2192,128]{1,0:T(8,128)(2,1)S(1)}, bf16[2192,128]{1,0:T(8,128)(2,1)S(1)}, u32[]{:S(2)}, u32[]{:S(2)}) collective-permute-start(bf16[2192,128]{1,0:T(8,128)(2,1)S(1)} %get-tuple-element.22), channel_id=1, source_target_pairs={{0,16},{16,0},{1,17},{17,1},{2,18},{18,2},{3,19},{19,3},{4,20},{20... | collective-permute-start | bytes 1683464 | tf_op jit(solution)/shard_map/ppermute | solution.py:706
  5.9 6.6 %copy-start = (s32[2,2,2]{2,1,0:T(2,128)S(1)}, s32[2,2,2]{2,1,0:T(2,128)}, u32[]{:S(2)}) copy-start(s32[2,2,2]{2,1,0:T(2,128)} %pair_ref.3) | copy-start | bytes 100
  5.9 6.6 %copy-start.1 = (s32[16,1]{0,1:T(1,128)S(1)}, s32[16,1]{0,1:T(1,128)}, u32[]{:S(2)}) copy-start(s32[16,1]{0,1:T(1,128)} %param.7) | copy-start | bytes 196
  5.9 6.5 %collective-permute-start.4 = (bf16[8,64,128]{2,1,0:T(8,128)(2,1)S(1)}, bf16[8,64,128]{2,1,0:T(8,128)(2,1)S(1)}, u32[]{:S(2)}, u32[]{:S(2)}) collective-permute-start(bf16[8,64,128]{2,1,0:T(8,128)(2,1)S(1)} %get-tuple-element.30), channel_id=1, source_target_pairs={{0,1},{1,0},{2,3},{3,2},{4,5},{5,4},{6,7},{7,6},{8,9},{9,8},{10,11... | collective-permute-start | bytes 393224 | tf_op jit(solution)/shard_map/ppermute | solution.py:720
  6.0 6.4 %collective-permute-start.5 = (bf16[8,64,128]{2,1,0:T(8,128)(2,1)S(1)}, bf16[8,64,128]{2,1,0:T(8,128)(2,1)S(1)}, u32[]{:S(2)}, u32[]{:S(2)}) collective-permute-start(bf16[8,64,128]{2,1,0:T(8,128)(2,1)S(1)} %get-tuple-element.31), channel_id=1, source_target_pairs={{0,4},{1,2},{2,1},{3,7},{4,0},{5,6},{6,5},{7,3},{8,12},{9,10},{10,... | collective-permute-start | bytes 393224 | tf_op jit(solution)/shard_map/ppermute | solution.py:720
  7.7 4.8 %collective-permute-start.2 = (bf16[2,128,128]{2,1,0:T(8,128)(2,1)S(1)}, bf16[2,128,128]{2,1,0:T(8,128)(2,1)S(1)}, u32[]{:S(2)}, u32[]{:S(2)}) collective-permute-start(bf16[2,128,128]{2,1,0:T(8,128)(2,1)S(1)} %get-tuple-element.28), channel_id=1, source_target_pairs={{0,4},{1,5},{2,6},{3,7},{4,0},{5,1},{6,2},{7,3},{8,12},{9,13},{10,... | collective-permute-start | bytes 196616 | tf_op jit(solution)/shard_map/ppermute | solution.py:720
  8.1 4.3 %collective-permute-start.3 = (bf16[2,128,128]{2,1,0:T(8,128)(2,1)S(1)}, bf16[2,128,128]{2,1,0:T(8,128)(2,1)S(1)}, u32[]{:S(2)}, u32[]{:S(2)}) collective-permute-start(bf16[2,128,128]{2,1,0:T(8,128)(2,1)S(1)} %get-tuple-element.29), channel_id=1, source_target_pairs={{0,1},{1,0},{2,3},{3,2},{4,8},{5,9},{6,10},{7,11},{8,4},{9,5},{10,... | collective-permute-start | bytes 196616 | tf_op jit(solution)/shard_map/ppermute | solution.py:720
  14.1 13.7 %collective-permute-start.6 = (bf16[1536,128]{1,0:T(8,128)(2,1)S(1)}, bf16[1536,128]{1,0:T(8,128)(2,1)S(1)}, u32[]{:S(2)}, u32[]{:S(2)}) collective-permute-start(bf16[1536,128]{1,0:T(8,128)(2,1)S(1)} %get-tuple-element.32), channel_id=1, source_target_pairs={{0,16},{16,0},{1,17},{17,1},{2,18},{18,2},{3,19},{19,3},{4,20},{20... | collective-permute-start | bytes 1179656 | tf_op jit(solution)/shard_map/ppermute | solution.py:750
  20.7 10.5 %collective-permute-start.1 = (bf16[768,128]{1,0:T(8,128)(2,1)S(1)}, bf16[768,128]{1,0:T(8,128)(2,1)S(1)}, u32[]{:S(2)}, u32[]{:S(2)}) collective-permute-start(bf16[768,128]{1,0:T(8,128)(2,1)S(1)} %get-tuple-element.27), channel_id=1, source_target_pairs={{0,16},{16,0},{1,17},{17,1},{2,18},{18,2},{3,19},{19,3},{4,20},{20... | collective-permute-start | bytes 589832 | tf_op jit(solution)/shard_map/ppermute | solution.py:752

commit v10 on v9

--- a/solution.py
+++ b/solution.py
@@ -294,18 +294,7 @@
     first, second = even_rows(blk)
     codes_ref[...] = jnp.full_like(codes_ref, -1.0)
     make_table(table_ref, dims)
-    copies[0].wait()
-    pairs = [(x, b) for x in range(nx) for b in range(py)]
-    both = {e: pair(p_ref[e[0], 2 * e[1]], p_ref[e[0], 2 * e[1] + 1]) for e in pairs}
-    tidy = {e: dot(clean, both[e]).astype(jnp.bfloat16) for e in pairs}
-    for x, b in pairs:
-        left_ref[x * py + b] = transposed_dot(spread, both[x, b]).astype(jnp.bfloat16)
-        zdn_ref[x * py + b] = tidy[x, b][:blk]
-        zup_ref[x * py + b] = tidy[x, b][blk:]
-
-    face = p_ref[jnp.where(lax.axis_index("gx") == 0, nx - 1, 0)]
-    send_ref[nb * rows + 2 * SUB :] = face.reshape(ny * blk, LANES)
-    for copy in copies[1:] + blocks:
+    for copy in copies:
         copy.wait()
     sent, _ = places(route_ref, where_ref, table_ref, dims, nb)
     for i in range(aggregates):
@@ -315,7 +304,21 @@
         codes_ref[pl.ds(where_ref[2, i], 1), :] = line
         codes_ref[pl.ds(where_ref[3, i], 1), :] = line
 
+    pairs = [(x, b) for x in range(nx) for b in range(py)]
+    both = {e: pair(p_ref[e[0], 2 * e[1]], p_ref[e[0], 2 * e[1] + 1]) for e in pairs}
+    tidy = {e: dot(clean, both[e]).astype(jnp.bfloat16) for e in pairs}
+    for x, b in pairs:
+        left_ref[x * py + b] = transposed_dot(spread, both[x, b]).astype(jnp.bfloat16)
+        zdn_ref[x * py + b] = tidy[x, b][:blk]
+        zup_ref[x * py + b] = tidy[x, b][blk:]
+
+    face = p_ref[jnp.where(lax.axis_index("gx") == 0, nx - 1, 0)]
+    send_ref[nb * rows + 2 * SUB :] = face.reshape(ny * blk, LANES)
+
     for x, y in [(x, y) for x in range(nx) for y in range(ny)]:
+        if y == 0 and x % px == 0:
+            for copy in blocks[x : x + px]:
+                copy.wait()
         here = a_ref.at[x, y]
         along_z = here[6] * first + here[5] * second
         right = jnp.concatenate(

time: 32.3 us -> 32.4 us (level)
  no operation moved by 1% of the time
where the time goes in v10:
time: 32.4 us; the launch traced here: 32.3 us
  waiting for transfers between devices  14.3 us (44%)
  Pallas kernels  9.58 us (30%)
  starting transfers between devices  8.32 us (26%)
    ppermute x1, waiting for transfers between devices, local(): got_0 = lax.ppermute(send_0, 'gx', swap)  5.1 us
    ppermute x1, waiting for transfers between devices, local(): got_yz = lax.ppermute(send_yz, 'gx', swap)  4.07 us
    ppermute x4, starting transfers between devices, local(): halos.append(lax.ppermute(value, ('gy', 'gz'), rounds[name]))  3.06 us
    ppermute x1, starting transfers between devices, local(): got_0 = lax.ppermute(send_0, 'gx', swap)  2.98 us
    pallas_call x1, Pallas kernels, local(): pl.pallas_call(functools.partial(inner_kernel, dims, grid), out_shape=(ne...  2.95 us
    pallas_call x2, Pallas kernels, outer(): pl.pallas_call(functools.partial(kernel, dims, grid), out_shape=(near(blo...  2.87 us
    ppermute x4, waiting for transfers between devices, local(): halos.append(lax.ppermute(value, ('gy', 'gz'), rounds[name]))  2.86 us
    ppermute x1, waiting for transfers between devices, local(): got_x = lax.ppermute(send_x, 'gx', swap)  2.24 us
  transfers between devices with their start and end apart: 7, of which 4 were waited for; matrix products, arithmetic and copies ran while one was open for 0% of the time, Pallas kernels for 17%

profile of v10, /device:TPU:0, one launch (start us, length us, event | category | flops | bytes accessed | tf_op | source)
XLA Modules:
  0.0 32.3 jit_solution(1823152119716352977)
XLA Ops:
  0.0 2.9 %inner_blocks.1 = (bf16[2192,128]{1,0:T(8,128)(2,1)S(1)}, f32[3840,128]{1,0:T(8,128)S(1)}, bf16[16,128]{1,0:T(8,128)(2,1)S(1)}, bf16[8,64,128]{2,1,0:T(8,128)(2,...) custom-call(s32[1,16]{1,0:T(1,128)} %bitcast.18, ...), custom_call_target="tpu_custom_call" | custom-call | flops 1000000000 | bytes 4000000 | tf_op jit(solution)/shard_map/inner_blocks/pallas_call | solution.py:682
  3.0 3.0 %collective-permute-start = (bf16[2192,128]{1,0:T(8,128)(2,1)S(1)}, bf16[2192,128]{1,0:T(8,128)(2,1)S(1)}, u32[]{:S(2)}, u32[]{:S(2)}) collective-permute-start(bf16[2192,128]{1,0:T(8,128)(2,1)S(1)} %get-tuple-element.22), channel_id=1, source_target_pairs={{0,16},{16,0},{1,17},{17,1},{2,18},{18,2},{3,19},{19,3},{4,20},{20... | collective-permute-start | bytes 1683464 | tf_op jit(solution)/shard_map/ppermute | solution.py:709
  5.9 0.1 faces.1
  6.0 0.0 copy-start
  6.1 0.0 copy-start.1
  6.1 0.1 collective-permute-start.4
  6.1 1.6 %collective-permute-start.5 = (bf16[8,64,128]{2,1,0:T(8,128)(2,1)S(1)}, bf16[8,64,128]{2,1,0:T(8,128)(2,1)S(1)}, u32[]{:S(2)}, u32[]{:S(2)}) collective-permute-start(bf16[8,64,128]{2,1,0:T(8,128)(2,1)S(1)} %get-tuple-element.31), channel_id=1, source_target_pairs={{0,4},{1,2},{2,1},{3,7},{4,0},{5,6},{6,5},{7,3},{8,12},{9,10},{10,... | collective-permute-start | bytes 393224 | tf_op jit(solution)/shard_map/ppermute | solution.py:723
  7.8 0.5 %collective-permute-start.2 = (bf16[2,128,128]{2,1,0:T(8,128)(2,1)S(1)}, bf16[2,128,128]{2,1,0:T(8,128)(2,1)S(1)}, u32[]{:S(2)}, u32[]{:S(2)}) collective-permute-start(bf16[2,128,128]{2,1,0:T(8,128)(2,1)S(1)} %get-tuple-element.28), channel_id=1, source_target_pairs={{0,4},{1,5},{2,6},{3,7},{4,0},{5,1},{6,2},{7,3},{8,12},{9,13},{10,... | collective-permute-start | bytes 196616 | tf_op jit(solution)/shard_map/ppermute | solution.py:723
  8.2 0.9 %collective-permute-start.3 = (bf16[2,128,128]{2,1,0:T(8,128)(2,1)S(1)}, bf16[2,128,128]{2,1,0:T(8,128)(2,1)S(1)}, u32[]{:S(2)}, u32[]{:S(2)}) collective-permute-start(bf16[2,128,128]{2,1,0:T(8,128)(2,1)S(1)} %get-tuple-element.29), channel_id=1, source_target_pairs={{0,1},{1,0},{2,3},{3,2},{4,8},{5,9},{6,10},{7,11},{8,4},{9,5},{10,... | collective-permute-start | bytes 196616 | tf_op jit(solution)/shard_map/ppermute | solution.py:723
  9.1 0.6 %outer_left.1.part_ref = bf16[4,4,3,64,128]{4,3,2,1,0:T(8,128)(2,1)S(1)} custom-call(bf16[8,128,128]{2,1,0:T(8,128)(2,1)S(1)} %get-tuple-element.23.left_ref, bf16[4,4,7,64,128]{4,3,2,1,0:T(8,128)(2,1)S(1)} %get-tuple-element.24.a_ref), custom_call_target="tpu_custom_call" | custom-call | flops 1000000000 | bytes 4000000 | tf_op jit(solution)/shard_map/outer_left/pallas_call | solution.py:726
  9.7 2.9 %collective-permute-done.2.ya_ref = bf16[2,128,128]{2,1,0:T(8,128)(2,1)S(1)} collective-permute-done((bf16[2,128,128]{2,1,0:T(8,128)(2,1)S(1)}, bf16[2,128,128]{2,1,0:T(8,128)(2,1)S(1)}, u32[]{:S(2)}, u32[]{:S(2)}) %collective-permute-start.2) | collective-permute-done | bytes 65568 | tf_op jit(solution)/shard_map/ppermute | solution.py:723
  12.6 0.0 collective-permute-done.3.yb_ref
  12.6 0.0 collective-permute-done.4.za_ref
  12.6 0.0 collective-permute-done.5.zb_ref
  12.6 0.0 copy-done
  12.6 0.0 copy-done.1
  12.6 1.6 %shard_map.47 = (bf16[1536,128]{1,0:T(8,128)(2,1)S(1)}, bf16[1536,128]{1,0:T(8,128)(2,1)S(1)}) custom-call(s32[1,16]{1,0:T(1,128)S(1)} %bitcast.19, s32[2,2,2]{2,1,0:T(2,128)S(1)} %copy-done, bf16[4,4,3,64,128]{4,3,2,1,0:T(8,128)(2,1)S(1)} %outer_left.1.part_ref, bf16[8,64,128]{2,1,0:T(8,128)(2,1)S(1)} %get-tuple-element.25.zup_ref, ...), custom_call_target="tpu_custom_call" | custom-call | flops 1000000000 | bytes 4000000 | tf_op jit(solution)/shard_map/pallas_call | solution.py:738
  14.2 0.2 collective-permute-start.6
  14.4 5.1 %collective-permute-done.early_ref = bf16[2192,128]{1,0:T(8,128)(2,1)S(1)} collective-permute-done((bf16[2192,128]{1,0:T(8,128)(2,1)S(1)}, bf16[2192,128]{1,0:T(8,128)(2,1)S(1)}, u32[]{:S(2)}, u32[]{:S(2)}) %collective-permute-start) | collective-permute-done | bytes 561184 | tf_op jit(solution)/shard_map/ppermute | solution.py:709
  19.5 1.3 %shard_map.46 = (bf16[768,128]{1,0:T(8,128)(2,1)S(1)}, bf16[768,128]{1,0:T(8,128)(2,1)S(1)}) custom-call(s32[1,16]{1,0:T(1,128)S(1)} %bitcast.20, s32[2,2,2]{2,1,0:T(2,128)S(1)} %copy-done, bf16[4,4,3,64,128]{4,3,2,1,0:T(8,128)(2,1)S(1)} %outer_left.1.part_ref, bf16[8,64,128]{2,1,0:T(8,128)(2,1)S(1)} %get-tuple-element.25.zup_ref, ...), custom_call_target="tpu_custom_call" | custom-call | flops 1000000000 | bytes 4000000 | tf_op jit(solution)/shard_map/pallas_call | solution.py:738
  20.8 2.1 %collective-permute-start.1 = (bf16[768,128]{1,0:T(8,128)(2,1)S(1)}, bf16[768,128]{1,0:T(8,128)(2,1)S(1)}, u32[]{:S(2)}, u32[]{:S(2)}) collective-permute-start(bf16[768,128]{1,0:T(8,128)(2,1)S(1)} %get-tuple-element.27), channel_id=1, source_target_pairs={{0,16},{16,0},{1,17},{17,1},{2,18},{18,2},{3,19},{19,3},{4,20},{20... | collective-permute-start | bytes 589832 | tf_op jit(solution)/shard_map/ppermute | solution.py:755
  22.9 1.0 %place_kept.1 = (bf16[11,128,128]{2,1,0:T(8,128)(2,1)S(1)}, bf16[11,768,128]{2,1,0:T(8,128)(2,1)}) custom-call(f32[3840,128]{1,0:T(8,128)S(1)} %get-tuple-element.33.total_ref, bf16[16,128]{1,0:T(8,128)(2,1)S(1)} %get-tuple-element.34.codes_ref, bf16[768,128]{1,0:T(8,128)(2,1)S(1)} %get-tuple-element.35.x_ref, bf16[1536,128]{1,0:T(8,128)(2,1)S(1)} %get-tuple-element.36.yz_ref), custom_call_target="tpu_custom_call" | custom-call | flops 1000000000 | bytes 4000000 | tf_op jit(solution)/shard_map/place_kept/pallas_call | solution.py:759
  23.8 4.1 %collective-permute-done.6.refs_0_.refs_1_ = bf16[1536,128]{1,0:T(8,128)(2,1)S(1)} collective-permute-done((bf16[1536,128]{1,0:T(8,128)(2,1)S(1)}, bf16[1536,128]{1,0:T(8,128)(2,1)S(1)}, u32[]{:S(2)}, u32[]{:S(2)}) %collective-permute-start.6) | collective-permute-done | bytes 393248 | tf_op jit(solution)/shard_map/ppermute | solution.py:753
  27.9 1.1 %place_yz.1.refs_3_ = bf16[11,768,128]{2,1,0:T(8,128)(2,1)} custom-call(bf16[2192,128]{1,0:T(8,128)(2,1)S(1)} %collective-permute-done.early_ref, bf16[1536,128]{1,0:T(8,128)(2,1)S(1)} %collective-permute-done.6.refs_0_.refs_1_, bf16[11,128,128]{2,1,0:T(8,128)(2,1)S(1)} %get-tuple-element.37.refs_1_.refs_2_, ...), custom_call_target="tpu_custom_call", output_to_operand_aliasing={{}: (3, {})} | custom-call | flops 1000000000 | bytes 4000000 | tf_op jit(solution)/shard_map/place_yz/pallas_call | solution.py:770
  29.0 2.2 %collective-permute-done.1.refs_0_ = bf16[768,128]{1,0:T(8,128)(2,1)S(1)} collective-permute-done((bf16[768,128]{1,0:T(8,128)(2,1)S(1)}, bf16[768,128]{1,0:T(8,128)(2,1)S(1)}, u32[]{:S(2)}, u32[]{:S(2)}) %collective-permute-start.1) | collective-permute-done | bytes 196640 | tf_op jit(solution)/shard_map/ppermute | solution.py:755
  31.3 1.0 %place_x.1 = bf16[11,768,128]{2,1,0:T(8,128)(2,1)} custom-call(bf16[2192,128]{1,0:T(8,128)(2,1)S(1)} %collective-permute-done.early_ref, bf16[768,128]{1,0:T(8,128)(2,1)S(1)} %collective-permute-done.1.refs_0_, bf16[1536,128]{1,0:T(8,128)(2,1)S(1)} %collective-permute-done.6.refs_0_.refs_1_, ...), custom_call_target="tpu_custom_call", output_to_operand_aliasing={{}: (4, {})} | custom-call | flops 1000000000 | bytes 4000000 | tf_op jit(solution)/shard_map/place_x/pallas_call | solution.py:770
Async XLA Ops:
  3.0 16.5 %collective-permute-start = (bf16[2192,128]{1,0:T(8,128)(2,1)S(1)}, bf16[2192,128]{1,0:T(8,128)(2,1)S(1)}, u32[]{:S(2)}, u32[]{:S(2)}) collective-permute-start(bf16[2192,128]{1,0:T(8,128)(2,1)S(1)} %get-tuple-element.22), channel_id=1, source_target_pairs={{0,16},{16,0},{1,17},{17,1},{2,18},{18,2},{3,19},{19,3},{4,20},{20... | collective-permute-start | bytes 1683464 | tf_op jit(solution)/shard_map/ppermute | solution.py:709
  6.0 6.6 %copy-start = (s32[2,2,2]{2,1,0:T(2,128)S(1)}, s32[2,2,2]{2,1,0:T(2,128)}, u32[]{:S(2)}) copy-start(s32[2,2,2]{2,1,0:T(2,128)} %pair_ref.3) | copy-start | bytes 100
  6.1 6.6 %copy-start.1 = (s32[16,1]{0,1:T(1,128)S(1)}, s32[16,1]{0,1:T(1,128)}, u32[]{:S(2)}) copy-start(s32[16,1]{0,1:T(1,128)} %param.7) | copy-start | bytes 196
  6.1 6.5 %collective-permute-start.4 = (bf16[8,64,128]{2,1,0:T(8,128)(2,1)S(1)}, bf16[8,64,128]{2,1,0:T(8,128)(2,1)S(1)}, u32[]{:S(2)}, u32[]{:S(2)}) collective-permute-start(bf16[8,64,128]{2,1,0:T(8,128)(2,1)S(1)} %get-tuple-element.30), channel_id=1, source_target_pairs={{0,1},{1,0},{2,3},{3,2},{4,5},{5,4},{6,7},{7,6},{8,9},{9,8},{10,11... | collective-permute-start | bytes 393224 | tf_op jit(solution)/shard_map/ppermute | solution.py:723
  6.1 6.4 %collective-permute-start.5 = (bf16[8,64,128]{2,1,0:T(8,128)(2,1)S(1)}, bf16[8,64,128]{2,1,0:T(8,128)(2,1)S(1)}, u32[]{:S(2)}, u32[]{:S(2)}) collective-permute-start(bf16[8,64,128]{2,1,0:T(8,128)(2,1)S(1)} %get-tuple-element.31), channel_id=1, source_target_pairs={{0,4},{1,2},{2,1},{3,7},{4,0},{5,6},{6,5},{7,3},{8,12},{9,10},{10,... | collective-permute-start | bytes 393224 | tf_op jit(solution)/shard_map/ppermute | solution.py:723
  7.8 4.8 %collective-permute-start.2 = (bf16[2,128,128]{2,1,0:T(8,128)(2,1)S(1)}, bf16[2,128,128]{2,1,0:T(8,128)(2,1)S(1)}, u32[]{:S(2)}, u32[]{:S(2)}) collective-permute-start(bf16[2,128,128]{2,1,0:T(8,128)(2,1)S(1)} %get-tuple-element.28), channel_id=1, source_target_pairs={{0,4},{1,5},{2,6},{3,7},{4,0},{5,1},{6,2},{7,3},{8,12},{9,13},{10,... | collective-permute-start | bytes 196616 | tf_op jit(solution)/shard_map/ppermute | solution.py:723
  8.2 4.3 %collective-permute-start.3 = (bf16[2,128,128]{2,1,0:T(8,128)(2,1)S(1)}, bf16[2,128,128]{2,1,0:T(8,128)(2,1)S(1)}, u32[]{:S(2)}, u32[]{:S(2)}) collective-permute-start(bf16[2,128,128]{2,1,0:T(8,128)(2,1)S(1)} %get-tuple-element.29), channel_id=1, source_target_pairs={{0,1},{1,0},{2,3},{3,2},{4,8},{5,9},{6,10},{7,11},{8,4},{9,5},{10,... | collective-permute-start | bytes 196616 | tf_op jit(solution)/shard_map/ppermute | solution.py:723
  14.2 13.7 %collective-permute-start.6 = (bf16[1536,128]{1,0:T(8,128)(2,1)S(1)}, bf16[1536,128]{1,0:T(8,128)(2,1)S(1)}, u32[]{:S(2)}, u32[]{:S(2)}) collective-permute-start(bf16[1536,128]{1,0:T(8,128)(2,1)S(1)} %get-tuple-element.32), channel_id=1, source_target_pairs={{0,16},{16,0},{1,17},{17,1},{2,18},{18,2},{3,19},{19,3},{4,20},{20... | collective-permute-start | bytes 1179656 | tf_op jit(solution)/shard_map/ppermute | solution.py:753
  20.8 10.5 %collective-permute-start.1 = (bf16[768,128]{1,0:T(8,128)(2,1)S(1)}, bf16[768,128]{1,0:T(8,128)(2,1)S(1)}, u32[]{:S(2)}, u32[]{:S(2)}) collective-permute-start(bf16[768,128]{1,0:T(8,128)(2,1)S(1)} %get-tuple-element.27), channel_id=1, source_target_pairs={{0,16},{16,0},{1,17},{17,1},{2,18},{18,2},{3,19},{19,3},{4,20},{20... | collective-permute-start | bytes 589832 | tf_op jit(solution)/shard_map/ppermute | solution.py:755

commit v11 on v10

--- a/solution.py
+++ b/solution.py
@@ -314,11 +314,10 @@
 
     face = p_ref[jnp.where(lax.axis_index("gx") == 0, nx - 1, 0)]
     send_ref[nb * rows + 2 * SUB :] = face.reshape(ny * blk, LANES)
+    for copy in blocks:
+        copy.wait()
 
     for x, y in [(x, y) for x in range(nx) for y in range(ny)]:
-        if y == 0 and x % px == 0:
-            for copy in blocks[x : x + px]:
-                copy.wait()
         here = a_ref.at[x, y]
         along_z = here[6] * first + here[5] * second
         right = jnp.concatenate(
@@ -702,7 +701,7 @@
             pltpu.SMEM((4, capacity), jnp.int32),
             pltpu.SemaphoreType.DMA((3 + nx,)),
         ],
-        compiler_params=room,
+        compiler_params=pltpu.CompilerParams(vmem_limit_bytes=24 * 2**20),
         cost_estimate=cost,
         name="inner_blocks",
     )(*[pltpu.with_memory_space_constraint(one, pltpu.HBM) for one in (route_row, pairing, p_view, a_view)])
@@ -778,7 +777,7 @@
                 pltpu.VMEM((11, full, LANES), half_type),
                 pltpu.SemaphoreType.DMA((2, 11)),
             ],
-            compiler_params=room,
+            compiler_params=pltpu.CompilerParams(vmem_limit_bytes=24 * 2**20),
             cost_estimate=cost,
             name="place_x" if with_x else "place_yz",
         )(*held(got_0, *late, half), out)

time: 32.4 us -> 32.3 us (level)
  transfers between devices with their start and end apart: 7 -> 7, of which waited for: 4 -> 4; matrix products, arithmetic and copies ran while one was open for 0% -> 0% of each run, Pallas kernels for 17% -> 18%
where the time goes in v11:
time: 32.3 us; the launch traced here: 32.1 us
  waiting for transfers between devices  14.3 us (44%)
  Pallas kernels  9.42 us (29%)
  starting transfers between devices  8.3 us (26%)
    ppermute x1, waiting for transfers between devices, local(): got_0 = lax.ppermute(send_0, 'gx', swap)  5.13 us
    ppermute x1, waiting for transfers between devices, local(): got_yz = lax.ppermute(send_yz, 'gx', swap)  4.07 us
    ppermute x4, starting transfers between devices, local(): halos.append(lax.ppermute(value, ('gy', 'gz'), rounds[name]))  3.06 us
    ppermute x1, starting transfers between devices, local(): got_0 = lax.ppermute(send_0, 'gx', swap)  3 us
    pallas_call x2, Pallas kernels, outer(): pl.pallas_call(functools.partial(kernel, dims, grid), out_shape=(near(blo...  2.87 us
    ppermute x4, waiting for transfers between devices, local(): halos.append(lax.ppermute(value, ('gy', 'gz'), rounds[name]))  2.87 us
    pallas_call x1, Pallas kernels, local(): pl.pallas_call(functools.partial(inner_kernel, dims, grid), out_shape=(ne...  2.79 us
    ppermute x1, waiting for transfers between devices, local(): got_x = lax.ppermute(send_x, 'gx', swap)  2.24 us
  transfers between devices with their start and end apart: 7, of which 4 were waited for; matrix products, arithmetic and copies ran while one was open for 0% of the time, Pallas kernels for 18%

profile of v11, /device:TPU:0, one launch (start us, length us, event | category | flops | bytes accessed | tf_op | source)
XLA Modules:
  0.0 32.1 jit_solution(16514228476613825080)
XLA Ops:
  0.0 2.8 %inner_blocks.1 = (bf16[2192,128]{1,0:T(8,128)(2,1)S(1)}, f32[3840,128]{1,0:T(8,128)S(1)}, bf16[16,128]{1,0:T(8,128)(2,1)S(1)}, bf16[8,64,128]{2,1,0:T(8,128)(2,...) custom-call(s32[1,16]{1,0:T(1,128)} %bitcast.18, ...), custom_call_target="tpu_custom_call" | custom-call | flops 1000000000 | bytes 4000000 | tf_op jit(solution)/shard_map/inner_blocks/pallas_call | solution.py:681
  2.8 3.0 %collective-permute-start = (bf16[2192,128]{1,0:T(8,128)(2,1)S(1)}, bf16[2192,128]{1,0:T(8,128)(2,1)S(1)}, u32[]{:S(2)}, u32[]{:S(2)}) collective-permute-start(bf16[2192,128]{1,0:T(8,128)(2,1)S(1)} %get-tuple-element.22), channel_id=1, source_target_pairs={{0,16},{16,0},{1,17},{17,1},{2,18},{18,2},{3,19},{19,3},{4,20},{20... | collective-permute-start | bytes 1683464 | tf_op jit(solution)/shard_map/ppermute | solution.py:708
  5.8 0.1 faces.1
  5.9 0.0 copy-start
  5.9 0.0 copy-start.1
  5.9 0.1 collective-permute-start.4
  6.0 1.6 %collective-permute-start.5 = (bf16[8,64,128]{2,1,0:T(8,128)(2,1)S(1)}, bf16[8,64,128]{2,1,0:T(8,128)(2,1)S(1)}, u32[]{:S(2)}, u32[]{:S(2)}) collective-permute-start(bf16[8,64,128]{2,1,0:T(8,128)(2,1)S(1)} %get-tuple-element.31), channel_id=1, source_target_pairs={{0,4},{1,2},{2,1},{3,7},{4,0},{5,6},{6,5},{7,3},{8,12},{9,10},{10,... | collective-permute-start | bytes 393224 | tf_op jit(solution)/shard_map/ppermute | solution.py:722
  7.6 0.5 %collective-permute-start.2 = (bf16[2,128,128]{2,1,0:T(8,128)(2,1)S(1)}, bf16[2,128,128]{2,1,0:T(8,128)(2,1)S(1)}, u32[]{:S(2)}, u32[]{:S(2)}) collective-permute-start(bf16[2,128,128]{2,1,0:T(8,128)(2,1)S(1)} %get-tuple-element.28), channel_id=1, source_target_pairs={{0,4},{1,5},{2,6},{3,7},{4,0},{5,1},{6,2},{7,3},{8,12},{9,13},{10,... | collective-permute-start | bytes 196616 | tf_op jit(solution)/shard_map/ppermute | solution.py:722
  8.1 0.9 %collective-permute-start.3 = (bf16[2,128,128]{2,1,0:T(8,128)(2,1)S(1)}, bf16[2,128,128]{2,1,0:T(8,128)(2,1)S(1)}, u32[]{:S(2)}, u32[]{:S(2)}) collective-permute-start(bf16[2,128,128]{2,1,0:T(8,128)(2,1)S(1)} %get-tuple-element.29), channel_id=1, source_target_pairs={{0,1},{1,0},{2,3},{3,2},{4,8},{5,9},{6,10},{7,11},{8,4},{9,5},{10,... | collective-permute-start | bytes 196616 | tf_op jit(solution)/shard_map/ppermute | solution.py:722
  9.0 0.6 %outer_left.1.part_ref = bf16[4,4,3,64,128]{4,3,2,1,0:T(8,128)(2,1)S(1)} custom-call(bf16[8,128,128]{2,1,0:T(8,128)(2,1)S(1)} %get-tuple-element.23.left_ref, bf16[4,4,7,64,128]{4,3,2,1,0:T(8,128)(2,1)S(1)} %get-tuple-element.24.a_ref), custom_call_target="tpu_custom_call" | custom-call | flops 1000000000 | bytes 4000000 | tf_op jit(solution)/shard_map/outer_left/pallas_call | solution.py:725
  9.6 2.9 %collective-permute-done.2.ya_ref = bf16[2,128,128]{2,1,0:T(8,128)(2,1)S(1)} collective-permute-done((bf16[2,128,128]{2,1,0:T(8,128)(2,1)S(1)}, bf16[2,128,128]{2,1,0:T(8,128)(2,1)S(1)}, u32[]{:S(2)}, u32[]{:S(2)}) %collective-permute-start.2) | collective-permute-done | bytes 65568 | tf_op jit(solution)/shard_map/ppermute | solution.py:722
  12.4 0.0 collective-permute-done.3.yb_ref
  12.4 0.0 collective-permute-done.4.za_ref
  12.5 0.0 collective-permute-done.5.zb_ref
  12.5 0.0 copy-done
  12.5 0.0 copy-done.1
  12.5 1.6 %shard_map.47 = (bf16[1536,128]{1,0:T(8,128)(2,1)S(1)}, bf16[1536,128]{1,0:T(8,128)(2,1)S(1)}) custom-call(s32[1,16]{1,0:T(1,128)S(1)} %bitcast.19, s32[2,2,2]{2,1,0:T(2,128)S(1)} %copy-done, bf16[4,4,3,64,128]{4,3,2,1,0:T(8,128)(2,1)S(1)} %outer_left.1.part_ref, bf16[8,64,128]{2,1,0:T(8,128)(2,1)S(1)} %get-tuple-element.25.zup_ref, ...), custom_call_target="tpu_custom_call" | custom-call | flops 1000000000 | bytes 4000000 | tf_op jit(solution)/shard_map/pallas_call | solution.py:737
  14.1 0.2 collective-permute-start.6
  14.2 5.1 %collective-permute-done.early_ref = bf16[2192,128]{1,0:T(8,128)(2,1)S(1)} collective-permute-done((bf16[2192,128]{1,0:T(8,128)(2,1)S(1)}, bf16[2192,128]{1,0:T(8,128)(2,1)S(1)}, u32[]{:S(2)}, u32[]{:S(2)}) %collective-permute-start) | collective-permute-done | bytes 561184 | tf_op jit(solution)/shard_map/ppermute | solution.py:708
  19.4 1.3 %shard_map.46 = (bf16[768,128]{1,0:T(8,128)(2,1)S(1)}, bf16[768,128]{1,0:T(8,128)(2,1)S(1)}) custom-call(s32[1,16]{1,0:T(1,128)S(1)} %bitcast.20, s32[2,2,2]{2,1,0:T(2,128)S(1)} %copy-done, bf16[4,4,3,64,128]{4,3,2,1,0:T(8,128)(2,1)S(1)} %outer_left.1.part_ref, bf16[8,64,128]{2,1,0:T(8,128)(2,1)S(1)} %get-tuple-element.25.zup_ref, ...), custom_call_target="tpu_custom_call" | custom-call | flops 1000000000 | bytes 4000000 | tf_op jit(solution)/shard_map/pallas_call | solution.py:737
  20.7 2.1 %collective-permute-start.1 = (bf16[768,128]{1,0:T(8,128)(2,1)S(1)}, bf16[768,128]{1,0:T(8,128)(2,1)S(1)}, u32[]{:S(2)}, u32[]{:S(2)}) collective-permute-start(bf16[768,128]{1,0:T(8,128)(2,1)S(1)} %get-tuple-element.27), channel_id=1, source_target_pairs={{0,16},{16,0},{1,17},{17,1},{2,18},{18,2},{3,19},{19,3},{4,20},{20... | collective-permute-start | bytes 589832 | tf_op jit(solution)/shard_map/ppermute | solution.py:754
  22.7 1.0 %place_kept.1 = (bf16[11,128,128]{2,1,0:T(8,128)(2,1)S(1)}, bf16[11,768,128]{2,1,0:T(8,128)(2,1)}) custom-call(f32[3840,128]{1,0:T(8,128)S(1)} %get-tuple-element.33.total_ref, bf16[16,128]{1,0:T(8,128)(2,1)S(1)} %get-tuple-element.34.codes_ref, bf16[768,128]{1,0:T(8,128)(2,1)S(1)} %get-tuple-element.35.x_ref, bf16[1536,128]{1,0:T(8,128)(2,1)S(1)} %get-tuple-element.36.yz_ref), custom_call_target="tpu_custom_call" | custom-call | flops 1000000000 | bytes 4000000 | tf_op jit(solution)/shard_map/place_kept/pallas_call | solution.py:758
  23.7 4.1 %collective-permute-done.6.refs_0_.refs_1_ = bf16[1536,128]{1,0:T(8,128)(2,1)S(1)} collective-permute-done((bf16[1536,128]{1,0:T(8,128)(2,1)S(1)}, bf16[1536,128]{1,0:T(8,128)(2,1)S(1)}, u32[]{:S(2)}, u32[]{:S(2)}) %collective-permute-start.6) | collective-permute-done | bytes 393248 | tf_op jit(solution)/shard_map/ppermute | solution.py:752
  27.8 1.1 %place_yz.1.refs_3_ = bf16[11,768,128]{2,1,0:T(8,128)(2,1)} custom-call(bf16[2192,128]{1,0:T(8,128)(2,1)S(1)} %collective-permute-done.early_ref, bf16[1536,128]{1,0:T(8,128)(2,1)S(1)} %collective-permute-done.6.refs_0_.refs_1_, bf16[11,128,128]{2,1,0:T(8,128)(2,1)S(1)} %get-tuple-element.37.refs_1_.refs_2_, ...), custom_call_target="tpu_custom_call", output_to_operand_aliasing={{}: (3, {})} | custom-call | flops 1000000000 | bytes 4000000 | tf_op jit(solution)/shard_map/place_yz/pallas_call | solution.py:769
  28.9 2.2 %collective-permute-done.1.refs_0_ = bf16[768,128]{1,0:T(8,128)(2,1)S(1)} collective-permute-done((bf16[768,128]{1,0:T(8,128)(2,1)S(1)}, bf16[768,128]{1,0:T(8,128)(2,1)S(1)}, u32[]{:S(2)}, u32[]{:S(2)}) %collective-permute-start.1) | collective-permute-done | bytes 196640 | tf_op jit(solution)/shard_map/ppermute | solution.py:754
  31.1 1.0 %place_x.1 = bf16[11,768,128]{2,1,0:T(8,128)(2,1)} custom-call(bf16[2192,128]{1,0:T(8,128)(2,1)S(1)} %collective-permute-done.early_ref, bf16[768,128]{1,0:T(8,128)(2,1)S(1)} %collective-permute-done.1.refs_0_, bf16[1536,128]{1,0:T(8,128)(2,1)S(1)} %collective-permute-done.6.refs_0_.refs_1_, ...), custom_call_target="tpu_custom_call", output_to_operand_aliasing={{}: (4, {})} | custom-call | flops 1000000000 | bytes 4000000 | tf_op jit(solution)/shard_map/place_x/pallas_call | solution.py:769
Async XLA Ops:
  2.8 16.6 %collective-permute-start = (bf16[2192,128]{1,0:T(8,128)(2,1)S(1)}, bf16[2192,128]{1,0:T(8,128)(2,1)S(1)}, u32[]{:S(2)}, u32[]{:S(2)}) collective-permute-start(bf16[2192,128]{1,0:T(8,128)(2,1)S(1)} %get-tuple-element.22), channel_id=1, source_target_pairs={{0,16},{16,0},{1,17},{17,1},{2,18},{18,2},{3,19},{19,3},{4,20},{20... | collective-permute-start | bytes 1683464 | tf_op jit(solution)/shard_map/ppermute | solution.py:708
  5.9 6.6 %copy-start = (s32[2,2,2]{2,1,0:T(2,128)S(1)}, s32[2,2,2]{2,1,0:T(2,128)}, u32[]{:S(2)}) copy-start(s32[2,2,2]{2,1,0:T(2,128)} %pair_ref.3) | copy-start | bytes 100
  5.9 6.6 %copy-start.1 = (s32[16,1]{0,1:T(1,128)S(1)}, s32[16,1]{0,1:T(1,128)}, u32[]{:S(2)}) copy-start(s32[16,1]{0,1:T(1,128)} %param.7) | copy-start | bytes 196
  5.9 6.5 %collective-permute-start.4 = (bf16[8,64,128]{2,1,0:T(8,128)(2,1)S(1)}, bf16[8,64,128]{2,1,0:T(8,128)(2,1)S(1)}, u32[]{:S(2)}, u32[]{:S(2)}) collective-permute-start(bf16[8,64,128]{2,1,0:T(8,128)(2,1)S(1)} %get-tuple-element.30), channel_id=1, source_target_pairs={{0,1},{1,0},{2,3},{3,2},{4,5},{5,4},{6,7},{7,6},{8,9},{9,8},{10,11... | collective-permute-start | bytes 393224 | tf_op jit(solution)/shard_map/ppermute | solution.py:722
  6.0 6.4 %collective-permute-start.5 = (bf16[8,64,128]{2,1,0:T(8,128)(2,1)S(1)}, bf16[8,64,128]{2,1,0:T(8,128)(2,1)S(1)}, u32[]{:S(2)}, u32[]{:S(2)}) collective-permute-start(bf16[8,64,128]{2,1,0:T(8,128)(2,1)S(1)} %get-tuple-element.31), channel_id=1, source_target_pairs={{0,4},{1,2},{2,1},{3,7},{4,0},{5,6},{6,5},{7,3},{8,12},{9,10},{10,... | collective-permute-start | bytes 393224 | tf_op jit(solution)/shard_map/ppermute | solution.py:722
  7.6 4.8 %collective-permute-start.2 = (bf16[2,128,128]{2,1,0:T(8,128)(2,1)S(1)}, bf16[2,128,128]{2,1,0:T(8,128)(2,1)S(1)}, u32[]{:S(2)}, u32[]{:S(2)}) collective-permute-start(bf16[2,128,128]{2,1,0:T(8,128)(2,1)S(1)} %get-tuple-element.28), channel_id=1, source_target_pairs={{0,4},{1,5},{2,6},{3,7},{4,0},{5,1},{6,2},{7,3},{8,12},{9,13},{10,... | collective-permute-start | bytes 196616 | tf_op jit(solution)/shard_map/ppermute | solution.py:722
  8.1 4.3 %collective-permute-start.3 = (bf16[2,128,128]{2,1,0:T(8,128)(2,1)S(1)}, bf16[2,128,128]{2,1,0:T(8,128)(2,1)S(1)}, u32[]{:S(2)}, u32[]{:S(2)}) collective-permute-start(bf16[2,128,128]{2,1,0:T(8,128)(2,1)S(1)} %get-tuple-element.29), channel_id=1, source_target_pairs={{0,1},{1,0},{2,3},{3,2},{4,8},{5,9},{6,10},{7,11},{8,4},{9,5},{10,... | collective-permute-start | bytes 196616 | tf_op jit(solution)/shard_map/ppermute | solution.py:722
  14.1 13.7 %collective-permute-start.6 = (bf16[1536,128]{1,0:T(8,128)(2,1)S(1)}, bf16[1536,128]{1,0:T(8,128)(2,1)S(1)}, u32[]{:S(2)}, u32[]{:S(2)}) collective-permute-start(bf16[1536,128]{1,0:T(8,128)(2,1)S(1)} %get-tuple-element.32), channel_id=1, source_target_pairs={{0,16},{16,0},{1,17},{17,1},{2,18},{18,2},{3,19},{19,3},{4,20},{20... | collective-permute-start | bytes 1179656 | tf_op jit(solution)/shard_map/ppermute | solution.py:752
  20.7 10.5 %collective-permute-start.1 = (bf16[768,128]{1,0:T(8,128)(2,1)S(1)}, bf16[768,128]{1,0:T(8,128)(2,1)S(1)}, u32[]{:S(2)}, u32[]{:S(2)}) collective-permute-start(bf16[768,128]{1,0:T(8,128)(2,1)S(1)} %get-tuple-element.27), channel_id=1, source_target_pairs={{0,16},{16,0},{1,17},{17,1},{2,18},{18,2},{3,19},{19,3},{4,20},{20... | collective-permute-start | bytes 589832 | tf_op jit(solution)/shard_map/ppermute | solution.py:754
